TPU v7x, 32 devices: a whole 2x2x4 slice. The times are simulated.
32 devices in a mesh: dp: 8 (over z, x), tensor: 4 (over y, core).
Axes of the slice: x: 2, y: 2, z: 4, core: 2. Of those that a mesh axis runs over, the one named last changes fastest.
Arguments:
- tokens: bfloat16 [16, 512, 768], P('dp', 'tensor'), may hold values from -6 to 6
- characters: bfloat16 [16, 2048, 256], P('dp', 'tensor'), may hold values from -6 to 6
- doc_lengths: int32 [16, 8], P('dp'), may hold values from 1 to 256, 512 in all within a row
- token_chars: int32 [16, 512], P('dp'), may hold values from 1 to 8, 2048 in all within a row
- w_qkv: bfloat16 [768, 3, 768], P(None, None, 'tensor'), may hold values from -0.21875 to 0.21875
- w_out: bfloat16 [768, 768], P('tensor'), may hold values from -0.875 to 0.875
- w_in: bfloat16 [768, 3072], P(None, 'tensor'), may hold values from -0.21875 to 0.21875
- w_down: bfloat16 [3072, 768], P('tensor'), may hold values from -0.109375 to 0.109375
- w_gru: bfloat16 [256, 2, 2, 384], P(None, None, None, 'tensor'), may hold values from -0.375 to 0.375
- gate_bias: float32 [2, 384], P(None, 'tensor'), may hold values from -4 to 1
- w_conv: bfloat16 [3, 1536, 768], P(None, None, 'tensor'), may hold values from -0.09375 to 0.09375
- w_merge: bfloat16 [768, 2, 768], P('tensor'), may hold values from -0.21875 to 0.21875
- norm_gain: float32 [4, 768], replicated, may hold values from 0.5 to 1.5
- norm_bias: float32 [4, 768], replicated, may hold values from -1.75 to 1.75
- token_cot: float32 [16, 512, 768], P('dp', 'tensor'), may hold values from -6 to 6
- char_cot: float32 [16, 512, 768], P('dp', 'tensor'), may hold values from -6 to 6
Outputs:
- token_out: bfloat16 [16, 512, 768], P('dp', 'tensor')
- char_out: bfloat16 [16, 512, 768], P('dp', 'tensor')
- grad_tokens: float32 [16, 512, 768], P('dp', 'tensor')
- grad_characters: float32 [16, 2048, 256], P('dp', 'tensor')
- grad_qkv: float32 [768, 3, 768], P(None, None, 'tensor')
- grad_out: float32 [768, 768], P('tensor')
- grad_in: float32 [768, 3072], P(None, 'tensor')
- grad_down: float32 [3072, 768], P('tensor')
- grad_gru: float32 [256, 2, 2, 384], P(None, None, None, 'tensor')
- grad_gate_bias: float32 [2, 384], P(None, 'tensor')
- grad_conv: float32 [3, 1536, 768], P(None, None, 'tensor')
- grad_merge: float32 [768, 2, 768], P('tensor')
- grad_gain: float32 [4, 768], replicated
- grad_bias: float32 [4, 768], replicated
Inputs may be any that keep to these rules, and one draw needn't show every extreme that they name: `doc_lengths`: A sequence's 8 entries are the token counts of its documents in order, summing to 512; in every sequence one document has exactly 256 tokens. `token_chars`: A sequence's 512 entries are the character counts of its tokens in order, summing to 2048; in every sequence some token has exactly 8 characters.
All inputs are finite; a program needn't handle non-finite values.
Results may differ from a plain program's by a relative error of at most 0.023.
Values may be sent and summed in bfloat16 or wider, within the bound.
A program may use at most 192 MiB of HBM per device.

v0:
```python
import jax
import jax.numpy as jnp
from jax import lax
from jax.sharding import PartitionSpec as P

HD = 64


NORM_EPSILON = 1e-06
MASK_VALUE = -1e30
HIGH_PRECISION = lax.Precision.HIGHEST


def layer_norm(row_values, gain_row, shift_row):
    average = jnp.mean(row_values, axis=-1, keepdims=True)
    centered = row_values - average
    spread = jnp.mean(centered * centered, axis=-1, keepdims=True)
    return centered * lax.rsqrt(spread + NORM_EPSILON) * gain_row + shift_row


def gelu_exact(values):
    return jax.nn.gelu(values, approximate=False)


def layout(doc_sizes, char_counts, char_total):
    length = char_counts.shape[0]
    doc_ends = jnp.cumsum(doc_sizes, dtype=jnp.int32)
    positions = jnp.arange(length, dtype=jnp.int32)
    segment = jnp.sum(
        (positions[:, None] >= doc_ends[None, :]).astype(jnp.int32), axis=1, dtype=jnp.int32
    )
    token_ends = jnp.cumsum(char_counts, dtype=jnp.int32)
    char_positions = jnp.arange(char_total, dtype=jnp.int32)
    char_token = jnp.searchsorted(token_ends, char_positions, side="right")
    last_char = token_ends - 1
    first_char = token_ends - char_counts
    char_segment = jnp.take(segment, char_token)
    char_same = (char_segment[1:] == char_segment[:-1]).astype(jnp.float32)
    token_same = (segment[1:] == segment[:-1]).astype(jnp.float32)
    zero_one = jnp.zeros((1,), jnp.float32)
    keep_forward = jnp.concatenate([zero_one, char_same])
    keep_backward = jnp.concatenate([char_same, zero_one])
    prev_ok = jnp.concatenate([zero_one, token_same])
    next_ok = jnp.concatenate([token_same, zero_one])
    return (segment, first_char, last_char, keep_forward, keep_backward, prev_ok, next_ok)


def gru_tokens(projected, gate_bias, keep_forward, keep_backward, first_char, last_char):
    char_total = projected.shape[0]
    units = projected.shape[3]
    logits = projected[:, :, 0, :] + gate_bias[None]
    gates = jax.nn.sigmoid(logits)
    drive = gates * projected[:, :, 1, :]
    log_decay = -jax.nn.softplus(logits)
    drive_all = jnp.concatenate([drive[:, 0], jnp.flip(drive[:, 1], axis=0)], axis=1)
    log_all = jnp.concatenate([log_decay[:, 0], jnp.flip(log_decay[:, 1], axis=0)], axis=1)
    cut_forward = jnp.broadcast_to((1.0 - keep_forward)[:, None], (char_total, units))
    cut_backward = jnp.broadcast_to(
        jnp.flip(1.0 - keep_backward, axis=0)[:, None], (char_total, units)
    )
    cut_all = jnp.concatenate([cut_forward, cut_backward], axis=1)
    block_size = min(128, char_total)
    block_total = char_total // block_size
    row_ids = jnp.arange(block_size, dtype=jnp.int32)
    lower = (row_ids[:, None] >= row_ids[None, :]).astype(jnp.float32)

    def block_step(carry, pieces):
        drive_block, log_block, cut_block = pieces
        level = jnp.dot(
            lower, log_block, precision=HIGH_PRECISION, preferred_element_type=jnp.float32
        )
        resets = jnp.dot(
            lower, cut_block, precision=HIGH_PRECISION, preferred_element_type=jnp.float32
        )
        linked = (resets[:, None, :] == resets[None, :, :]) & (lower[:, :, None] > 0.5)
        gap = jnp.where(linked, level[:, None, :] - level[None, :, :], 0.0)
        weights = jnp.where(linked, jnp.exp(gap), 0.0)
        inside = jnp.sum(weights * drive_block[None, :, :], axis=1)
        entering = jnp.where(resets < 0.5, jnp.exp(level), 0.0) * carry[None, :]
        states = inside + entering
        return (states[-1], states)

    start = jnp.zeros((2 * units,), jnp.float32)
    unused_last, states = lax.scan(
        jax.checkpoint(block_step),
        start,
        (
            drive_all.reshape(block_total, block_size, 2 * units),
            log_all.reshape(block_total, block_size, 2 * units),
            cut_all.reshape(block_total, block_size, 2 * units),
        ),
    )
    states = states.reshape(char_total, 2 * units)
    forward_states = states[:, :units]
    backward_states = jnp.flip(states[:, units:], axis=0)
    return jnp.stack(
        [
            jnp.take(forward_states, last_char, axis=0),
            jnp.take(backward_states, first_char, axis=0),
        ],
        axis=1,
    )


def conv_inputs(joined, prev_ok, next_ok):
    zero_row = jnp.zeros((1, joined.shape[1]), joined.dtype)
    preceding = jnp.concatenate([zero_row, joined[:-1]], axis=0) * prev_ok[:, None].astype(
        joined.dtype
    )
    following = jnp.concatenate([joined[1:], zero_row], axis=0) * next_ok[:, None].astype(
        joined.dtype
    )
    return jnp.concatenate([preceding, joined, following], axis=1)


def conv_back(grad_stacked, prev_ok, next_ok):
    column_count = grad_stacked.shape[1] // 3
    from_prev = grad_stacked[:, :column_count] * prev_ok[:, None]
    from_next = grad_stacked[:, 2 * column_count :] * next_ok[:, None]
    zero_row = jnp.zeros((1, column_count), jnp.float32)
    middle = grad_stacked[:, column_count : 2 * column_count]
    return (
        middle
        + jnp.concatenate([from_prev[1:], zero_row], axis=0)
        + jnp.concatenate([zero_row, from_next[:-1]], axis=0)
    )


def inner_rows(left_rows, right_rows):
    return lax.dot_general(
        left_rows, right_rows, (((0,), (0,)), ((), ())), preferred_element_type=jnp.float32
    )


def times_transposed(left_rows, right_matrix):
    return lax.dot_general(
        left_rows, right_matrix, (((1,), (1,)), ((), ())), preferred_element_type=jnp.float32
    )


def reduce_weights(grads):
    return lax.psum(
        (grads[0], grads[1], grads[2], grads[3], grads[4], grads[5], grads[6], grads[7]), "dp"
    )


def local(
    tokens,
    characters,
    doc_lengths,
    token_chars,
    w_qkv,
    w_out,
    w_in,
    w_down,
    w_gru,
    gate_bias,
    w_conv,
    w_merge,
    norm_gain,
    norm_bias,
    token_cot,
    char_cot,
):
    micro_count = tokens.shape[0]
    shard_len = tokens.shape[1]
    model_width = tokens.shape[2]
    char_width = characters.shape[2]
    group_size = lax.axis_size("tensor")
    group_rank = lax.axis_index("tensor")
    length = shard_len * group_size
    char_total = characters.shape[1] * group_size
    head_cols = w_qkv.shape[2]
    heads_here = head_cols // HD
    units_here = w_gru.shape[3]
    merge_here = w_conv.shape[2]
    row_start = group_rank * shard_len
    qkv_matrix = w_qkv.reshape(model_width, 3 * head_cols)
    gru_matrix = w_gru.reshape(char_width, 4 * units_here)
    conv_matrix = w_conv.reshape(3 * 2 * model_width, merge_here)
    merge_matrix = w_merge.reshape(merge_here, 2 * model_width)
    token_outs = []
    char_outs = []
    token_grads = []
    char_grads = []
    weight_total = None
    gain_total = jnp.zeros((4, model_width), jnp.float32)
    bias_total = jnp.zeros((4, model_width), jnp.float32)
    for micro_index in range(micro_count):
        token_rows = tokens[micro_index]
        char_rows = characters[micro_index]
        segment, first_char, last_char, keep_forward, keep_backward, prev_ok, next_ok = layout(
            doc_lengths[micro_index], token_chars[micro_index], char_total
        )
        all_tokens, all_chars = (
            lax.all_gather(token_rows, "tensor", axis=0, tiled=True),
            lax.all_gather(char_rows, "tensor", axis=0, tiled=True),
        )
        qkv = jnp.dot(all_tokens, qkv_matrix, preferred_element_type=jnp.float32).reshape(
            length, 3, heads_here, HD
        )
        queries = (qkv[:, 0] * 0.125).astype(jnp.bfloat16)
        key_low = qkv[:, 1].astype(jnp.bfloat16)
        value_low = qkv[:, 2].astype(jnp.bfloat16)
        query_block = queries
        same_doc = (segment[:, None] == segment[None, :])[None]
        scores = jnp.einsum(
            "qhd,khd->hqk", query_block, key_low, preferred_element_type=jnp.float32
        )
        scores = jnp.where(same_doc, scores, MASK_VALUE)
        row_max = jnp.max(scores, axis=-1, keepdims=True)
        log_total = row_max + jnp.log(jnp.sum(jnp.exp(scores - row_max), axis=-1, keepdims=True))
        prob_low = jnp.exp(scores - log_total).astype(jnp.bfloat16)
        context_parts = jnp.einsum(
            "hqk,khd->qhd", prob_low, value_low, preferred_element_type=jnp.float32
        )
        context_low = context_parts.reshape(length, head_cols).astype(jnp.bfloat16)
        attn_share = lax.psum_scatter(
            jnp.dot(context_low, w_out, preferred_element_type=jnp.float32).astype(jnp.bfloat16),
            "tensor",
            scatter_dimension=0,
            tiled=True,
        ).astype(jnp.float32)
        residual_one = token_rows.astype(jnp.float32) + attn_share
        hidden = layer_norm(residual_one, norm_gain[0], norm_bias[0])
        hidden_all = lax.all_gather(hidden.astype(jnp.bfloat16), "tensor", axis=0, tiled=True)
        pre_act = jnp.dot(hidden_all, w_in, preferred_element_type=jnp.float32)
        activation = gelu_exact(pre_act).astype(jnp.bfloat16)
        ffn_share = lax.psum_scatter(
            jnp.dot(activation, w_down, preferred_element_type=jnp.float32).astype(jnp.bfloat16),
            "tensor",
            scatter_dimension=0,
            tiled=True,
        ).astype(jnp.float32)
        residual_two = hidden + ffn_share
        token_mid = layer_norm(residual_two, norm_gain[1], norm_bias[1])
        projected = jnp.dot(all_chars, gru_matrix, preferred_element_type=jnp.float32).reshape(
            char_total, 2, 2, units_here
        )

        def char_path(proj_in, bias_in):
            return gru_tokens(proj_in, bias_in, keep_forward, keep_backward, first_char, last_char)

        char_tokens, pull_gru = jax.vjp(char_path, projected, gate_bias)
        mid_all, char_all = (
            lax.all_gather(token_mid.astype(jnp.bfloat16), "tensor", axis=0, tiled=True),
            lax.all_gather(char_tokens.astype(jnp.bfloat16), "tensor", axis=2, tiled=True),
        )
        char_flat = char_all.reshape(length, model_width)
        joined = jnp.concatenate([mid_all, char_flat], axis=1)
        stacked = conv_inputs(joined, prev_ok, next_ok)
        pre_merge = jnp.dot(stacked, conv_matrix, preferred_element_type=jnp.float32)
        merged_low = gelu_exact(pre_merge).astype(jnp.bfloat16)
        merge_share = lax.psum_scatter(
            jnp.dot(merged_low, merge_matrix, preferred_element_type=jnp.float32).astype(
                jnp.bfloat16
            ),
            "tensor",
            scatter_dimension=0,
            tiled=True,
        ).astype(jnp.float32)
        char_mine = lax.dynamic_slice_in_dim(char_flat, row_start, shard_len, 0).astype(jnp.float32)
        residual_three = token_mid + merge_share[:, :model_width]
        residual_four = char_mine + merge_share[:, model_width:]
        token_final, pull_three = jax.vjp(layer_norm, residual_three, norm_gain[2], norm_bias[2])
        char_final, pull_four = jax.vjp(layer_norm, residual_four, norm_gain[3], norm_bias[3])
        token_outs.append(token_final.astype(jnp.bfloat16))
        char_outs.append(char_final.astype(jnp.bfloat16))
        grad_res3, grad_g3, grad_b3 = pull_three(token_cot[micro_index])
        grad_res4, grad_g4, grad_b4 = pull_four(char_cot[micro_index])
        branch_grad = jnp.concatenate([grad_res3, grad_res4], axis=1).astype(jnp.bfloat16)
        branch_all = lax.all_gather(branch_grad, "tensor", axis=0, tiled=True)
        grad_merge_w = inner_rows(merged_low, branch_all)
        grad_merged = times_transposed(branch_all, merge_matrix)
        unused_merge, pull_merge = jax.vjp(gelu_exact, pre_merge)
        grad_pre_merge = pull_merge(grad_merged)[0].astype(jnp.bfloat16)
        grad_conv_w = inner_rows(stacked, grad_pre_merge)
        grad_joined = conv_back(times_transposed(grad_pre_merge, conv_matrix), prev_ok, next_ok)
        placed = lax.dynamic_update_slice_in_dim(
            jnp.zeros((length, model_width), jnp.float32), grad_res4, row_start, 0
        )
        grad_char_part = (grad_joined[:, model_width:] + placed).reshape(
            length, 2, units_here * group_size
        )
        grad_mid_conv, grad_char_tokens = (
            lax.psum_scatter(
                grad_joined[:, :model_width].astype(jnp.bfloat16),
                "tensor",
                scatter_dimension=0,
                tiled=True,
            ).astype(jnp.float32),
            lax.psum_scatter(
                grad_char_part.astype(jnp.bfloat16), "tensor", scatter_dimension=2, tiled=True
            ).astype(jnp.float32),
        )
        grad_mid = grad_res3 + grad_mid_conv
        unused_two, pull_two = jax.vjp(layer_norm, residual_two, norm_gain[1], norm_bias[1])
        grad_res2, grad_g2, grad_b2 = pull_two(grad_mid)
        ffn_grad_all = lax.all_gather(grad_res2.astype(jnp.bfloat16), "tensor", axis=0, tiled=True)
        grad_down_w = inner_rows(activation, ffn_grad_all)
        grad_activation = times_transposed(ffn_grad_all, w_down)
        unused_act, pull_act = jax.vjp(gelu_exact, pre_act)
        grad_pre = pull_act(grad_activation)[0].astype(jnp.bfloat16)
        grad_in_w = inner_rows(hidden_all, grad_pre)
        grad_hidden = grad_res2 + lax.psum_scatter(
            times_transposed(grad_pre, w_in).astype(jnp.bfloat16),
            "tensor",
            scatter_dimension=0,
            tiled=True,
        ).astype(jnp.float32)
        unused_one, pull_one = jax.vjp(layer_norm, residual_one, norm_gain[0], norm_bias[0])
        grad_res1, grad_g1, grad_b1 = pull_one(grad_hidden)
        attn_grad_all = lax.all_gather(grad_res1.astype(jnp.bfloat16), "tensor", axis=0, tiled=True)
        grad_out_w = inner_rows(context_low, attn_grad_all)
        grad_context = (
            times_transposed(attn_grad_all, w_out)
            .astype(jnp.bfloat16)
            .reshape(length, heads_here, HD)
        )
        query_block = queries
        same_doc = (segment[:, None] == segment[None, :])[None]
        scores = jnp.einsum(
            "qhd,khd->hqk", query_block, key_low, preferred_element_type=jnp.float32
        )
        scores = jnp.where(same_doc, scores, MASK_VALUE)
        prob_full = jnp.exp(scores - log_total)
        grad_probs = jnp.einsum(
            "qhd,khd->hqk", grad_context, value_low, preferred_element_type=jnp.float32
        )
        row_dot = jnp.sum(prob_full * grad_probs, axis=-1, keepdims=True)
        grad_scores = (prob_full * (grad_probs - row_dot)).astype(jnp.bfloat16)
        query_grads = jnp.einsum(
            "hqk,khd->qhd", grad_scores, key_low, preferred_element_type=jnp.float32
        )
        grad_keys = jnp.einsum(
            "hqk,qhd->khd", grad_scores, query_block, preferred_element_type=jnp.float32
        )
        grad_values = jnp.einsum(
            "hqk,qhd->khd",
            prob_full.astype(jnp.bfloat16),
            grad_context,
            preferred_element_type=jnp.float32,
        )
        query_grad = query_grads.astype(jnp.bfloat16) * 0.125
        grad_qkv_low = jnp.stack(
            [query_grad, grad_keys.astype(jnp.bfloat16), grad_values.astype(jnp.bfloat16)], axis=1
        ).reshape(length, 3 * head_cols)
        grad_qkv_w = inner_rows(all_tokens, grad_qkv_low)
        token_part = times_transposed(grad_qkv_low, qkv_matrix)
        grad_projected, grad_gate = pull_gru(grad_char_tokens)
        grad_proj_low = grad_projected.reshape(char_total, 4 * units_here).astype(jnp.bfloat16)
        grad_gru_w = inner_rows(all_chars, grad_proj_low)
        char_part = times_transposed(grad_proj_low, gru_matrix)
        token_back, char_back = (
            lax.psum_scatter(
                token_part.astype(jnp.bfloat16), "tensor", scatter_dimension=0, tiled=True
            ).astype(jnp.float32),
            lax.psum_scatter(
                char_part.astype(jnp.bfloat16), "tensor", scatter_dimension=0, tiled=True
            ).astype(jnp.float32),
        )
        token_grads.append(grad_res1 + token_back)
        char_grads.append(char_back)
        gain_total = gain_total + jnp.stack([grad_g1, grad_g2, grad_g3, grad_g4], axis=0)
        bias_total = bias_total + jnp.stack([grad_b1, grad_b2, grad_b3, grad_b4], axis=0)
        micro_grads = (
            grad_qkv_w.reshape(model_width, 3, head_cols),
            grad_out_w,
            grad_in_w,
            grad_down_w,
            grad_gru_w.reshape(char_width, 2, 2, units_here),
            grad_gate,
            grad_conv_w.reshape(3, 2 * model_width, merge_here),
            grad_merge_w.reshape(merge_here, 2, model_width),
        )
        if weight_total is None:
            weight_total = micro_grads
        else:
            weight_total = jax.tree.map(jnp.add, weight_total, micro_grads)
    weight_final = reduce_weights(weight_total)
    gain_grad, bias_grad = lax.psum((gain_total, bias_total), ("dp", "tensor"))
    return (
        jnp.stack(token_outs, axis=0),
        jnp.stack(char_outs, axis=0),
        jnp.stack(token_grads, axis=0),
        jnp.stack(char_grads, axis=0),
        weight_final[0],
        weight_final[1],
        weight_final[2],
        weight_final[3],
        weight_final[4],
        weight_final[5],
        weight_final[6],
        weight_final[7],
        gain_grad,
        bias_grad,
    )


def solution(mesh):
    return jax.shard_map(
        local,
        mesh=mesh,
        in_specs=(
            P("dp", "tensor", None),
            P("dp", "tensor", None),
            P("dp", None),
            P("dp", None),
            P(None, None, "tensor"),
            P("tensor", None),
            P(None, "tensor"),
            P("tensor", None),
            P(None, None, None, "tensor"),
            P(None, "tensor"),
            P(None, None, "tensor"),
            P("tensor", None, None),
            P(),
            P(),
            P("dp", "tensor", None),
            P("dp", "tensor", None),
        ),
        out_specs=(
            P("dp", "tensor", None),
            P("dp", "tensor", None),
            P("dp", "tensor", None),
            P("dp", "tensor", None),
            P(None, None, "tensor"),
            P("tensor", None),
            P(None, "tensor"),
            P("tensor", None),
            P(None, None, None, "tensor"),
            P(None, "tensor"),
            P(None, None, "tensor"),
            P("tensor", None, None),
            P(),
            P(),
        ),
        check_vma=False,
    )
```

profile of v0, /device:TPU:0, one launch (start us, length us, event | category | flops | bytes accessed | tf_op | source)
XLA Modules:
  0.0 2957.1 jit_solution(12711246228756902147)
XLA Ops:
  51.2 132.9 %while.116 = (s32[]{:T(128)}, u32[2048]{0:T(1024)S(1)}, u32[2048]{0:T(1024)S(1)}, s32[512]{0:T(512)S(1)}, s32[]{:T(128)}, /*index=5*/s32[]{:T(128)}, s32[]{}) while((s32[]{:T(128)}, u32[2048]{0:T(1024)S(1)}, u32[2048]{0:T(1024)S(1)}, s32[512]{0:T(512)S(1)}, s32[]{:T(128)}, /*index=5*/s32[]{:T(128)}, s32[]{}) %tuple.377), condition=%wide.region_33.37_spmd.clone, body=%wide.region_32.36_spmd.clone.sunk | while | flops 38916 | bytes 127077 | solution.py:34
  77.8 13.2 gather_fusion.1
  91.1 13.2 gather_fusion.1
  104.4 13.2 gather_fusion.1
  117.7 13.2 gather_fusion.1
  197.4 132.9 %while.115 = (s32[]{:T(128)}, u32[2048]{0:T(1024)S(1)}, u32[2048]{0:T(1024)S(1)}, s32[512]{0:T(512)S(1)}, s32[]{:T(128)}, /*index=5*/s32[]{:T(128)}, s32[]{}) while((s32[]{:T(128)}, u32[2048]{0:T(1024)S(1)}, u32[2048]{0:T(1024)S(1)}, s32[512]{0:T(512)S(1)}, s32[]{:T(128)}, /*index=5*/s32[]{:T(128)}, s32[]{}) %tuple.383), condition=%wide.region_13.15_spmd.clone, body=%wide.region_12.14_spmd.clone.sunk | while | flops 38916 | bytes 127077 | solution.py:34
  416.8 382.9 %while.114 = (s32[]{:T(128)}, f32[192]{0:T(256)S(1)}, bf16[16,128,192]{1,2,0:T(8,128)(2,1)}, f32[16,192]{1,0:T(8,128)}, f32[16,128,192]{2,1,0:T(8,128)}, /*index...) while((s32[]{:T(128)}, f32[192]{0:T(256)S(1)}, ...), condition=%wide.region_36.40_spmd.clone.clone, body=%wide.region_34.39_spmd.clone.clone.sunk | while | flops 97705984 | bytes 2366613 | solution.py:84
  423.8 13.5 multiply_reduce_fusion.35
  447.7 13.5 multiply_reduce_fusion.35
  471.7 13.5 multiply_reduce_fusion.35
  495.6 13.5 multiply_reduce_fusion.35
  519.5 13.5 multiply_reduce_fusion.35
  543.4 13.5 multiply_reduce_fusion.35
  567.4 13.5 multiply_reduce_fusion.35
  591.3 13.5 multiply_reduce_fusion.35
  615.2 13.5 multiply_reduce_fusion.35
  639.2 13.5 multiply_reduce_fusion.35
  663.1 13.5 multiply_reduce_fusion.35
  687.1 13.5 multiply_reduce_fusion.35
  711.0 13.5 multiply_reduce_fusion.35
  734.9 13.5 multiply_reduce_fusion.35
  758.9 13.5 multiply_reduce_fusion.35
  782.8 13.5 multiply_reduce_fusion.35
  910.9 291.4 %while.113 = (s32[]{:T(128)}, f32[192]{0:T(256)S(1)}, bf16[16,128,192]{1,2,0:T(8,128)(2,1)}, f32[16,192]{1,0:T(8,128)S(1)}, f32[16,128,192]{2,1,0:T(8,128)}, /*i...) while((s32[]{:T(128)}, f32[192]{0:T(256)S(1)}, ...), condition=%wide.region_16.19_spmd.clone.clone, body=%wide.region_14.18_spmd.clone.clone.sunk | while | flops 97705984 | bytes 2363257 | solution.py:84
  1261.8 23.9 reduce-scatter.19.cloned.1.call-done
  1301.2 13.9 all-gather.11.cloned.1.call-done
  1374.2 16.2 all-reduce.36.cloned.1.call-done
  1416.5 440.1 %while.111 = (s32[]{:T(128)}, f32[192]{0:T(256)S(1)}, f32[16,128,192]{1,0,2:T(8,128)}, f32[16,128,192]{1,0,2:T(8,128)}, f32[16,192]{1,0:T(8,128)}, /*index=5*/f3...) while((s32[]{:T(128)}, f32[192]{0:T(256)S(1)}, ...), condition=%wide.region_76.80_spmd.clone, body=%wide.region_71.79_spmd.clone.sunk | while | flops 154386240 | bytes 4445589 | solution.py:84
  1420.5 15.1 fusion.397
  1448.0 15.1 fusion.397
  1475.5 15.1 fusion.397
  1503.0 15.1 fusion.397
  1530.5 15.1 fusion.397
  1558.0 15.1 fusion.397
  1585.5 15.1 fusion.397
  1613.0 15.1 fusion.397
  1640.5 15.1 fusion.397
  1668.0 15.1 fusion.397
  1695.5 15.1 fusion.397
  1723.0 15.1 fusion.397
  1750.5 15.1 fusion.397
  1778.0 15.1 fusion.397
  1805.5 15.1 fusion.397
  1833.0 15.1 fusion.397
  1876.5 439.5 %while.112 = (s32[]{:T(128)}, f32[192]{0:T(256)S(1)}, f32[16,128,192]{1,0,2:T(8,128)}, f32[16,128,192]{1,0,2:T(8,128)}, f32[16,192]{1,0:T(8,128)}, /*index=5*/f3...) while((s32[]{:T(128)}, f32[192]{0:T(256)S(1)}, ...), condition=%wide.region_86.90_spmd.clone, body=%wide.region_81.89_spmd.clone.sunk | while | flops 154386240 | bytes 4445589 | solution.py:84
  1880.5 15.1 fusion.407
  1907.9 15.1 fusion.407
  1935.4 15.1 fusion.407
  1962.8 15.1 fusion.407
  1990.3 15.1 fusion.407
  2017.7 15.1 fusion.407
  2045.2 15.1 fusion.407
  2072.7 15.1 fusion.407
  2100.1 15.1 fusion.407
  2127.6 15.1 fusion.407
  2155.1 15.1 fusion.407
  2182.6 15.1 fusion.407
  2210.0 15.1 fusion.407
  2237.5 15.1 fusion.407
  2265.0 15.1 fusion.407
  2292.5 15.1 fusion.407
  2479.3 22.2 psum.75
  2503.8 41.6 %all-reduce.28 = (f32[4,768]{1,0:T(4,128)}, f32[4,768]{1,0:T(4,128)}) all-reduce(f32[4,768]{1,0:T(4,128)S(1)} %maximum_add_fusion, f32[4,768]{1,0:T(4,128)S(1)} %maximum_add_fusion.1), channel_id=1, replica_groups=mesh['dp'=8,'tensor'=4] {'dp','tensor'}, use_global_device_ids=true, to_apply=%region_106.110 | all-reduce | flops 6144 | bytes 49152 | tf_op jit(solution)/shard_map/psum | solution.py:381
  2548.5 387.8 %all-reduce.34.cloned.1.call-done = (f32[768,3,192]{0,2,1:T(8,128)}, f32[192,768]{1,0:T(8,128)}, f32[768,768]{1,0:T(8,128)}, f32[768,768]{1,0:T(8,128)}, f32[256...) async-done(((f32[768,3,192]{0,2,1:T(8,128)}, f32[192,768]{1,0:T(8,128)}, f32[768,768]{1,0:T(8,128)}, f32[768,768]{1,0:T(8,128)}, ...) | async-done | bytes 12189712 | tf_op jit(solution)/shard_map/psum | solution.py:142
  (1866 shorter events, 1675.4 us)
Async XLA Ops:
  7.2 359.2 %copy-start = (bf16[768,768]{1,0:T(8,128)(2,1)S(1)}, bf16[768,768]{1,0:T(8,128)(2,1)}, u32[]{:S(2)}) copy-start(bf16[768,768]{1,0:T(8,128)(2,1)} %param.39) | copy-start | bytes 3538948
  7.2 12.6 copy-start.69
  7.2 345.8 %reduce-scatter.15.cloned.1.call-start = ((), (), s32[]{:S(2)}) async-start(), calls=%async_computation.14 | async-start | bytes 983040 | tf_op jit(solution)/shard_map/reduce_scatter | solution.py:218
  8.6 13.8 copy-start.33
  26.4 327.7 %reduce-scatter.21.cloned.1.call-start = ((), (), s32[]{:S(2)}) async-start(), calls=%async_computation.17 | async-start | bytes 983040 | tf_op jit(solution)/shard_map/reduce_scatter | solution.py:218
  41.9 332.6 %all-gather.15.cloned.1.call-start = ((), (), s32[]{:S(2)}) async-start(), calls=%async_computation.31 | async-start | bytes 1310720 | tf_op jit(solution)/shard_map/all_gather | solution.py:197
  42.8 335.2 %all-gather.13.cloned.1.call-start = ((), (), s32[]{:S(2)}) async-start(), calls=%async_computation.30 | async-start | bytes 1310720 | tf_op jit(solution)/shard_map/all_gather | solution.py:197
  43.4 763.3 %reduce-scatter.17.cloned.1.call-start = ((), (), s32[]{:S(2)}) async-start(), calls=%async_computation.15 | async-start | bytes 983040 | tf_op jit(solution)/shard_map/reduce_scatter | solution.py:229
  330.4 13.7 copy-start.183
  330.4 14.3 copy-start.184
  330.4 14.9 copy-start.134
  344.7 11.2 copy-start.142
  345.3 10.6 copy-start.152
  354.0 17.7 copy-start.177
  374.3 516.3 %reduce-scatter.23.cloned.1.call-start = ((), (), s32[]{:S(2)}) async-start(), calls=%async_computation.18 | async-start | bytes 983040 | tf_op jit(solution)/shard_map/reduce_scatter | solution.py:229
  825.8 410.4 %reduce-scatter.25.cloned.1.call-start = ((), (), s32[]{:S(2)}) async-start(), calls=%async_computation.19 | async-start | bytes 1966080 | tf_op jit(solution)/shard_map/reduce_scatter | solution.py:254
  851.3 10.7 copy-start.190
  853.8 11.1 copy-start.189
  853.8 13.2 copy-start.225
  891.7 345.5 %copy-start.175 = (f32[128]{0:T(128)}, f32[128]{0:T(128)S(1)}, u32[]{:S(2)}) copy-start(f32[128]{0:T(128)S(1)} %broadcast_multiply_fusion.3) | copy-start | bytes 1540
  891.9 9.6 copy-start.236
  892.0 9.6 copy-start.200
  909.8 375.8 %reduce-scatter.19.cloned.1.call-start = ((), (), s32[]{:S(2)}) async-start(), calls=%async_computation.16 | async-start | bytes 1966080 | tf_op jit(solution)/shard_map/reduce_scatter | solution.py:254
  1207.1 11.0 copy-start.224
  1256.4 30.3 %copy-start.14 = (f32[128,768]{1,0:T(8,128)S(1)}, f32[128,768]{1,0:T(8,128)}, u32[]{:S(2)}) copy-start(f32[128,768]{1,0:T(8,128)} %get-tuple-element.1308) | copy-start | bytes 1179652
  1256.4 30.3 %copy-start.181 = (f32[128]{0:T(128)S(1)}, f32[128]{0:T(128)}, u32[]{:S(2)}) copy-start(f32[128]{0:T(128)} %copy-done.180) | copy-start | bytes 1540
  1256.5 58.6 %all-gather.11.cloned.1.call-start = ((), (), s32[]{:S(2)}) async-start(), calls=%async_computation.24 | async-start | bytes 1966080 | tf_op jit(solution)/shard_map/all_gather | solution.py:272
  1257.2 28.5 copy-start.209
  1295.3 40.9 %all-gather.9.cloned.1.call-start = ((), (), s32[]{:S(2)}) async-start(), calls=%async_computation.20 | async-start | bytes 1966080 | tf_op jit(solution)/shard_map/all_gather | solution.py:272
  1298.0 19.6 copy-start.207
  1301.0 89.4 %all-reduce.36.cloned.1.call-start = ((), (), s32[]{:S(2)}) async-start(), calls=%async_computation.33 | async-start | bytes 3145728
  1347.1 972.2 %reduce-scatter.33.cloned.1.call-start = ((), (), s32[]{:S(2)}) async-start(), calls=%async_computation.25 | async-start | bytes 983040 | tf_op jit(solution)/shard_map/reduce_scatter | solution.py:286
  1353.3 966.0 %reduce-scatter.27.cloned.1.call-start = ((), (), s32[]{:S(2)}) async-start(), calls=%async_computation.21 | async-start | bytes 983040 | tf_op jit(solution)/shard_map/reduce_scatter | solution.py:286
  1374.1 1052.0 %reduce-scatter.29.cloned.1.call-start = ((), (), s32[]{:S(2)}) async-start(), calls=%async_computation.22 | async-start | bytes 983040 | tf_op jit(solution)/shard_map/reduce_scatter | solution.py:305
  2321.6 9.5 copy-start.249
  2321.6 9.5 copy-start.252
  2321.6 9.4 copy-start.253
  2334.8 91.3 %reduce-scatter.35.cloned.1.call-start = ((), (), s32[]{:S(2)}) async-start(), calls=%async_computation.26 | async-start | bytes 983040 | tf_op jit(solution)/shard_map/reduce_scatter | solution.py:305
  2350.1 12.9 copy-start.250
  2368.9 132.6 %reduce-scatter.41.cloned.1.call-start = ((), (), s32[]{:S(2)}) async-start(), calls=%async_computation.29 | async-start | bytes 1310720 | tf_op jit(solution)/shard_map/reduce_scatter | solution.py:358
  2384.9 116.7 %reduce-scatter.39.cloned.1.call-start = ((), (), s32[]{:S(2)}) async-start(), calls=%async_computation.28 | async-start | bytes 1310720 | tf_op jit(solution)/shard_map/reduce_scatter | solution.py:358
  2416.4 129.0 %reduce-scatter.37.cloned.1.call-start = ((), (), s32[]{:S(2)}) async-start(), calls=%async_computation.27 | async-start | bytes 983040 | tf_op jit(solution)/shard_map/reduce_scatter | solution.py:355
  2428.5 10.0 copy-start.55
  2428.5 10.9 copy-start.4
  2429.0 9.9 copy-start.67
  2429.0 15.4 copy-start.65
  2429.0 10.3 copy-start.36
  2429.0 10.3 copy-start.98
  2429.1 10.3 copy-start.150
  2429.1 11.4 copy-start.220
  2444.4 10.3 copy-start.89
  2444.4 10.3 copy-start.70
  2444.4 12.0 copy-start.222
  2456.5 90.0 %reduce-scatter.31.cloned.1.call-start = ((), (), s32[]{:S(2)}) async-start(), calls=%async_computation.23 | async-start | bytes 983040 | tf_op jit(solution)/shard_map/reduce_scatter | solution.py:355
  2466.2 470.0 %all-reduce.34.cloned.1.call-start = ((), (), s32[]{:S(2)}) async-start(), calls=%async_computation.32 | async-start | bytes 26738688 | tf_op jit(solution)/shard_map/psum | solution.py:142
  2476.7 24.8 copy-start.167
  2477.7 26.0 copy-start.171
  2477.7 26.0 copy-start.170
  2477.7 26.0 copy-start.169
  2477.7 26.0 copy-start.168
  2477.7 67.7 %copy-start.68 = (f32[128,768]{1,0:T(8,128)S(1)}, f32[128,768]{1,0:T(8,128)}, u32[]{:S(2)}) copy-start(f32[128,768]{1,0:T(8,128)} %copy-done.67) | copy-start | bytes 1179652
  2477.7 67.7 %copy-start.221 = (f32[128]{0:T(128)S(1)}, f32[128]{0:T(128)}, u32[]{:S(2)}) copy-start(f32[128]{0:T(128)} %copy-done.220) | copy-start | bytes 1540
  2478.5 68.0 %copy-start.66 = (f32[128,768]{1,0:T(8,128)S(1)}, f32[128,768]{1,0:T(8,128)}, u32[]{:S(2)}) copy-start(f32[128,768]{1,0:T(8,128)} %copy-done.65) | copy-start | bytes 1179652
  2478.5 68.0 %copy-start.223 = (f32[128]{0:T(128)S(1)}, f32[128]{0:T(128)}, u32[]{:S(2)}) copy-start(f32[128]{0:T(128)} %copy-done.222) | copy-start | bytes 1540
  (225 other events, 537.4 us)
Sparse Core Ops, SparseCore 0:
  26.5 24.1 reduce-scatter.14
  54.0 23.2 reduce-scatter.20
  79.4 16.7 all-gather.14
  98.2 16.7 all-gather.12
  374.4 24.1 reduce-scatter.16
  825.9 24.2 reduce-scatter.22
  909.9 29.0 reduce-scatter.24
  1256.6 28.9 reduce-scatter.18
  1295.4 19.6 all-gather.10
  1316.5 19.6 all-gather.8
  1347.2 43.0 all-reduce.35
  1393.3 23.2 reduce-scatter.32
  1419.3 23.2 reduce-scatter.26
  2335.0 27.8 reduce-scatter.28
  2369.0 23.3 reduce-scatter.34
  2395.4 24.8 reduce-scatter.40
  2423.4 24.9 reduce-scatter.38
  2456.6 23.3 reduce-scatter.36
  2483.3 23.2 reduce-scatter.30
  2512.7 423.4 all-reduce.33
where the time goes:
time: 2980 us; the launch traced here: 2960 us
  other arithmetic  1050 us (35%)
  local copies, waits for them, and re-layouts  1040 us (35%)
  waiting for transfers between devices  447 us (15%)
  matrix products  216 us (7%)
  blocking collectives  176 us (6%)
    reduce_sum x32, other arithmetic, block_step(): gap = jnp.where(linked, level[:, None, :] - level[None, :, :], 0.0)  483 us
    reduce_sum x32, other arithmetic, block_step(): inside = jnp.sum(weights * drive_block[None, :, :], axis=1)  421 us
    psum x1, waiting for transfers between devices, reduce_weights(): lax.psum((grads[0], grads[1], grads[2], grads[3], grads[4], grads[5], gra...  388 us
    dynamic_update_slice x96, local copies, waits for them, and re-layouts, gru_tokens(): lax.scan(jax.checkpoint(block_step), start, (drive_all.reshape(block_tota...  277 us
    gather x20, local copies, waits for them, and re-layouts, layout(): char_token = jnp.searchsorted(token_ends, char_positions, side='right')  264 us
    dot_general x96, matrix products, block_step(): jnp.dot(lower, log_block, precision=HIGH_PRECISION, preferred_element_typ...  65.8 us
    unnamed x529, local copies, waits for them, and re-layouts  65.1 us
    squeeze x64, local copies, waits for them, and re-layouts, gru_tokens(): lax.scan(jax.checkpoint(block_step), start, (drive_all.reshape(block_tota...  62.5 us
  transfers between devices with their start and end apart: 20, of which 5 were waited for; matrix products, arithmetic and copies ran while one was open for 75% of the time, Pallas kernels for 0%

commit v1 on v0

--- a/solution.py
+++ b/solution.py
@@ -1,6 +1,8 @@
 import jax
 import jax.numpy as jnp
 from jax import lax
+from jax.experimental import pallas as pl
+from jax.experimental.pallas import tpu as pltpu
 from jax.sharding import PartitionSpec as P
 
 HD = 64
@@ -24,82 +26,167 @@
 
 def layout(doc_sizes, char_counts, char_total):
     length = char_counts.shape[0]
-    doc_ends = jnp.cumsum(doc_sizes, dtype=jnp.int32)
+    docs = doc_sizes.shape[0]
+    doc_ids = jnp.arange(docs, dtype=jnp.int32)
+    doc_ends = jnp.sum(
+        jnp.where(doc_ids[None, :] <= doc_ids[:, None], doc_sizes[None, :], 0), axis=1
+    )
     positions = jnp.arange(length, dtype=jnp.int32)
     segment = jnp.sum(
         (positions[:, None] >= doc_ends[None, :]).astype(jnp.int32), axis=1, dtype=jnp.int32
     )
-    token_ends = jnp.cumsum(char_counts, dtype=jnp.int32)
-    char_positions = jnp.arange(char_total, dtype=jnp.int32)
-    char_token = jnp.searchsorted(token_ends, char_positions, side="right")
+    token_ends = jnp.sum(
+        jnp.where(positions[None, :] <= positions[:, None], char_counts[None, :], 0), axis=1
+    )
     last_char = token_ends - 1
     first_char = token_ends - char_counts
-    char_segment = jnp.take(segment, char_token)
-    char_same = (char_segment[1:] == char_segment[:-1]).astype(jnp.float32)
-    token_same = (segment[1:] == segment[:-1]).astype(jnp.float32)
-    zero_one = jnp.zeros((1,), jnp.float32)
-    keep_forward = jnp.concatenate([zero_one, char_same])
-    keep_backward = jnp.concatenate([char_same, zero_one])
-    prev_ok = jnp.concatenate([zero_one, token_same])
-    next_ok = jnp.concatenate([token_same, zero_one])
+    char_ends = jnp.sum(
+        jnp.where(positions[None, :] < doc_ends[:, None], char_counts[None, :], 0), axis=1
+    )
+    char_positions = jnp.arange(char_total, dtype=jnp.int32)
+    starts = char_ends - jnp.sum(
+        jnp.where(
+            (positions[None, :] < doc_ends[:, None])
+            & (positions[None, :] >= (doc_ends - doc_sizes)[:, None]),
+            char_counts[None, :],
+            0,
+        ),
+        axis=1,
+    )
+    keep_forward = 1.0 - jnp.any(char_positions[:, None] == starts[None, :], axis=1).astype(
+        jnp.float32
+    )
+    keep_backward = 1.0 - jnp.any(
+        char_positions[:, None] == (char_ends - 1)[None, :], axis=1
+    ).astype(jnp.float32)
+    token_starts = doc_ends - doc_sizes
+    prev_ok = 1.0 - jnp.any(positions[:, None] == token_starts[None, :], axis=1).astype(
+        jnp.float32
+    )
+    next_ok = 1.0 - jnp.any(positions[:, None] == (doc_ends - 1)[None, :], axis=1).astype(
+        jnp.float32
+    )
     return (segment, first_char, last_char, keep_forward, keep_backward, prev_ok, next_ok)
 
 
-def gru_tokens(projected, gate_bias, keep_forward, keep_backward, first_char, last_char):
-    char_total = projected.shape[0]
-    units = projected.shape[3]
-    logits = projected[:, :, 0, :] + gate_bias[None]
-    gates = jax.nn.sigmoid(logits)
-    drive = gates * projected[:, :, 1, :]
-    log_decay = -jax.nn.softplus(logits)
-    drive_all = jnp.concatenate([drive[:, 0], jnp.flip(drive[:, 1], axis=0)], axis=1)
-    log_all = jnp.concatenate([log_decay[:, 0], jnp.flip(log_decay[:, 1], axis=0)], axis=1)
-    cut_forward = jnp.broadcast_to((1.0 - keep_forward)[:, None], (char_total, units))
-    cut_backward = jnp.broadcast_to(
-        jnp.flip(1.0 - keep_backward, axis=0)[:, None], (char_total, units)
-    )
-    cut_all = jnp.concatenate([cut_forward, cut_backward], axis=1)
-    block_size = min(128, char_total)
-    block_total = char_total // block_size
-    row_ids = jnp.arange(block_size, dtype=jnp.int32)
-    lower = (row_ids[:, None] >= row_ids[None, :]).astype(jnp.float32)
-
-    def block_step(carry, pieces):
-        drive_block, log_block, cut_block = pieces
-        level = jnp.dot(
-            lower, log_block, precision=HIGH_PRECISION, preferred_element_type=jnp.float32
-        )
-        resets = jnp.dot(
-            lower, cut_block, precision=HIGH_PRECISION, preferred_element_type=jnp.float32
-        )
-        linked = (resets[:, None, :] == resets[None, :, :]) & (lower[:, :, None] > 0.5)
-        gap = jnp.where(linked, level[:, None, :] - level[None, :, :], 0.0)
-        weights = jnp.where(linked, jnp.exp(gap), 0.0)
-        inside = jnp.sum(weights * drive_block[None, :, :], axis=1)
-        entering = jnp.where(resets < 0.5, jnp.exp(level), 0.0) * carry[None, :]
-        states = inside + entering
-        return (states[-1], states)
-
-    start = jnp.zeros((2 * units,), jnp.float32)
-    unused_last, states = lax.scan(
-        jax.checkpoint(block_step),
-        start,
-        (
-            drive_all.reshape(block_total, block_size, 2 * units),
-            log_all.reshape(block_total, block_size, 2 * units),
-            cut_all.reshape(block_total, block_size, 2 * units),
-        ),
-    )
-    states = states.reshape(char_total, 2 * units)
-    forward_states = states[:, :units]
-    backward_states = jnp.flip(states[:, units:], axis=0)
-    return jnp.stack(
-        [
-            jnp.take(forward_states, last_char, axis=0),
-            jnp.take(backward_states, first_char, axis=0),
-        ],
-        axis=1,
-    )
+LANE = 128
+CHUNKS = 32
+VMEM = pl.BlockSpec(memory_space=pltpu.VMEM)
+
+
+def recur(first, second, decays, drives, outs, steps):
+    ups = (first, second)
+
+    def at(ref, tile, step):
+        row = step if ups[tile] else steps - 1 - step
+        return ref[tile, pl.ds(row, CHUNKS, stride=steps), :]
+
+    def put(ref, tile, step, value):
+        row = step if ups[tile] else steps - 1 - step
+        ref[tile, pl.ds(row, CHUNKS, stride=steps), :] = value
+
+    zero = jnp.zeros((CHUNKS, LANE), jnp.float32)
+    one = jnp.ones((CHUNKS, LANE), jnp.float32)
+
+    def summary(step, carry):
+        new = []
+        for tile in range(2):
+            state, mult = carry[2 * tile], carry[2 * tile + 1]
+            decay = at(decays, tile, step)
+            new += [decay * state + at(drives, tile, step), decay * mult]
+        return tuple(new)
+
+    ends = lax.fori_loop(0, steps, summary, (zero, one, zero, one), unroll=4)
+    starts = []
+    for tile in range(2):
+        final, mult = ends[2 * tile], ends[2 * tile + 1]
+        order = range(CHUNKS) if ups[tile] else range(CHUNKS - 1, -1, -1)
+        carry = jnp.zeros((1, LANE), jnp.float32)
+        rows = [None] * CHUNKS
+        for chunk in order:
+            rows[chunk] = carry
+            carry = mult[chunk : chunk + 1] * carry + final[chunk : chunk + 1]
+        starts.append(jnp.concatenate(rows, axis=0))
+
+    def write(step, carry):
+        new = []
+        for tile in range(2):
+            state = at(decays, tile, step) * carry[tile] + at(drives, tile, step)
+            put(outs, tile, step, state)
+            new.append(state)
+        return tuple(new)
+
+    lax.fori_loop(0, steps, write, tuple(starts), unroll=4)
+
+
+def gates_of(chars, w_ref, bias_ref, keep_ref, gate_ref, cand_ref, decay_ref, drive_ref):
+    proj = jnp.dot(chars, w_ref[...], preferred_element_type=jnp.float32)
+    for tile in range(2):
+        cols = pl.ds(tile * LANE, LANE)
+        logits = proj[:, tile * LANE : (tile + 1) * LANE] + bias_ref[:, cols]
+        gate = jax.nn.sigmoid(logits)
+        cand = proj[:, (2 + tile) * LANE : (3 + tile) * LANE]
+        gate_ref[tile] = gate
+        cand_ref[tile] = cand
+        decay_ref[tile] = (1.0 - gate) * keep_ref[:, tile : tile + 1]
+        drive_ref[tile] = gate * cand
+
+
+def gru_fwd_kernel(chars_ref, w_ref, bias_ref, keep_ref, pick_ref, tok_ref, state_ref,
+                   gate_ref, cand_ref, decay_ref, drive_ref):
+    total = chars_ref.shape[0]
+    steps = total // CHUNKS
+    gates_of(chars_ref[...], w_ref, bias_ref, keep_ref, gate_ref, cand_ref, decay_ref, drive_ref)
+    recur(True, False, decay_ref, drive_ref, state_ref, steps)
+    length = pick_ref.shape[0]
+    ids = lax.broadcasted_iota(jnp.int32, (length, total), 1)
+    for tile in range(2):
+        hot = (ids == pick_ref[:, tile : tile + 1]).astype(jnp.bfloat16)
+        cols = pl.ds(tile * LANE, LANE)
+        low = state_ref[tile].astype(jnp.bfloat16)
+        tok_ref[:, cols] = jnp.dot(hot, low, preferred_element_type=jnp.float32).astype(
+            jnp.bfloat16
+        )
+
+
+def gru_bwd_kernel(chars_ref, w_ref, bias_ref, keep_ref, pick_ref, state_ref, grad_ref,
+                   proj_grad_ref, bias_grad_ref, gate_ref, cand_ref, decay_ref, drive_ref, flow_ref):
+    total = chars_ref.shape[0]
+    steps = total // CHUNKS
+    gates_of(chars_ref[...], w_ref, bias_ref, keep_ref, gate_ref, cand_ref, decay_ref, drive_ref)
+    length = pick_ref.shape[1]
+    ids = lax.broadcasted_iota(jnp.int32, (total, length), 0)
+    for tile in range(2):
+        hot = (ids == pick_ref[tile : tile + 1, :]).astype(jnp.bfloat16)
+        cols = pl.ds(tile * LANE, LANE)
+        drive_ref[tile] = jnp.dot(hot, grad_ref[:, cols], preferred_element_type=jnp.float32)
+    flow_ref[0, pl.ds(0, total - 1), :] = decay_ref[0, pl.ds(1, total - 1), :]
+    flow_ref[0, pl.ds(total - 1, 1), :] = jnp.zeros((1, LANE), jnp.float32)
+    flow_ref[1, pl.ds(1, total - 1), :] = decay_ref[1, pl.ds(0, total - 1), :]
+    flow_ref[1, pl.ds(0, 1), :] = jnp.zeros((1, LANE), jnp.float32)
+    recur(False, True, flow_ref, drive_ref, decay_ref, steps)
+    for tile in range(2):
+        flow = decay_ref[tile] * gate_ref[tile]
+        logit_grad = flow * (cand_ref[tile] - state_ref[tile])
+        proj_grad_ref[:, pl.ds(tile * LANE, LANE)] = logit_grad.astype(jnp.bfloat16)
+        proj_grad_ref[:, pl.ds((2 + tile) * LANE, LANE)] = flow.astype(jnp.bfloat16)
+        bias_grad_ref[:, pl.ds(tile * LANE, LANE)] = jnp.sum(logit_grad, axis=0, keepdims=True)
+
+
+def gru_call(kernel, outs, scratch_count, total):
+    return pl.pallas_call(
+        kernel,
+        out_shape=outs,
+        scratch_shapes=[pltpu.VMEM((2, total, LANE), jnp.float32)] * scratch_count,
+        compiler_params=pltpu.CompilerParams(vmem_limit_bytes=48 * 1024 * 1024),
+    )
+
+
+def gru_weights(w_gru, gate_bias):
+    width, _, _, units = w_gru.shape
+    matrix = jnp.pad(jnp.swapaxes(w_gru, 1, 2), ((0, 0), (0, 0), (0, 0), (0, LANE - units)))
+    bias = jnp.pad(gate_bias, ((0, 0), (0, LANE - units)))
+    return matrix.reshape(width, 4 * LANE), bias.reshape(1, 2 * LANE)
 
 
 def conv_inputs(joined, prev_ok, next_ok):
@@ -139,9 +226,8 @@
 
 
 def reduce_weights(grads):
-    return lax.psum(
-        (grads[0], grads[1], grads[2], grads[3], grads[4], grads[5], grads[6], grads[7]), "dp"
-    )
+    low = lax.psum(tuple(g.astype(jnp.bfloat16) for g in grads), "dp")
+    return tuple(g.astype(jnp.float32) for g in low)
 
 
 def local(
@@ -176,7 +262,7 @@
     merge_here = w_conv.shape[2]
     row_start = group_rank * shard_len
     qkv_matrix = w_qkv.reshape(model_width, 3 * head_cols)
-    gru_matrix = w_gru.reshape(char_width, 4 * units_here)
+    gru_matrix, gru_bias = gru_weights(w_gru, gate_bias)
     conv_matrix = w_conv.reshape(3 * 2 * model_width, merge_here)
     merge_matrix = w_merge.reshape(merge_here, 2 * model_width)
     token_outs = []
@@ -234,14 +320,18 @@
         ).astype(jnp.float32)
         residual_two = hidden + ffn_share
         token_mid = layer_norm(residual_two, norm_gain[1], norm_bias[1])
-        projected = jnp.dot(all_chars, gru_matrix, preferred_element_type=jnp.float32).reshape(
-            char_total, 2, 2, units_here
-        )
-
-        def char_path(proj_in, bias_in):
-            return gru_tokens(proj_in, bias_in, keep_forward, keep_backward, first_char, last_char)
-
-        char_tokens, pull_gru = jax.vjp(char_path, projected, gate_bias)
+        keep = jnp.stack([keep_forward, keep_backward], axis=1)
+        picks = jnp.stack([last_char, first_char], axis=1)
+        char_padded, char_states = gru_call(
+            gru_fwd_kernel,
+            (
+                jax.ShapeDtypeStruct((length, 2 * LANE), jnp.bfloat16),
+                jax.ShapeDtypeStruct((2, char_total, LANE), jnp.float32),
+            ),
+            4,
+            char_total,
+        )(all_chars, gru_matrix, gru_bias, keep, picks)
+        char_tokens = char_padded.reshape(length, 2, LANE)[:, :, :units_here]
         mid_all, char_all = (
             lax.all_gather(token_mid.astype(jnp.bfloat16), "tensor", axis=0, tiled=True),
             lax.all_gather(char_tokens.astype(jnp.bfloat16), "tensor", axis=2, tiled=True),
@@ -347,9 +437,24 @@
         ).reshape(length, 3 * head_cols)
         grad_qkv_w = inner_rows(all_tokens, grad_qkv_low)
         token_part = times_transposed(grad_qkv_low, qkv_matrix)
-        grad_projected, grad_gate = pull_gru(grad_char_tokens)
-        grad_proj_low = grad_projected.reshape(char_total, 4 * units_here).astype(jnp.bfloat16)
-        grad_gru_w = inner_rows(all_chars, grad_proj_low)
+        grad_tok_pad = jnp.pad(
+            grad_char_tokens.astype(jnp.bfloat16), ((0, 0), (0, 0), (0, LANE - units_here))
+        ).reshape(length, 2 * LANE)
+        grad_proj_low, grad_gate = gru_call(
+            gru_bwd_kernel,
+            (
+                jax.ShapeDtypeStruct((char_total, 4 * LANE), jnp.bfloat16),
+                jax.ShapeDtypeStruct((1, 2 * LANE), jnp.float32),
+            ),
+            5,
+            char_total,
+        )(all_chars, gru_matrix, gru_bias, keep, picks.T, char_states, grad_tok_pad)
+        grad_gate = grad_gate.reshape(2, LANE)[:, :units_here]
+        grad_gru_w = jnp.swapaxes(
+            inner_rows(all_chars, grad_proj_low).reshape(char_width, 2, 2, LANE)[..., :units_here],
+            1,
+            2,
+        )
         char_part = times_transposed(grad_proj_low, gru_matrix)
         token_back, char_back = (
             lax.psum_scatter(
@@ -368,7 +473,7 @@
             grad_out_w,
             grad_in_w,
             grad_down_w,
-            grad_gru_w.reshape(char_width, 2, 2, units_here),
+            grad_gru_w,
             grad_gate,
             grad_conv_w.reshape(3, 2 * model_width, merge_here),
             grad_merge_w.reshape(merge_here, 2, model_width),

time: 2980 us -> 857 us (0.29)
  other arithmetic: 1050 us -> 70.2 us
  local copies, waits for them, and re-layouts: 1040 us -> 96.1 us
  matrix products: 216 us -> 95.6 us
  waiting for transfers between devices: 447 us -> 337 us
  Pallas kernels: 0 us -> 44.9 us
    reduce_sum x66 -> x6, other arithmetic: 914 us -> 0.97 us  [the longest x2 0.44 us: layout(): jnp.sum(jnp.where((positions[None, :] < doc_ends[:, None]) & (positions[N...]
    gather x26 -> x0, local copies, waits for them, and re-layouts: 300 us -> none  [the longest x20 264 us: layout(): char_token = jnp.searchsorted(token_ends, char_positions, side='right')]
    dynamic_update_slice x96 -> x0, local copies, waits for them, and re-layouts: 277 us -> none  [gru_tokens(): lax.scan(jax.checkpoint(block_step), start, (drive_all.reshape(block_tota...]
    psum x1, waiting for transfers between devices: 388 us -> 209 us  [reduce_weights(): low = lax.psum(tuple((g.astype(jnp.bfloat16) for g in grads)), 'dp')]
    dot_general x162 -> x0, matrix products: 124 us -> none  [the longest x96 65.8 us: block_step(): jnp.dot(lower, log_block, precision=HIGH_PRECISION, preferred_element_typ...]
    rev x12 -> x0, local copies, waits for them, and re-layouts: 95.4 us -> none  [the longest x4 36.2 us: gru_tokens(): jnp.flip(log_decay[:, 1], axis=0)]
    squeeze x66 -> x0, local copies, waits for them, and re-layouts: 68 us -> none  [the longest x64 62.5 us: gru_tokens(): lax.scan(jax.checkpoint(block_step), start, (drive_all.reshape(block_tota...]
    pallas_call x0 -> x4, Pallas kernels: none -> 44.9 us  [the longest x2 25.4 us: local(): gru_call(gru_bwd_kernel, (jax.ShapeDtypeStruct((char_total, 4 * LANE), jn...]
  transfers between devices with their start and end apart: 20 -> 20, of which waited for: 5 -> 9; matrix products, arithmetic and copies ran while one was open for 75% -> 22% of each run, Pallas kernels for 0% -> 5%
where the time goes in v1:
time: 857 us; the launch traced here: 846 us
  waiting for transfers between devices  337 us (39%)
  blocking collectives  182 us (21%)
  local copies, waits for them, and re-layouts  96.1 us (11%)
  matrix products  95.6 us (11%)
  other arithmetic  70.2 us (8%)
  Pallas kernels  44.9 us (5%)
  between operations  18.1 us (2%)
    psum x1, waiting for transfers between devices, reduce_weights(): low = lax.psum(tuple((g.astype(jnp.bfloat16) for g in grads)), 'dp')  209 us
    unnamed x390, local copies, waits for them, and re-layouts  44.1 us
    psum x1, blocking collectives, local(): gain_grad, bias_grad = lax.psum((gain_total, bias_total), ('dp', 'tensor'))  38 us
    reduce_scatter x2, waiting for transfers between devices, local(): lax.psum_scatter(jnp.dot(context_low, w_out, preferred_element_type=jnp.f...  34.8 us
    dot_general x14, matrix products, inner_rows(): lax.dot_general(left_rows, right_rows, (((0,), (0,)), ((), ())), preferre...  29.6 us
    all_gather x2, waiting for transfers between devices, local(): branch_all = lax.all_gather(branch_grad, 'tensor', axis=0, tiled=True)  26.2 us
    pallas_call x2, Pallas kernels, local(): gru_call(gru_bwd_kernel, (jax.ShapeDtypeStruct((char_total, 4 * LANE), jn...  25.4 us
    all_gather x2, blocking collectives, local(): lax.all_gather(char_tokens.astype(jnp.bfloat16), 'tensor', axis=2, tiled=...  24.9 us
  transfers between devices with their start and end apart: 20, of which 9 were waited for; matrix products, arithmetic and copies ran while one was open for 22% of the time, Pallas kernels for 5%

profile of v1, /device:TPU:0, one launch (start us, length us, event | category | flops | bytes accessed | tf_op | source)
XLA Modules:
  0.0 846.3 jit_solution(11410807563333743844)
XLA Ops:
  9.7 10.1 %all-gather = bf16[1,512,768]{2,1,0:T(8,128)(2,1)S(1)} all-gather(bf16[1,128,768]{2,1,0:T(8,128)(2,1)S(1)} %get-tuple-element.192), channel_id=2, replica_groups=mesh['dp'=8,'tensor'=4] {'tensor'}, dimensions={1}, use_global_device_ids=true | all-gather | bytes 983040 | tf_op jit(solution)/shard_map/all_gather | solution.py:282
  26.5 8.7 %all-gather.2 = bf16[1,512,768]{2,1,0:T(8,128)(2,1)S(1)} all-gather(bf16[1,128,768]{2,1,0:T(8,128)(2,1)S(1)} %get-tuple-element.191), channel_id=4, replica_groups=mesh['dp'=8,'tensor'=4] {'tensor'}, dimensions={1}, use_global_device_ids=true | all-gather | bytes 983040 | tf_op jit(solution)/shard_map/all_gather | solution.py:282
  41.3 9.2 %reduce-scatter.15.cloned.1.call-done = bf16[128,768]{1,0:T(8,128)(2,1)} async-done(((bf16[512,768]{1,0:T(8,128)(2,1)}), bf16[128,768]{1,0:T(8,128)(2,1)}) %reduce-scatter.15.cloned.1.call-update) | async-done | bytes 196624 | tf_op jit(solution)/shard_map/reduce_scatter | solution.py:304
  51.6 25.5 %reduce-scatter.21.cloned.1.call-done = bf16[128,768]{1,0:T(8,128)(2,1)} async-done(((bf16[512,768]{1,0:T(8,128)(2,1)}), bf16[128,768]{1,0:T(8,128)(2,1)}) %reduce-scatter.21.cloned.1.call-update) | async-done | bytes 196624 | tf_op jit(solution)/shard_map/reduce_scatter | solution.py:304
  79.7 8.2 all_gather.49
  87.8 5.4 multiply_convert_fusion.3
  95.0 2.0 fusion.153
  97.1 21.7 %reduce-scatter.17.cloned.1.call-done = bf16[128,768]{1,0:T(8,128)(2,1)} async-done(((bf16[512,768]{1,0:T(8,128)(2,1)}), bf16[128,768]{1,0:T(8,128)(2,1)}) %reduce-scatter.17.cloned.1.call-update) | async-done | bytes 196624 | tf_op jit(solution)/shard_map/reduce_scatter | solution.py:315
  120.6 8.6 %all_gather.54 = bf16[512,768]{1,0:T(8,128)(2,1)S(1)} all-gather(bf16[128,768]{1,0:T(8,128)(2,1)S(1)} %get-tuple-element.182), channel_id=1, replica_groups=mesh['dp'=8,'tensor'=4] {'tensor'}, dimensions={0}, use_global_device_ids=true | all-gather | bytes 983040 | tf_op jit(solution)/shard_map/all_gather | solution.py:312
  129.3 5.4 multiply_convert_fusion.2
  140.7 3.2 copy.134
  145.1 9.8 %shard_map.264 = (bf16[512,256]{1,0:T(8,128)(2,1)S(1)}, f32[2,2048,128]{2,1,0:T(8,128)S(1)}) custom-call(bf16[2048,256]{1,0:T(8,128)(2,1)S(1)} %bitcast.345, bf16[256,512]{1,0:T(8,128)(2,1)S(1)} %reshape.634.w_ref, f32[1,256]{1,0:T(1,128)S(1)} %bitcast.351, f32[2048,2]{1,0:T(8,128)S(1)} %copy.98.keep_ref, s32[512,2]{1,0:T(8,128)S(1)} %copy.99.pick_ref), custom_call_target="tpu_custom_call" | custom-call | tf_op jit(solution)/shard_map/pallas_call | solution.py:325
  156.6 12.0 %all_gather.57 = bf16[512,2,384]{0,1,2:T(2,128)(2,1)} all-gather(bf16[512,2,96]{0,1,2:T(2,128)(2,1)S(1)} %copy.128), channel_id=1, replica_groups=mesh['dp'=8,'tensor'=4] {'tensor'}, dimensions={2}, use_global_device_ids=true | all-gather | bytes 983040 | tf_op jit(solution)/shard_map/all_gather | solution.py:337
  168.7 2.7 copy.101
  174.0 12.6 %all_gather.55 = bf16[512,768]{1,0:T(8,128)(2,1)S(1)} all-gather(bf16[128,768]{1,0:T(8,128)(2,1)S(1)} %fusion.63), channel_id=1, replica_groups=mesh['dp'=8,'tensor'=4] {'tensor'}, dimensions={0}, use_global_device_ids=true | all-gather | bytes 983040 | tf_op jit(solution)/shard_map/all_gather | solution.py:336
  190.4 3.3 multiply_convert_fusion.4
  198.1 9.8 %shard_map.263 = (bf16[512,256]{1,0:T(8,128)(2,1)S(1)}, f32[2,2048,128]{2,1,0:T(8,128)S(1)}) custom-call(bf16[2048,256]{1,0:T(8,128)(2,1)S(1)} %bitcast.347, bf16[256,512]{1,0:T(8,128)(2,1)S(1)} %reshape.634.w_ref, f32[1,256]{1,0:T(1,128)S(1)} %bitcast.352, f32[2048,2]{1,0:T(8,128)S(1)} %copy.92.keep_ref, s32[512,2]{1,0:T(8,128)S(1)} %copy.93.pick_ref), custom_call_target="tpu_custom_call" | custom-call | tf_op jit(solution)/shard_map/pallas_call | solution.py:325
  209.7 12.9 %all_gather.52 = bf16[512,2,384]{0,1,2:T(2,128)(2,1)} all-gather(bf16[512,2,96]{0,1,2:T(2,128)(2,1)S(1)} %copy.127), channel_id=1, replica_groups=mesh['dp'=8,'tensor'=4] {'tensor'}, dimensions={2}, use_global_device_ids=true | all-gather | bytes 983040 | tf_op jit(solution)/shard_map/all_gather | solution.py:337
  222.6 3.7 copy.95
  226.3 2.2 copy.135
  229.8 2.5 fusion.140
  232.4 8.8 %all_gather.50 = bf16[512,768]{1,0:T(8,128)(2,1)S(1)} all-gather(bf16[128,768]{1,0:T(8,128)(2,1)S(1)} %get-tuple-element.193), channel_id=1, replica_groups=mesh['dp'=8,'tensor'=4] {'tensor'}, dimensions={0}, use_global_device_ids=true | all-gather | bytes 983040 | tf_op jit(solution)/shard_map/all_gather | solution.py:336
  244.4 3.3 multiply_convert_fusion.5
  253.0 24.8 %reduce-scatter.19.cloned.1.call-done = bf16[128,1536]{1,0:T(8,128)(2,1)} async-done(((bf16[512,1536]{1,0:T(8,128)(2,1)}), bf16[128,1536]{1,0:T(8,128)(2,1)}) %reduce-scatter.19.cloned.1.call-update) | async-done | bytes 393232 | tf_op jit(solution)/shard_map/reduce_scatter | solution.py:344
  290.2 16.3 %all-gather.11.cloned.1.call-done = bf16[512,1536]{1,0:T(8,128)(2,1)} async-done(((bf16[128,1536]{1,0:T(8,128)(2,1)}), bf16[512,1536]{1,0:T(8,128)(2,1)}) %all-gather.11.cloned.1.call-update) | async-done | bytes 1572880 | tf_op jit(solution)/shard_map/all_gather | solution.py:362
  306.5 2.6 add_convert_fusion.5
  312.4 2.7 fusion.1
  315.1 2.5 slice.384
  317.7 9.9 %all-gather.9.cloned.1.call-done = bf16[512,1536]{1,0:T(8,128)(2,1)} async-done(((bf16[128,1536]{1,0:T(8,128)(2,1)}), bf16[512,1536]{1,0:T(8,128)(2,1)}) %all-gather.9.cloned.1.call-update) | async-done | bytes 1572880 | tf_op jit(solution)/shard_map/all_gather | solution.py:362
  327.6 2.6 add_convert_fusion.6
  337.4 2.9 slice.273
  343.3 2.4 convert_element_type.549
  345.7 2.8 convert_element_type.550
  348.5 3.7 copy.111
  352.2 2.0 add_dynamic-update-slice_fusion.1
  354.1 2.4 convert_element_type.546
  356.5 2.7 convert_element_type.547
  359.2 3.8 copy.108
  363.5 16.4 %reduce-scatter.27.cloned.1.call-done = bf16[128,768]{1,0:T(8,128)(2,1)} async-done(((bf16[512,768]{1,0:T(8,128)(2,1)}), bf16[128,768]{1,0:T(8,128)(2,1)}) %reduce-scatter.27.cloned.1.call-update) | async-done | bytes 196624 | tf_op jit(solution)/shard_map/reduce_scatter | solution.py:376
  379.9 2.4 multiply_reduce_fusion.2
  384.4 11.3 %all_gather.59 = bf16[512,768]{1,0:T(8,128)(2,1)S(1)} all-gather(bf16[128,768]{1,0:T(8,128)(2,1)S(1)} %add_convert_fusion.16), channel_id=1, replica_groups=mesh['dp'=8,'tensor'=4] {'tensor'}, dimensions={0}, use_global_device_ids=true | all-gather | bytes 983040 | tf_op jit(solution)/shard_map/all_gather | solution.py:389
  400.7 8.9 %all_gather.62 = bf16[512,768]{1,0:T(8,128)(2,1)S(1)} all-gather(bf16[128,768]{1,0:T(8,128)(2,1)S(1)} %add_convert_fusion.12), channel_id=1, replica_groups=mesh['dp'=8,'tensor'=4] {'tensor'}, dimensions={0}, use_global_device_ids=true | all-gather | bytes 983040 | tf_op jit(solution)/shard_map/all_gather | solution.py:389
  409.5 3.3 add_convert_fusion.3
  416.8 3.0 fusion.165
  419.8 4.8 fusion.28
  424.6 3.1 all-reduce.22.cloned.1.call-done
  429.5 1.9 copy.132
  432.6 12.6 %shard_map.265 = (bf16[2048,512]{1,0:T(8,128)(2,1)S(1)}, f32[1,256]{1,0:T(1,128)S(1)}) custom-call(bf16[2048,256]{1,0:T(8,128)(2,1)S(1)} %bitcast.348, bf16[256,512]{1,0:T(8,128)(2,1)S(1)} %reshape.634.w_ref, f32[1,256]{1,0:T(1,128)S(1)} %bitcast.353, f32[2048,2]{1,0:T(8,128)S(1)} %copy.92.keep_ref, s32[2,512]{1,0:T(2,128)S(1)} %get-tuple-element.194.pick_ref, ...), custom_call_target="tpu_custom_call" | custom-call | tf_op jit(solution)/shard_map/pallas_call | solution.py:443
  448.6 3.0 fusion.3
  451.7 2.7 convert_element_type.571
  454.3 5.6 fusion
  459.9 5.2 convert_element_type.568
  471.4 12.8 %shard_map.266 = (bf16[2048,512]{1,0:T(8,128)(2,1)S(1)}, f32[1,256]{1,0:T(1,128)S(1)}) custom-call(bf16[2048,256]{1,0:T(8,128)(2,1)S(1)} %bitcast.346, bf16[256,512]{1,0:T(8,128)(2,1)S(1)} %reshape.634.w_ref, f32[1,256]{1,0:T(1,128)S(1)} %bitcast.354, f32[2048,2]{1,0:T(8,128)S(1)} %copy-done.6, s32[2,512]{1,0:T(2,128)S(1)} %get-tuple-element.196.pick_ref, ...), custom_call_target="tpu_custom_call" | custom-call | tf_op jit(solution)/shard_map/pallas_call | solution.py:443
  488.3 2.1 fusion.164
  492.6 2.2 multiply_reduce_fusion.5
  495.6 12.0 %all_gather.63 = bf16[512,768]{1,0:T(8,128)(2,1)S(1)} all-gather(bf16[128,768]{1,0:T(8,128)(2,1)S(1)} %add_convert_fusion.11), channel_id=1, replica_groups=mesh['dp'=8,'tensor'=4] {'tensor'}, dimensions={0}, use_global_device_ids=true | all-gather | bytes 983040 | tf_op jit(solution)/shard_map/all_gather | solution.py:403
  513.2 8.9 %all_gather.60 = bf16[512,768]{1,0:T(8,128)(2,1)S(1)} all-gather(bf16[128,768]{1,0:T(8,128)(2,1)S(1)} %add_convert_fusion.15), channel_id=1, replica_groups=mesh['dp'=8,'tensor'=4] {'tensor'}, dimensions={0}, use_global_device_ids=true | all-gather | bytes 983040 | tf_op jit(solution)/shard_map/all_gather | solution.py:403
  524.3 3.2 multiply_reduce_fusion.1
  534.7 2.3 fusion.163
  548.2 21.1 %psum.75 = bf16[2,96]{1,0:T(2,128)(2,1)S(1)} all-reduce(bf16[2,96]{1,0:T(2,128)(2,1)S(1)} %add_convert_fusion.19), channel_id=1, replica_groups=mesh['dp'=8,'tensor'=4] {'dp'}, use_global_device_ids=true, to_apply=%region_77.78 | all-reduce | flops 192 | bytes 768 | tf_op jit(solution)/shard_map/psum | solution.py:229
  572.6 2.1 maximum_convert_fusion
  574.9 38.0 %all-reduce.14 = (f32[4,768]{1,0:T(4,128)}, f32[4,768]{1,0:T(4,128)}) all-reduce(f32[4,768]{1,0:T(4,128)S(1)} %maximum_add_fusion, f32[4,768]{1,0:T(4,128)S(1)} %maximum_add_fusion.1), channel_id=1, replica_groups=mesh['dp'=8,'tensor'=4] {'dp','tensor'}, use_global_device_ids=true, to_apply=%region_88.89 | all-reduce | flops 6144 | bytes 49152 | tf_op jit(solution)/shard_map/psum | solution.py:486
  615.9 209.0 %all-reduce.20.cloned.1.call-done = (bf16[3,1536,192]{1,0,2:T(4,128)(2,1)}, bf16[768,3,192]{0,2,1:T(8,128)(2,1)}, bf16[192,768]{1,0:T(8,128)(2,1)}, bf16[768,768...) async-done(((bf16[3,1536,192]{1,0,2:T(4,128)(2,1)}, bf16[768,3,192]{0,2,1:T(8,128)(2,1)}, ...) | async-done | bytes 6094864 | tf_op jit(solution)/shard_map/psum | solution.py:229
  828.5 4.1 copy.116
  (651 shorter events, 150.3 us)
Async XLA Ops:
  7.2 80.7 %copy-start = (bf16[768,768]{1,0:T(8,128)(2,1)S(1)}, bf16[768,768]{1,0:T(8,128)(2,1)}, u32[]{:S(2)}) copy-start(bf16[768,768]{1,0:T(8,128)(2,1)} %param.22) | copy-start | bytes 3538948
  7.2 12.6 %copy-start.69 = (bf16[768,3,192]{0,2,1:T(8,128)(2,1)S(1)}, bf16[768,3,192]{0,2,1:T(8,128)(2,1)}, u32[]{:S(2)}) copy-start(bf16[768,3,192]{0,2,1:T(8,128)(2,1)} %param.20) | copy-start | bytes 2654212
  7.2 43.3 %reduce-scatter.15.cloned.1.call-start = ((), (), s32[]{:S(2)}) async-start(), calls=%async_computation.14 | async-start | bytes 983040 | tf_op jit(solution)/shard_map/reduce_scatter | solution.py:304
  8.5 13.8 %copy-start.43 = (pred[512,512]{0,1:T(8,128)(4,1)}, pred[512,512]{0,1:T(8,128)(4,1)S(1)}, u32[]{:S(2)}) copy-start(pred[512,512]{0,1:T(8,128)(4,1)S(1)} %broadcast_compare_fusion.1) | copy-start | bytes 786436
  26.3 50.9 %reduce-scatter.21.cloned.1.call-start = ((), (), s32[]{:S(2)}) async-start(), calls=%async_computation.17 | async-start | bytes 983040 | tf_op jit(solution)/shard_map/reduce_scatter | solution.py:304
  39.8 38.6 %copy-start.106 = (bf16[3,64,512]{2,1,0:T(8,128)(2,1)}, bf16[3,64,512]{2,1,0:T(8,128)(2,1)S(1)}, u32[]{:S(2)}) copy-start(bf16[3,64,512]{2,1,0:T(8,128)(2,1)S(1)} %convolution_convert_fusion.18) | copy-start | bytes 589828
  41.1 77.7 %reduce-scatter.17.cloned.1.call-start = ((), (), s32[]{:S(2)}) async-start(), calls=%async_computation.15 | async-start | bytes 983040 | tf_op jit(solution)/shard_map/reduce_scatter | solution.py:315
  41.2 131.1 %copy-start.125 = (f32[768]{0:T(1024)}, f32[768]{0:T(1024)S(1)}, u32[]{:S(2)}) copy-start(f32[768]{0:T(1024)S(1)} %get-tuple-element.107) | copy-start | bytes 9220
  51.6 67.2 %copy-start.142 = (f32[128]{0:T(128)}, f32[128]{0:T(128)S(1)}, u32[]{:S(2)}) copy-start(f32[128]{0:T(128)S(1)} %broadcast_multiply_fusion.7) | copy-start | bytes 1540
  78.4 14.9 %copy-start.177 = (f32[128]{0:T(128)}, f32[128]{0:T(128)S(1)}, u32[]{:S(2)}) copy-start(f32[128]{0:T(128)S(1)} %get-tuple-element.103) | copy-start | bytes 1540
  78.4 94.0 %copy-start.140 = (f32[128]{0:T(128)}, f32[128]{0:T(128)S(1)}, u32[]{:S(2)}) copy-start(f32[128]{0:T(128)S(1)} %broadcast_multiply_fusion.4) | copy-start | bytes 1540
  78.4 40.4 %copy-start.150 = (f32[128]{0:T(128)}, f32[128]{0:T(128)S(1)}, u32[]{:S(2)}) copy-start(f32[128]{0:T(128)S(1)} %fusion.99) | copy-start | bytes 1540
  79.6 17.4 %copy-start.166 = (f32[128]{0:T(128)}, f32[128]{0:T(128)S(1)}, u32[]{:S(2)}) copy-start(f32[128]{0:T(128)S(1)} %get-tuple-element.190) | copy-start | bytes 1540
  94.9 23.9 %copy-start.38 = (bf16[128,768]{1,0:T(8,128)(2,1)S(1)}, bf16[128,768]{1,0:T(8,128)(2,1)}, u32[]{:S(2)}) copy-start(bf16[128,768]{1,0:T(8,128)(2,1)} %reduce-scatter.15.cloned.1.call-done) | copy-start | bytes 589828
  94.9 23.9 %copy-start.40 = (bf16[128,768]{1,0:T(8,128)(2,1)S(1)}, bf16[128,768]{1,0:T(8,128)(2,1)}, u32[]{:S(2)}) copy-start(bf16[128,768]{1,0:T(8,128)(2,1)} %reduce-scatter.21.cloned.1.call-done) | copy-start | bytes 589828
  95.0 48.9 %all-gather.15.cloned.1.call-start = ((), (), s32[]{:S(2)}) async-start(), calls=%async_computation.31 | async-start | bytes 1310720 | tf_op jit(solution)/shard_map/all_gather | solution.py:283
  97.0 75.4 %reduce-scatter.23.cloned.1.call-start = ((), (), s32[]{:S(2)}) async-start(), calls=%async_computation.18 | async-start | bytes 983040 | tf_op jit(solution)/shard_map/reduce_scatter | solution.py:315
  97.1 75.3 %copy-start.152 = (f32[128]{0:T(128)}, f32[128]{0:T(128)S(1)}, u32[]{:S(2)}) copy-start(f32[128]{0:T(128)S(1)} %fusion.102) | copy-start | bytes 1540
  136.4 60.5 %all-gather.13.cloned.1.call-start = ((), (), s32[]{:S(2)}) async-start(), calls=%async_computation.30 | async-start | bytes 1310720 | tf_op jit(solution)/shard_map/all_gather | solution.py:283
  137.0 91.7 %reduce-scatter.25.cloned.1.call-start = ((), (), s32[]{:S(2)}) async-start(), calls=%async_computation.19 | async-start | bytes 1966080 | tf_op jit(solution)/shard_map/reduce_scatter | solution.py:344
  173.6 13.1 %copy-start.21 = (f32[128,768]{1,0:T(8,128)}, f32[128,768]{1,0:T(8,128)S(1)}, u32[]{:S(2)}) copy-start(f32[128,768]{1,0:T(8,128)S(1)} %get-tuple-element.161) | copy-start | bytes 1179652
  173.8 12.9 %copy-start.168 = (f32[128]{0:T(128)}, f32[128]{0:T(128)S(1)}, u32[]{:S(2)}) copy-start(f32[128]{0:T(128)S(1)} %multiply_reduce_fusion.17) | copy-start | bytes 1540
  173.8 12.9 %copy-start.154 = (f32[128]{0:T(128)}, f32[128]{0:T(128)S(1)}, u32[]{:S(2)}) copy-start(f32[128]{0:T(128)S(1)} %fusion.103) | copy-start | bytes 1540
  173.8 12.9 %copy-start.61 = (bf16[64,8,2,384]{3,1,2,0:T(8,128)(2,1)S(1)}, bf16[64,8,2,384]{3,1,2,0:T(8,128)(2,1)}, u32[]{:S(2)}) copy-start(bf16[64,8,2,384]{3,1,2,0:T(8,128)(2,1)} %copy.137) | copy-start | bytes 2359300
  195.4 82.4 %reduce-scatter.19.cloned.1.call-start = ((), (), s32[]{:S(2)}) async-start(), calls=%async_computation.16 | async-start | bytes 1966080 | tf_op jit(solution)/shard_map/reduce_scatter | solution.py:344
  249.5 57.1 %all-gather.11.cloned.1.call-start = ((), (), s32[]{:S(2)}) async-start(), calls=%async_computation.24 | async-start | bytes 1966080 | tf_op jit(solution)/shard_map/all_gather | solution.py:362
  250.7 29.6 %copy-start.172 = (f32[128]{0:T(128)}, f32[128]{0:T(128)S(1)}, u32[]{:S(2)}) copy-start(f32[128]{0:T(128)S(1)} %multiply_reduce_fusion.16) | copy-start | bytes 1540
  286.7 40.9 %all-gather.9.cloned.1.call-start = ((), (), s32[]{:S(2)}) async-start(), calls=%async_computation.20 | async-start | bytes 1966080 | tf_op jit(solution)/shard_map/all_gather | solution.py:362
  290.0 73.5 %reduce-scatter.33.cloned.1.call-start = ((), (), s32[]{:S(2)}) async-start(), calls=%async_computation.25 | async-start | bytes 983040 | tf_op jit(solution)/shard_map/reduce_scatter | solution.py:376
  317.7 62.2 %reduce-scatter.27.cloned.1.call-start = ((), (), s32[]{:S(2)}) async-start(), calls=%async_computation.21 | async-start | bytes 983040 | tf_op jit(solution)/shard_map/reduce_scatter | solution.py:376
  337.3 90.4 %all-reduce.22.cloned.1.call-start = ((), (), s32[]{:S(2)}) async-start(), calls=%async_computation.33 | async-start | bytes 3145728
  363.0 19.3 %copy-start.171 = (f32[128]{0:T(128)S(1)}, f32[128]{0:T(128)}, u32[]{:S(2)}) copy-start(f32[128]{0:T(128)} %copy-done.170) | copy-start | bytes 1540
  363.0 19.3 %copy-start.169 = (f32[128]{0:T(128)S(1)}, f32[128]{0:T(128)}, u32[]{:S(2)}) copy-start(f32[128]{0:T(128)} %copy-done.168) | copy-start | bytes 1540
  363.0 129.4 %reduce-scatter.29.cloned.1.call-start = ((), (), s32[]{:S(2)}) async-start(), calls=%async_computation.22 | async-start | bytes 983040 | tf_op jit(solution)/shard_map/reduce_scatter | solution.py:395
  382.4 14.3 %copy-start.182 = (bf16[768,768]{1,0:T(8,128)(2,1)S(1)}, bf16[768,768]{1,0:T(8,128)(2,1)}, u32[]{:S(2)}) copy-start(bf16[768,768]{1,0:T(8,128)(2,1)} %param.23) | copy-start | bytes 3538948
  382.4 14.3 %copy-start.185 = (f32[512,768]{1,0:T(8,128)S(1)}, f32[512,768]{1,0:T(8,128)}, u32[]{:S(2)}) copy-start(f32[512,768]{1,0:T(8,128)} %get-tuple-element.155) | copy-start | bytes 4718596
  382.4 14.2 %copy-start.186 = (f32[512,768]{1,0:T(8,128)S(1)}, f32[512,768]{1,0:T(8,128)}, u32[]{:S(2)}) copy-start(f32[512,768]{1,0:T(8,128)} %get-tuple-element.237) | copy-start | bytes 4718596
  383.5 14.3 %copy-start.156 = (f32[128]{0:T(128)}, f32[128]{0:T(128)S(1)}, u32[]{:S(2)}) copy-start(f32[128]{0:T(128)S(1)} %negate_multiply_fusion.9) | copy-start | bytes 1540
  400.5 92.0 %reduce-scatter.35.cloned.1.call-start = ((), (), s32[]{:S(2)}) async-start(), calls=%async_computation.26 | async-start | bytes 983040 | tf_op jit(solution)/shard_map/reduce_scatter | solution.py:395
  400.5 12.3 %copy-start.158 = (f32[128]{0:T(128)}, f32[128]{0:T(128)S(1)}, u32[]{:S(2)}) copy-start(f32[128]{0:T(128)S(1)} %negate_multiply_fusion.5) | copy-start | bytes 1540
  415.5 157.1 %reduce-scatter.39.cloned.1.call-start = ((), (), s32[]{:S(2)}) async-start(), calls=%async_computation.28 | async-start | bytes 1310720 | tf_op jit(solution)/shard_map/reduce_scatter | solution.py:463
  448.4 124.2 %reduce-scatter.41.cloned.1.call-start = ((), (), s32[]{:S(2)}) async-start(), calls=%async_computation.29 | async-start | bytes 1310720 | tf_op jit(solution)/shard_map/reduce_scatter | solution.py:463
  471.4 12.9 %copy-start.8 = (bf16[2048,512]{1,0:T(8,128)(2,1)S(1)}, bf16[2048,512]{1,0:T(8,128)(2,1)}, u32[]{:S(2)}) copy-start(bf16[2048,512]{1,0:T(8,128)(2,1)} %copy-done.7) | copy-start | bytes 6291460
  488.2 124.6 %reduce-scatter.37.cloned.1.call-start = ((), (), s32[]{:S(2)}) async-start(), calls=%async_computation.27 | async-start | bytes 983040 | tf_op jit(solution)/shard_map/reduce_scatter | solution.py:460
  494.8 12.7 %copy-start.60 = (bf16[192,768]{1,0:T(8,128)(2,1)S(1)}, bf16[192,768]{1,0:T(8,128)(2,1)}, u32[]{:S(2)}) copy-start(bf16[192,768]{1,0:T(8,128)(2,1)} %param.21) | copy-start | bytes 884740
  494.9 13.1 %copy-start.14 = (f32[3,512,512]{1,2,0:T(8,128)S(1)}, f32[3,512,512]{1,2,0:T(8,128)}, u32[]{:S(2)}) copy-start(f32[3,512,512]{1,2,0:T(8,128)} %copy-done.13) | copy-start | bytes 9437188
  495.4 12.6 %copy-start.67 = (f32[128,768]{1,0:T(8,128)}, f32[128,768]{1,0:T(8,128)S(1)}, u32[]{:S(2)}) copy-start(f32[128,768]{1,0:T(8,128)S(1)} %get-tuple-element.188) | copy-start | bytes 1179652
  495.4 17.7 %copy-start.65 = (f32[128,768]{1,0:T(8,128)}, f32[128,768]{1,0:T(8,128)S(1)}, u32[]{:S(2)}) copy-start(f32[128,768]{1,0:T(8,128)S(1)} %get-tuple-element.129) | copy-start | bytes 1179652
  495.4 12.6 %copy-start.46 = (pred[512,512]{0,1:T(8,128)(4,1)S(1)}, pred[512,512]{0,1:T(8,128)(4,1)}, u32[]{:S(2)}) copy-start(pred[512,512]{0,1:T(8,128)(4,1)} %copy-done.45) | copy-start | bytes 786436
  495.4 12.6 %copy-start.91 = (bf16[512,3,3,64]{0,3,2,1:T(8,128)(2,1)S(1)}, bf16[512,3,3,64]{0,3,2,1:T(8,128)(2,1)}, u32[]{:S(2)}) copy-start(bf16[512,3,3,64]{0,3,2,1:T(8,128)(2,1)} %copy-done.90) | copy-start | bytes 1769476
  495.4 12.6 %copy-start.130 = (f32[3,512]{1,0:T(4,128)S(1)}, f32[3,512]{1,0:T(4,128)}, u32[]{:S(2)}) copy-start(f32[3,512]{1,0:T(4,128)} %copy-done.129) | copy-start | bytes 18436
  495.5 12.5 %copy-start.160 = (f32[128]{0:T(128)}, f32[128]{0:T(128)S(1)}, u32[]{:S(2)}) copy-start(f32[128]{0:T(128)S(1)} %negate_multiply_fusion.4) | copy-start | bytes 1540
  524.2 89.7 %reduce-scatter.31.cloned.1.call-start = ((), (), s32[]{:S(2)}) async-start(), calls=%async_computation.23 | async-start | bytes 983040 | tf_op jit(solution)/shard_map/reduce_scatter | solution.py:460
  534.4 290.6 %all-reduce.20.cloned.1.call-start = ((), (), s32[]{:S(2)}) async-start(), calls=%async_computation.32 | async-start | bytes 13369344 | tf_op jit(solution)/shard_map/psum | solution.py:229
  546.5 28.2 %copy-start.138 = (f32[768]{0:T(1024)S(1)}, f32[768]{0:T(1024)}, u32[]{:S(2)}) copy-start(f32[768]{0:T(1024)} %get-tuple-element.74) | copy-start | bytes 9220
  546.5 28.2 %copy-start.137 = (f32[768]{0:T(1024)S(1)}, f32[768]{0:T(1024)}, u32[]{:S(2)}) copy-start(f32[768]{0:T(1024)} %get-tuple-element.98) | copy-start | bytes 9220
  546.5 28.2 %copy-start.136 = (f32[768]{0:T(1024)S(1)}, f32[768]{0:T(1024)}, u32[]{:S(2)}) copy-start(f32[768]{0:T(1024)} %get-tuple-element.100) | copy-start | bytes 9220
  546.5 28.2 %copy-start.135 = (f32[768]{0:T(1024)S(1)}, f32[768]{0:T(1024)}, u32[]{:S(2)}) copy-start(f32[768]{0:T(1024)} %get-tuple-element.102) | copy-start | bytes 9220
  546.5 28.2 %copy-start.146 = (f32[1,768]{1,0:T(1,128)S(1)}, f32[1,768]{1,0:T(1,128)}, u32[]{:S(2)}) copy-start(f32[1,768]{1,0:T(1,128)} %reshape.666) | copy-start | bytes 9220
  546.6 28.2 %copy-start.147 = (f32[1,768]{1,0:T(1,128)S(1)}, f32[1,768]{1,0:T(1,128)}, u32[]{:S(2)}) copy-start(f32[1,768]{1,0:T(1,128)} %reshape.662) | copy-start | bytes 9220
  546.6 66.3 %copy-start.68 = (f32[128,768]{1,0:T(8,128)S(1)}, f32[128,768]{1,0:T(8,128)}, u32[]{:S(2)}) copy-start(f32[128,768]{1,0:T(8,128)} %copy-done.67) | copy-start | bytes 1179652
  546.6 66.3 %copy-start.161 = (f32[128]{0:T(128)S(1)}, f32[128]{0:T(128)}, u32[]{:S(2)}) copy-start(f32[128]{0:T(128)} %copy-done.160) | copy-start | bytes 1540
  547.4 66.6 %copy-start.66 = (f32[128,768]{1,0:T(8,128)S(1)}, f32[128,768]{1,0:T(8,128)}, u32[]{:S(2)}) copy-start(f32[128,768]{1,0:T(8,128)} %copy-done.65) | copy-start | bytes 1179652
  547.4 66.6 %copy-start.163 = (f32[128]{0:T(128)S(1)}, f32[128]{0:T(128)}, u32[]{:S(2)}) copy-start(f32[128]{0:T(128)} %copy-done.162) | copy-start | bytes 1540
  (143 other events, 360.0 us)
Sparse Core Ops, SparseCore 0:
  26.4 24.1 reduce-scatter.14
  53.8 23.2 reduce-scatter.20
  95.1 23.6 reduce-scatter.16
  120.9 16.7 all-gather.14
  140.7 26.3 reduce-scatter.22
  169.1 19.8 all-gather.12
  195.5 31.3 reduce-scatter.24
  249.6 28.2 reduce-scatter.18
  286.9 19.6 all-gather.10
  307.9 19.6 all-gather.8
  330.7 23.2 reduce-scatter.32
  356.6 23.2 reduce-scatter.26
  382.3 45.4 all-reduce.21
  430.7 23.2 reduce-scatter.28
  456.6 23.2 reduce-scatter.34
  482.3 27.1 reduce-scatter.38
  512.6 25.4 reduce-scatter.40
  541.1 23.2 reduce-scatter.36
  567.7 23.4 reduce-scatter.30
  597.5 227.4 all-reduce.19

commit v2 on v1

v2 whole, which is shorter than its diff:
```python
import functools

import jax
import jax.numpy as jnp
from jax import lax
from jax.experimental import pallas as pl
from jax.experimental.pallas import tpu as pltpu
from jax.sharding import PartitionSpec as P

HD = 64


NORM_EPSILON = 1e-06
MASK_VALUE = -1e30
HIGH_PRECISION = lax.Precision.HIGHEST


def layer_norm(row_values, gain_row, shift_row):
    average = jnp.mean(row_values, axis=-1, keepdims=True)
    centered = row_values - average
    spread = jnp.mean(centered * centered, axis=-1, keepdims=True)
    return centered * lax.rsqrt(spread + NORM_EPSILON) * gain_row + shift_row


def gelu_exact(values):
    return jax.nn.gelu(values, approximate=False)


def layout(doc_sizes, char_counts, char_total):
    length = char_counts.shape[0]
    docs = doc_sizes.shape[0]
    doc_ids = jnp.arange(docs, dtype=jnp.int32)
    doc_ends = jnp.sum(
        jnp.where(doc_ids[None, :] <= doc_ids[:, None], doc_sizes[None, :], 0), axis=1
    )
    positions = jnp.arange(length, dtype=jnp.int32)
    segment = jnp.sum(
        (positions[:, None] >= doc_ends[None, :]).astype(jnp.int32), axis=1, dtype=jnp.int32
    )
    token_ends = jnp.sum(
        jnp.where(positions[None, :] <= positions[:, None], char_counts[None, :], 0), axis=1
    )
    last_char = token_ends - 1
    first_char = token_ends - char_counts
    char_ends = jnp.sum(
        jnp.where(positions[None, :] < doc_ends[:, None], char_counts[None, :], 0), axis=1
    )
    char_positions = jnp.arange(char_total, dtype=jnp.int32)
    starts = char_ends - jnp.sum(
        jnp.where(
            (positions[None, :] < doc_ends[:, None])
            & (positions[None, :] >= (doc_ends - doc_sizes)[:, None]),
            char_counts[None, :],
            0,
        ),
        axis=1,
    )
    keep_forward = 1.0 - jnp.any(char_positions[:, None] == starts[None, :], axis=1).astype(
        jnp.float32
    )
    keep_backward = 1.0 - jnp.any(
        char_positions[:, None] == (char_ends - 1)[None, :], axis=1
    ).astype(jnp.float32)
    token_starts = doc_ends - doc_sizes
    prev_ok = 1.0 - jnp.any(positions[:, None] == token_starts[None, :], axis=1).astype(
        jnp.float32
    )
    next_ok = 1.0 - jnp.any(positions[:, None] == (doc_ends - 1)[None, :], axis=1).astype(
        jnp.float32
    )
    return (segment, first_char, last_char, keep_forward, keep_backward, prev_ok, next_ok)


F32 = jnp.float32
BF16 = jnp.bfloat16
LANE = 128
CHUNKS = 32
MIB = 1024 * 1024
VMEM = pl.BlockSpec(memory_space=pltpu.VMEM)


def recur(first, second, decays, drives, outs, steps):
    ups = (first, second)

    def at(ref, tile, step):
        row = step if ups[tile] else steps - 1 - step
        return ref[tile, pl.ds(row, CHUNKS, stride=steps), :]

    def put(ref, tile, step, value):
        row = step if ups[tile] else steps - 1 - step
        ref[tile, pl.ds(row, CHUNKS, stride=steps), :] = value

    zero = jnp.zeros((CHUNKS, LANE), jnp.float32)
    one = jnp.ones((CHUNKS, LANE), jnp.float32)

    def summary(step, carry):
        new = []
        for tile in range(2):
            state, mult = carry[2 * tile], carry[2 * tile + 1]
            decay = at(decays, tile, step)
            new += [decay * state + at(drives, tile, step), decay * mult]
        return tuple(new)

    ends = lax.fori_loop(0, steps, summary, (zero, one, zero, one), unroll=4)
    starts = []
    for tile in range(2):
        final, mult = ends[2 * tile], ends[2 * tile + 1]
        order = range(CHUNKS) if ups[tile] else range(CHUNKS - 1, -1, -1)
        carry = jnp.zeros((1, LANE), jnp.float32)
        rows = [None] * CHUNKS
        for chunk in order:
            rows[chunk] = carry
            carry = mult[chunk : chunk + 1] * carry + final[chunk : chunk + 1]
        starts.append(jnp.concatenate(rows, axis=0))

    def write(step, carry):
        new = []
        for tile in range(2):
            state = at(decays, tile, step) * carry[tile] + at(drives, tile, step)
            put(outs, tile, step, state)
            new.append(state)
        return tuple(new)

    lax.fori_loop(0, steps, write, tuple(starts), unroll=4)


def gates_of(chars, w_ref, bias_ref, keep_ref, gate_ref, cand_ref, decay_ref, drive_ref):
    proj = jnp.dot(chars, w_ref[...], preferred_element_type=jnp.float32)
    for tile in range(2):
        cols = pl.ds(tile * LANE, LANE)
        logits = proj[:, tile * LANE : (tile + 1) * LANE] + bias_ref[:, cols]
        gate = jax.nn.sigmoid(logits)
        cand = proj[:, (2 + tile) * LANE : (3 + tile) * LANE]
        gate_ref[tile] = gate
        cand_ref[tile] = cand
        decay_ref[tile] = (1.0 - gate) * keep_ref[:, tile : tile + 1]
        drive_ref[tile] = gate * cand


def gru_bwd_kernel(chars_ref, w_ref, bias_ref, keep_ref, pick_ref, state_ref, grad_ref,
                   proj_grad_ref, bias_grad_ref, gate_ref, cand_ref, decay_ref, drive_ref, flow_ref):
    total = chars_ref.shape[0]
    steps = total // CHUNKS
    gates_of(chars_ref[...], w_ref, bias_ref, keep_ref, gate_ref, cand_ref, decay_ref, drive_ref)
    length = pick_ref.shape[1]
    ids = lax.broadcasted_iota(jnp.int32, (total, length), 0)
    for tile in range(2):
        hot = (ids == pick_ref[tile : tile + 1, :]).astype(jnp.bfloat16)
        cols = pl.ds(tile * LANE, LANE)
        drive_ref[tile] = jnp.dot(hot, grad_ref[:, cols], preferred_element_type=jnp.float32)
    flow_ref[0, pl.ds(0, total - 1), :] = decay_ref[0, pl.ds(1, total - 1), :]
    flow_ref[0, pl.ds(total - 1, 1), :] = jnp.zeros((1, LANE), jnp.float32)
    flow_ref[1, pl.ds(1, total - 1), :] = decay_ref[1, pl.ds(0, total - 1), :]
    flow_ref[1, pl.ds(0, 1), :] = jnp.zeros((1, LANE), jnp.float32)
    recur(False, True, flow_ref, drive_ref, decay_ref, steps)
    for tile in range(2):
        flow = decay_ref[tile] * gate_ref[tile]
        logit_grad = flow * (cand_ref[tile] - state_ref[tile])
        proj_grad_ref[:, pl.ds(tile * LANE, LANE)] = logit_grad.astype(jnp.bfloat16)
        proj_grad_ref[:, pl.ds((2 + tile) * LANE, LANE)] = flow.astype(jnp.bfloat16)
        bias_grad_ref[:, pl.ds(tile * LANE, LANE)] = jnp.sum(logit_grad, axis=0, keepdims=True)


def gru_call(kernel, outs, scratch_count, total):
    return pl.pallas_call(
        kernel,
        out_shape=outs,
        scratch_shapes=[pltpu.VMEM((2, total, LANE), jnp.float32)] * scratch_count,
        compiler_params=pltpu.CompilerParams(vmem_limit_bytes=48 * 1024 * 1024),
    )


def gru_weights(w_gru, gate_bias):
    width, _, _, units = w_gru.shape
    matrix = jnp.pad(jnp.swapaxes(w_gru, 1, 2), ((0, 0), (0, 0), (0, 0), (0, LANE - units)))
    bias = jnp.pad(gate_bias, ((0, 0), (0, LANE - units)))
    return matrix.reshape(width, 4 * LANE), bias.reshape(1, 2 * LANE)


def conv_inputs(joined, prev_ok, next_ok):
    zero_row = jnp.zeros((1, joined.shape[1]), joined.dtype)
    preceding = jnp.concatenate([zero_row, joined[:-1]], axis=0) * prev_ok[:, None].astype(
        joined.dtype
    )
    following = jnp.concatenate([joined[1:], zero_row], axis=0) * next_ok[:, None].astype(
        joined.dtype
    )
    return jnp.concatenate([preceding, joined, following], axis=1)


def conv_back(grad_stacked, prev_ok, next_ok):
    column_count = grad_stacked.shape[1] // 3
    from_prev = grad_stacked[:, :column_count] * prev_ok[:, None]
    from_next = grad_stacked[:, 2 * column_count :] * next_ok[:, None]
    zero_row = jnp.zeros((1, column_count), jnp.float32)
    middle = grad_stacked[:, column_count : 2 * column_count]
    return (
        middle
        + jnp.concatenate([from_prev[1:], zero_row], axis=0)
        + jnp.concatenate([zero_row, from_next[:-1]], axis=0)
    )


def inner_rows(left_rows, right_rows):
    return lax.dot_general(
        left_rows, right_rows, (((0,), (0,)), ((), ())), preferred_element_type=jnp.float32
    )


def times_transposed(left_rows, right_matrix):
    return lax.dot_general(
        left_rows, right_matrix, (((1,), (1,)), ((), ())), preferred_element_type=jnp.float32
    )


def nn(left, right):
    return jnp.dot(left, right, preferred_element_type=F32)


def nt(left, right):
    return lax.dot_general(left, right, (((1,), (1,)), ((), ())), preferred_element_type=F32)


def tn(left, right):
    return lax.dot_general(left, right, (((0,), (0,)), ((), ())), preferred_element_type=F32)


def gelu_pair(values):
    cdf = 0.5 * (1.0 + lax.erf(values * 0.7071067811865476))
    density = 0.3989422804014327 * jnp.exp(-0.5 * values * values)
    return values * cdf, cdf + values * density


def normalize(rows):
    centered = rows - jnp.mean(rows, axis=-1, keepdims=True)
    scale = lax.rsqrt(jnp.mean(centered * centered, axis=-1, keepdims=True) + NORM_EPSILON)
    return centered * scale, scale


def normalize_back(unit, scale, grad_unit):
    return scale * (
        grad_unit
        - jnp.mean(grad_unit, axis=-1, keepdims=True)
        - unit * jnp.mean(grad_unit * unit, axis=-1, keepdims=True)
    )


class Group:
    def __init__(self, send, recv, seqs):
        self.me = lax.axis_index("tensor")
        self.low = self.me % 2
        self.high = self.me // 2
        self.pair = self.high * 2 + (1 - self.low)
        self.far = (1 - self.high) * 2 + self.low
        self.send, self.recv, self.seqs, self.used = send, recv, seqs, 0

    def block(self, turn):
        left = 3 - turn
        return ((self.high + left // 2) % 2) * 2 + (self.low + left % 2) % 2

    def slots(self, count):
        first = self.used
        self.used += count
        return [first + i for i in range(count)]

    def copy(self, slot, seq, source, target, peer):
        index = slot * self.seqs + seq
        return pltpu.make_async_remote_copy(
            src_ref=source,
            dst_ref=target,
            send_sem=self.send.at[index],
            recv_sem=self.recv.at[index],
            device_id={"tensor": peer},
            device_id_type=pl.DeviceIdType.MESH,
        )

    def greet(self):
        barrier = pltpu.get_barrier_semaphore()
        for peer in (self.pair, self.far):
            pl.semaphore_signal(
                barrier, inc=1, device_id={"tensor": peer}, device_id_type=pl.DeviceIdType.MESH
            )
        pl.semaphore_wait(barrier, 2)


class Gather:
    def __init__(self, group, buf, source=None):
        self.group, self.buf, self.source = group, buf, source
        self.near, self.over, self.fwd = group.slots(3)

    def own(self, seq):
        return self.buf.at[seq, self.group.me] if self.source is None else self.source.at[seq]

    def near_copy(self, seq):
        g = self.group
        return g.copy(self.near, seq, self.own(seq), self.buf.at[seq, g.me], g.pair)

    def over_copy(self, seq):
        g = self.group
        return g.copy(self.over, seq, self.own(seq), self.buf.at[seq, g.me], g.far)

    def fwd_copy(self, seq):
        g = self.group
        other = self.buf.at[seq, g.far]
        return g.copy(self.fwd, seq, other, other, g.pair)

    def start(self, seq):
        self.over_copy(seq).start()
        self.near_copy(seq).start()

    def forward(self, seq):
        self.over_copy(seq).wait_recv()
        self.fwd_copy(seq).start()

    def finish(self, seq):
        near = self.near_copy(seq)
        fwd = self.fwd_copy(seq)
        near.wait_recv()
        fwd.wait_recv()
        near.wait_send()
        self.over_copy(seq).wait_send()
        fwd.wait_send()


class Scatter:
    def __init__(self, group, stage, got, own, temp):
        self.group, self.stage, self.got, self.held, self.temp = group, stage, got, own, temp
        self.names = group.slots(3)

    def copies(self, seq):
        g = self.group
        peers = (g.pair, g.pair, g.far)
        return [
            g.copy(self.names[i], seq, self.stage(seq, i), self.got(seq, i), peers[i])
            for i in range(3)
        ]

    def start(self, seq, part):
        mine, other, over = self.copies(seq)

        def turn(step, carry):
            self.temp[...] = part(self.group.block(step))

            @pl.when(step == 0)
            def _():
                self.stage(seq, 1)[...] = self.temp[...].astype(BF16)
                other.start()

            @pl.when(step == 1)
            def _():
                other.wait_recv()
                self.stage(seq, 2)[...] = (self.temp[...] + self.got(seq, 1)[...]).astype(BF16)
                over.start()

            @pl.when(step == 2)
            def _():
                self.stage(seq, 0)[...] = self.temp[...].astype(BF16)
                mine.start()

            @pl.when(step == 3)
            def _():
                self.held(seq)[...] = self.temp[...]

            return carry

        lax.fori_loop(0, 4, turn, 0)

    def finish(self, seq):
        mine, other, over = self.copies(seq)
        mine.wait_recv()
        over.wait_recv()
        total = self.held(seq)[...] + self.got(seq, 0)[...] + self.got(seq, 2)[...]
        mine.wait_send()
        other.wait_send()
        over.wait_send()
        return total


def recur_plain(ups, decays, drives, outs, steps):
    def rows(tile, step):
        row = step if ups[tile] else steps - 1 - step
        return pl.ds(row, CHUNKS, stride=steps)

    zero = jnp.zeros((CHUNKS, LANE), F32)
    one = jnp.ones((CHUNKS, LANE), F32)

    def summary(step, carry):
        new = []
        for tile in range(2):
            state, mult = carry[2 * tile], carry[2 * tile + 1]
            decay = decays[tile, rows(tile, step), :]
            new += [decay * state + drives[tile, rows(tile, step), :], decay * mult]
        return tuple(new)

    ends = lax.fori_loop(0, steps, summary, (zero, one, zero, one), unroll=4)
    starts = []
    for tile in range(2):
        final, mult = ends[2 * tile], ends[2 * tile + 1]
        order = range(CHUNKS) if ups[tile] else range(CHUNKS - 1, -1, -1)
        carry = jnp.zeros((1, LANE), F32)
        heads = [None] * CHUNKS
        for chunk in order:
            heads[chunk] = carry
            carry = mult[chunk : chunk + 1] * carry + final[chunk : chunk + 1]
        starts.append(jnp.concatenate(heads, axis=0))

    def write(step, carry):
        new = []
        for tile in range(2):
            here = rows(tile, step)
            state = decays[tile, here, :] * carry[tile] + drives[tile, here, :]
            outs[tile, here, :] = state
            new.append(state)
        return tuple(new)

    lax.fori_loop(0, steps, write, tuple(starts), unroll=4)


def forward_kernel(
    units, tokens, chars, wq, wout, win, wdown, wg, gate_bias, wc, wm, gain, bias, cot_t, cot_c,
    segc, segr, pickc, keep, edges,
    token_out, char_out, o_x, o_c, o_qkv, o_p, o_ctx, o_h, o_act, o_dact, o_mid, o_st, o_mg,
    o_dmg, o_states, o_unit0, o_unit1, o_scale, o_res3, o_branch, norm_grads,
    x, c, qkv, p, ctx, h, act, dact, mid, st, mg, dmg, states, unit0, unit1, scale, res3, branch,
    hidden, middle, outs_t, outs_c, decay, drive, taps, perm,
    stage, got, held, temp, send, recv, local,
):
    seqs, length = tokens.shape[0], segr.shape[2]
    shard, width = tokens.shape[1], tokens.shape[2]
    block_chars = chars.shape[1]
    heads = p.shape[1]
    g = Group(send, recv, seqs)
    me = g.me
    saves = []

    def keep_out(seq, source, target):
        saves.append((source, target, len(saves)))

    def local_copy(number, seq, source, target):
        return pltpu.make_async_copy(source, target, local.at[number * seqs + seq])

    gx, gc = Gather(g, x, tokens), Gather(g, c, chars)
    gh, gm, gs = Gather(g, h), Gather(g, mid), Gather(g, st)
    narrow = lambda ref: (lambda s, i: ref.at[s, i, :, pl.ds(0, width)])
    wide = lambda ref: (lambda s, i: ref.at[s, i])
    own_n = lambda s: held.at[s, :, pl.ds(0, width)]
    own_w = lambda s: held.at[s]
    thin = temp.at[:, pl.ds(0, width)]
    s_attn = Scatter(g, narrow(stage), narrow(got), own_n, thin)
    s_ffn = Scatter(g, narrow(stage), narrow(got), own_n, thin)
    s_branch = Scatter(g, wide(stage), wide(got), own_w, temp)

    def own_x(seq):
        return local_copy(0, seq, tokens.at[seq], x.at[seq, me])

    def own_c(seq):
        return local_copy(1, seq, chars.at[seq], c.at[seq, me])

    plan = [
        (x, o_x), (c, o_c), (qkv, o_qkv), (p, o_p), (ctx, o_ctx), (h, o_h), (act, o_act),
        (dact, o_dact), (mid, o_mid), (st, o_st), (mg, o_mg), (dmg, o_dmg), (states, o_states),
        (unit0, o_unit0), (unit1, o_unit1), (scale, o_scale), (res3, o_res3), (branch, o_branch),
        (outs_t, token_out), (outs_c, char_out),
    ]

    def save(seq, *names):
        for name in names:
            for number, (source, target) in enumerate(plan):
                if source is name:
                    local_copy(2 + number, seq, source.at[seq], target.at[seq]).start()

    def each(body):
        def run(seq, carry):
            body(seq)
            return carry

        lax.fori_loop(0, seqs, run, 0)

    each(lambda s: (own_x(s).start(), own_c(s).start()))
    g.greet()
    each(gx.start)
    each(gc.start)

    for t in range(4):
        for d in range(2):
            row = lax.broadcasted_iota(jnp.int32, (LANE, width), 0)
            col = lax.broadcasted_iota(jnp.int32, (LANE, width), 1)
            first = d * 4 * units + t * units
            hit = (col - first == row) & (row < units)
            perm[pl.ds((2 * t + d) * LANE, LANE), :] = hit.astype(F32).astype(BF16)
    taps[...] = jnp.zeros_like(taps)
    norm_grads[...] = jnp.zeros_like(norm_grads)

    lane = lax.broadcasted_iota(jnp.int32, (shard, LANE), 1)
    left = lane < HD

    def attention(s):
        gx.forward(s)
        gx.finish(s)
        own_x(s).wait()
        save(s, x)

        def project(t, carry):
            rows = pl.ds(pl.multiple_of(t * shard, shard), shard)
            out = nn(x[s, t], wq[...])
            cols = qkv.shape[3]
            qkv[s, 0, rows, :] = (out[:, :cols] * 0.125).astype(BF16)
            qkv[s, 1, rows, :] = out[:, cols : 2 * cols].astype(BF16)
            qkv[s, 2, rows, :] = out[:, 2 * cols :].astype(BF16)
            return carry

        lax.fori_loop(0, 4, project, 0)
        save(s, qkv)

        def part(b):
            rows = pl.ds(pl.multiple_of(b * shard, shard), shard)
            same = segc[s, rows, :] == segr[s]
            for tile in range(qkv.shape[3] // LANE):
                cols = pl.ds(tile * LANE, LANE)
                result = None
                for half in range(2):
                    head = 2 * tile + half
                    if head >= heads:
                        continue
                    query = qkv[s, 0, rows, cols]
                    if 2 * tile + 1 < heads:
                        query = jnp.where(left if half == 0 else ~left, query, jnp.zeros_like(query))
                    scores = jnp.where(same, nt(query, qkv[s, 1, :, cols]), MASK_VALUE)
                    power = jnp.exp(scores - jnp.max(scores, axis=-1, keepdims=True))
                    probs = (power * (1.0 / jnp.sum(power, axis=-1, keepdims=True))).astype(BF16)
                    p[s, head, rows, :] = probs
                    mixed = nn(probs, qkv[s, 2, :, cols])
                    result = mixed if result is None else jnp.where(left, result, mixed)
                ctx[s, rows, cols] = result.astype(BF16)
            return nn(ctx[s, rows, :], wout[...])

        s_attn.start(s, part)
        save(s, p, ctx)

    each(attention)

    def first_norm(s):
        total = x[s, me].astype(F32) + s_attn.finish(s)
        unit, spread = normalize(total)
        unit0[s] = unit
        scale[s, 0] = jnp.broadcast_to(spread, (shard, LANE))
        hidden[s] = unit * gain[0:1] + bias[0:1]
        h[s, me] = hidden[s].astype(BF16)
        gh.start(s)
        save(s, unit0)

    def gru(s):
        gc.forward(s)
        gc.finish(s)
        own_c(s).wait()
        save(s, c)

        def gates(t, carry):
            rows = pl.ds(pl.multiple_of(t * LANE, LANE), LANE)
            per = block_chars // LANE
            inner = pl.ds(pl.multiple_of((t % per) * LANE, LANE), LANE)
            proj = nn(c[s, t // per, inner, :], wg[...])
            for tile in range(2):
                cols = slice(tile * LANE, (tile + 1) * LANE)
                gate = jax.nn.sigmoid(proj[:, cols] + gate_bias_pad(tile))
                cand = proj[:, (2 + tile) * LANE : (3 + tile) * LANE]
                decay[tile, rows, :] = (1.0 - gate) * keep[s, rows, tile : tile + 1]
                drive[tile, rows, :] = gate * cand
            return carry

        def gate_bias_pad(tile):
            return gate_bias[:, tile * LANE : (tile + 1) * LANE]

        total = 4 * block_chars
        lax.fori_loop(0, total // LANE, gates, 0)
        recur_plain((True, False), decay, drive, states.at[s], total // CHUNKS)

        def pick(t, carry):
            rows = pl.ds(pl.multiple_of(t * shard, shard), shard)
            for tile in range(2):
                ids = lax.broadcasted_iota(jnp.int32, (shard, total), 1)
                hot = (ids == pickc[s, rows, tile : tile + 1]).astype(F32).astype(BF16)
                out = nn(hot, states[s, tile].astype(BF16))
                st[s, me, rows, pl.ds(tile * LANE, LANE)] = out.astype(BF16)
            return carry

        lax.fori_loop(0, 4, pick, 0)
        gs.start(s)
        save(s, states)

    def norm_and_gru(s):
        first_norm(s)
        gru(s)

    each(norm_and_gru)

    def ffn(s):
        gh.forward(s)
        gh.finish(s)
        save(s, h)

        def part(b):
            value, slope = gelu_pair(nn(h[s, b], win[...]))
            act[s, b] = value.astype(BF16)
            dact[s, b] = slope.astype(BF16)
            return nn(act[s, b], wdown[...])

        s_ffn.start(s, part)
        save(s, act, dact)

    each(ffn)

    def second_norm(s):
        unit, spread = normalize(hidden[s] + s_ffn.finish(s))
        unit1[s] = unit
        scale[s, 1] = jnp.broadcast_to(spread, (shard, LANE))
        middle[s] = unit * gain[1:2] + bias[1:2]
        mid[s, me] = middle[s].astype(BF16)
        gm.start(s)
        save(s, unit1, scale)

    each(second_norm)

    def merge(s):
        gs.forward(s)
        gm.forward(s)
        gs.finish(s)
        gm.finish(s)
        save(s, mid, st)
        cols = mg.shape[2]

        def mix(t, carry):
            rows = pl.ds(pl.multiple_of(t * shard, shard), shard)
            total = nn(mid[s, t], wc[pl.ds(0, width), :])
            for u in range(4):
                weights = wc[pl.ds(width + u * 2 * LANE, 2 * LANE), :]
                total = total + nn(st[s, u, rows, :], weights)
            taps[pl.ds(pl.multiple_of(8 + t * shard, 8), shard), :] = total
            return carry

        lax.fori_loop(0, 4, mix, 0)

        def shifted(t, carry):
            rows = pl.ds(pl.multiple_of(t * shard, shard), shard)
            window = taps[pl.ds(pl.multiple_of(t * shard, 8), shard + 16), :]
            before = window[7 : 7 + shard, :cols] * edges[s, rows, 0:1]
            after = window[9 : 9 + shard, 2 * cols :] * edges[s, rows, 1:2]
            value, slope = gelu_pair(before + window[8 : 8 + shard, cols : 2 * cols] + after)
            mg[s, rows, :] = value.astype(BF16)
            dmg[s, rows, :] = slope.astype(BF16)
            return carry

        lax.fori_loop(0, 4, shifted, 0)

        def part(b):
            rows = pl.ds(pl.multiple_of(b * shard, shard), shard)
            return nn(mg[s, rows, :], wm[...])

        s_branch.start(s, part)
        save(s, mg, dmg)

    each(merge)

    def last_norms(s):
        total = s_branch.finish(s)
        rows = pl.ds(pl.multiple_of(me * shard, shard), shard)
        unit, spread = normalize(middle[s] + total[:, :width])
        outs_t[s] = (unit * gain[2:3] + bias[2:3]).astype(BF16)
        cot = cot_t[s]
        norm_grads[0:1] += jnp.sum(cot * unit, axis=0, keepdims=True)
        norm_grads[2:3] += jnp.sum(cot, axis=0, keepdims=True)
        back = normalize_back(unit, spread, cot * gain[2:3])
        res3[s] = back
        branch[s, :, pl.ds(0, width)] = back.astype(BF16)
        mine = total[:, width:]
        for u in range(4):
            mine = mine + nn(st[s, u, rows, :], perm[pl.ds(u * 2 * LANE, 2 * LANE), :])
        unit, spread = normalize(mine)
        outs_c[s] = (unit * gain[3:4] + bias[3:4]).astype(BF16)
        cot = cot_c[s]
        norm_grads[1:2] += jnp.sum(cot * unit, axis=0, keepdims=True)
        norm_grads[3:4] += jnp.sum(cot, axis=0, keepdims=True)
        branch[s, :, pl.ds(width, width)] = normalize_back(unit, spread, cot * gain[3:4]).astype(
            BF16
        )
        save(s, outs_t, outs_c, res3, branch)

    each(last_norms)

    def drain(s):
        for number, (source, target) in enumerate(plan):
            local_copy(2 + number, s, source.at[s], target.at[s]).wait()

    each(drain)


def forward_call(tokens, chars, weights, small, group_slots=27):
    seqs, shard, width = tokens.shape
    length, block_chars = shard * 4, chars.shape[1]
    total = block_chars * 4
    wq, wout, win, wdown, wg, gate_bias, wc, wm = weights
    cols = wq.shape[1] // 3
    heads = small["heads"]
    sds = jax.ShapeDtypeStruct
    big = {
        "x": ((seqs, 4, shard, width), BF16),
        "c": ((seqs, 4, block_chars, chars.shape[2]), BF16),
        "qkv": ((seqs, 3, length, cols), BF16),
        "p": ((seqs, heads, length, length), BF16),
        "ctx": ((seqs, length, cols), BF16),
        "h": ((seqs, 4, shard, width), BF16),
        "act": ((seqs, 4, shard, win.shape[1]), BF16),
        "dact": ((seqs, 4, shard, win.shape[1]), BF16),
        "mid": ((seqs, 4, shard, width), BF16),
        "st": ((seqs, 4, length, 2 * LANE), BF16),
        "mg": ((seqs, length, wm.shape[0]), BF16),
        "dmg": ((seqs, length, wm.shape[0]), BF16),
        "states": ((seqs, 2, total, LANE), F32),
        "unit0": ((seqs, shard, width), F32),
        "unit1": ((seqs, shard, width), F32),
        "scale": ((seqs, 2, shard, LANE), F32),
        "res3": ((seqs, shard, width), F32),
        "branch": ((seqs, shard, 2 * width), BF16),
    }
    rows = ((seqs, shard, width), F32)
    low_rows = ((seqs, shard, width), BF16)
    scratch = list(big.values()) + [
        rows, rows, low_rows, low_rows,
        ((2, total, LANE), F32), ((2, total, LANE), F32),
        ((length + 16, 3 * wm.shape[0]), F32),
        ((8 * LANE, width), BF16),
        ((seqs, 3, shard, 2 * width), BF16), ((seqs, 3, shard, 2 * width), BF16),
        ((seqs, shard, 2 * width), F32), ((shard, 2 * width), F32),
    ]
    anyspace = pl.BlockSpec(memory_space=pl.ANY)
    vmem = pl.BlockSpec(memory_space=pltpu.VMEM)
    out_shapes = [sds(low_rows[0], BF16)] * 2 + [sds(*v) for v in big.values()]
    ins = (
        tokens, chars, wq, wout, win, wdown, wg, gate_bias, wc, wm, small["gain"], small["bias"],
        small["cot_t"], small["cot_c"], small["segc"], small["segr"], small["pickc"],
        small["keep"], small["edges"],
    )
    outs = pl.pallas_call(
        functools.partial(forward_kernel, small["units"]),
        out_shape=out_shapes + [sds((4, width), F32)],
        in_specs=[anyspace] * 2 + [vmem] * (len(ins) - 2),
        out_specs=[anyspace] * len(out_shapes) + [vmem],
        scratch_shapes=[pltpu.VMEM(*v) for v in scratch]
        + [
            pltpu.SemaphoreType.DMA((group_slots * seqs,)),
            pltpu.SemaphoreType.DMA((group_slots * seqs,)),
            pltpu.SemaphoreType.DMA((24 * seqs,)),
        ],
        compiler_params=pltpu.CompilerParams(
            collective_id=0, has_side_effects=True, vmem_limit_bytes=62 * MIB
        ),
    )(*ins)
    names = ["token_out", "char_out"] + list(big) + ["norm_grads"]
    return dict(zip(names, outs))


def reduce_weights(grads):
    low = lax.psum(tuple(g.astype(jnp.bfloat16) for g in grads), "dp")
    return tuple(g.astype(jnp.float32) for g in low)


def local(
    tokens,
    characters,
    doc_lengths,
    token_chars,
    w_qkv,
    w_out,
    w_in,
    w_down,
    w_gru,
    gate_bias,
    w_conv,
    w_merge,
    norm_gain,
    norm_bias,
    token_cot,
    char_cot,
):
    micro_count = tokens.shape[0]
    shard_len = tokens.shape[1]
    model_width = tokens.shape[2]
    char_width = characters.shape[2]
    group_size = lax.axis_size("tensor")
    group_rank = lax.axis_index("tensor")
    length = shard_len * group_size
    char_total = characters.shape[1] * group_size
    head_cols = w_qkv.shape[2]
    heads_here = head_cols // HD
    units_here = w_gru.shape[3]
    merge_here = w_conv.shape[2]
    row_start = group_rank * shard_len
    qkv_matrix = w_qkv.reshape(model_width, 3 * head_cols)
    gru_matrix, gru_bias = gru_weights(w_gru, gate_bias)
    conv_matrix = w_conv.reshape(3 * 2 * model_width, merge_here)
    merge_matrix = w_merge.reshape(merge_here, 2 * model_width)
    spare = -head_cols % LANE
    wq = jnp.pad(w_qkv, ((0, 0), (0, 0), (0, spare))).reshape(model_width, -1)
    wout = jnp.pad(w_out, ((0, spare), (0, 0)))
    more = -merge_here % LANE
    wm = jnp.pad(merge_matrix, ((0, more), (0, 0)))
    conv_pad = jnp.pad(w_conv, ((0, 0), (0, 0), (0, more)))
    conv_mid = jnp.swapaxes(conv_pad[:, :model_width], 0, 1).reshape(model_width, -1)
    conv_char = conv_pad[:, model_width:].reshape(3, 2, group_size, units_here, -1)
    conv_char = jnp.pad(conv_char, ((0, 0),) * 3 + ((0, LANE - units_here), (0, 0)))
    conv_char = conv_char.transpose(2, 1, 3, 0, 4).reshape(group_size * 2 * LANE, -1)
    wc = jnp.concatenate([conv_mid, conv_char], axis=0)
    layouts = [layout(doc_lengths[i], token_chars[i], char_total) for i in range(micro_count)]
    stacked_layout = [jnp.stack(parts) for parts in zip(*layouts)]
    segment, first_char, last_char, keep_forward, keep_backward, prev_ok, next_ok = stacked_layout
    keep = jnp.stack([keep_forward, keep_backward], axis=2)
    picks = jnp.stack([last_char, first_char], axis=2)
    small = dict(
        gain=norm_gain, bias=norm_bias, cot_t=token_cot, cot_c=char_cot,
        segc=segment[:, :, None], segr=segment[:, None, :], pickc=picks, keep=keep,
        edges=jnp.stack([prev_ok, next_ok], axis=2), heads=heads_here, units=units_here,
    )
    fw = forward_call(
        tokens, characters, (wq, wout, w_in, w_down, gru_matrix, gru_bias, wc, wm), small
    )
    token_grads = []
    char_grads = []
    weight_total = None
    gain_total = jnp.zeros((4, model_width), jnp.float32).at[2:].set(fw["norm_grads"][:2])
    bias_total = jnp.zeros((4, model_width), jnp.float32).at[2:].set(fw["norm_grads"][2:])
    for i in range(micro_count):
        all_tokens = fw["x"][i].reshape(length, model_width)
        all_chars = fw["c"][i].reshape(char_total, char_width)
        hidden_all = fw["h"][i].reshape(length, model_width)
        activation = fw["act"][i].reshape(length, -1)
        queries, key_low, value_low = [
            fw["qkv"][i, k, :, :head_cols].reshape(length, heads_here, HD) for k in range(3)
        ]
        context_low = fw["ctx"][i, :, :head_cols]
        merged_low = fw["mg"][i, :, :merge_here]
        char_flat = (
            fw["st"][i].reshape(group_size, length, 2, LANE)[..., :units_here]
            .transpose(1, 2, 0, 3).reshape(length, model_width)
        )
        mid_all = fw["mid"][i].reshape(length, model_width)
        joined = jnp.concatenate([mid_all, char_flat], axis=1)
        stacked = conv_inputs(joined, prev_ok[i], next_ok[i])
        branch_grad = fw["branch"][i]
        grad_res3 = fw["res3"][i]
        grad_res4 = branch_grad[:, model_width:].astype(F32)
        branch_all = lax.all_gather(branch_grad, "tensor", axis=0, tiled=True)
        grad_merge_w = inner_rows(merged_low, branch_all)
        grad_merged = times_transposed(branch_all, merge_matrix)
        grad_pre_merge = (grad_merged * fw["dmg"][i, :, :merge_here]).astype(BF16)
        grad_conv_w = inner_rows(stacked, grad_pre_merge)
        grad_joined = conv_back(
            times_transposed(grad_pre_merge, conv_matrix), prev_ok[i], next_ok[i]
        )
        placed = lax.dynamic_update_slice_in_dim(
            jnp.zeros((length, model_width), F32), grad_res4, row_start, 0
        )
        grad_char_part = (grad_joined[:, model_width:] + placed).reshape(
            length, 2, units_here * group_size
        )
        scatter = lambda part, dim: lax.psum_scatter(
            part.astype(BF16), "tensor", scatter_dimension=dim, tiled=True
        ).astype(F32)
        grad_mid = grad_res3 + scatter(grad_joined[:, :model_width], 0)
        grad_char_tokens = scatter(grad_char_part, 2)

        def norm_grad(k, unit, spread, cot):
            back = normalize_back(unit, spread, cot * norm_gain[k])
            return back, jnp.sum(cot * unit, axis=0), jnp.sum(cot, axis=0)

        grad_res2, grad_g2, grad_b2 = norm_grad(
            1, fw["unit1"][i], fw["scale"][i, 1, :, :1], grad_mid
        )
        ffn_grad_all = lax.all_gather(grad_res2.astype(BF16), "tensor", axis=0, tiled=True)
        grad_down_w = inner_rows(activation, ffn_grad_all)
        slope = fw["dact"][i].reshape(length, -1)
        grad_pre = (times_transposed(ffn_grad_all, w_down) * slope).astype(BF16)
        grad_in_w = inner_rows(hidden_all, grad_pre)
        grad_hidden = grad_res2 + scatter(times_transposed(grad_pre, w_in), 0)
        grad_res1, grad_g1, grad_b1 = norm_grad(
            0, fw["unit0"][i], fw["scale"][i, 0, :, :1], grad_hidden
        )
        attn_grad_all = lax.all_gather(grad_res1.astype(BF16), "tensor", axis=0, tiled=True)
        grad_out_w = inner_rows(context_low, attn_grad_all)
        grad_context = (
            times_transposed(attn_grad_all, w_out).astype(BF16).reshape(length, heads_here, HD)
        )
        prob = fw["p"][i]
        grad_probs = jnp.einsum(
            "qhd,khd->hqk", grad_context, value_low, preferred_element_type=F32
        )
        prob_full = prob.astype(F32)
        row_dot = jnp.sum(prob_full * grad_probs, axis=-1, keepdims=True)
        grad_scores = (prob_full * (grad_probs - row_dot)).astype(BF16)
        query_grads = jnp.einsum(
            "hqk,khd->qhd", grad_scores, key_low, preferred_element_type=F32
        )
        grad_keys = jnp.einsum("hqk,qhd->khd", grad_scores, queries, preferred_element_type=F32)
        grad_values = jnp.einsum("hqk,qhd->khd", prob, grad_context, preferred_element_type=F32)
        grad_qkv_low = jnp.stack(
            [query_grads.astype(BF16) * 0.125, grad_keys.astype(BF16), grad_values.astype(BF16)],
            axis=1,
        ).reshape(length, 3 * head_cols)
        grad_qkv_w = inner_rows(all_tokens, grad_qkv_low)
        token_part = times_transposed(grad_qkv_low, qkv_matrix)
        grad_tok_pad = jnp.pad(
            grad_char_tokens.astype(BF16), ((0, 0), (0, 0), (0, LANE - units_here))
        ).reshape(length, 2 * LANE)
        grad_proj_low, grad_gate = gru_call(
            gru_bwd_kernel,
            (
                jax.ShapeDtypeStruct((char_total, 4 * LANE), BF16),
                jax.ShapeDtypeStruct((1, 2 * LANE), F32),
            ),
            5,
            char_total,
        )(all_chars, gru_matrix, gru_bias, keep[i], picks[i].T, fw["states"][i], grad_tok_pad)
        grad_gate = grad_gate.reshape(2, LANE)[:, :units_here]
        grad_gru_w = jnp.swapaxes(
            inner_rows(all_chars, grad_proj_low).reshape(char_width, 2, 2, LANE)[
                ..., :units_here
            ],
            1,
            2,
        )
        char_part = times_transposed(grad_proj_low, gru_matrix)
        token_grads.append(grad_res1 + scatter(token_part, 0))
        char_grads.append(scatter(char_part, 0))
        gain_total = gain_total.at[:2].add(jnp.stack([grad_g1, grad_g2]))
        bias_total = bias_total.at[:2].add(jnp.stack([grad_b1, grad_b2]))
        micro_grads = (
            grad_qkv_w.reshape(model_width, 3, head_cols),
            grad_out_w,
            grad_in_w,
            grad_down_w,
            grad_gru_w,
            grad_gate,
            grad_conv_w.reshape(3, 2 * model_width, merge_here),
            grad_merge_w.reshape(merge_here, 2, model_width),
        )
        if weight_total is None:
            weight_total = micro_grads
        else:
            weight_total = jax.tree.map(jnp.add, weight_total, micro_grads)
    weight_final = reduce_weights(weight_total)
    gain_grad, bias_grad = lax.psum((gain_total, bias_total), ("dp", "tensor"))
    return (
        fw["token_out"],
        fw["char_out"],
        jnp.stack(token_grads, axis=0),
        jnp.stack(char_grads, axis=0),
        weight_final[0],
        weight_final[1],
        weight_final[2],
        weight_final[3],
        weight_final[4],
        weight_final[5],
        weight_final[6],
        weight_final[7],
        gain_grad,
        bias_grad,
    )


def solution(mesh):
    return jax.shard_map(
        local,
        mesh=mesh,
        in_specs=(
            P("dp", "tensor", None),
            P("dp", "tensor", None),
            P("dp", None),
            P("dp", None),
            P(None, None, "tensor"),
            P("tensor", None),
            P(None, "tensor"),
            P("tensor", None),
            P(None, None, None, "tensor"),
            P(None, "tensor"),
            P(None, None, "tensor"),
            P("tensor", None, None),
            P(),
            P(),
            P("dp", "tensor", None),
            P("dp", "tensor", None),
        ),
        out_specs=(
            P("dp", "tensor", None),
            P("dp", "tensor", None),
            P("dp", "tensor", None),
            P("dp", "tensor", None),
            P(None, None, "tensor"),
            P("tensor", None),
            P(None, "tensor"),
            P("tensor", None),
            P(None, None, None, "tensor"),
            P(None, "tensor"),
            P(None, None, "tensor"),
            P("tensor", None, None),
            P(),
            P(),
        ),
        check_vma=False,
    )
```

time: 857 us -> 741 us (0.86)
  waiting for transfers between devices: 337 us -> 216 us
  Pallas kernels: 44.9 us -> 138 us
  blocking collectives: 182 us -> 98.2 us
  local copies, waits for them, and re-layouts: 96.1 us -> 137 us
  matrix products: 95.6 us -> 60.7 us
  other arithmetic: 70.2 us -> 49.7 us
  starting transfers between devices: 2.04 us -> 12.8 us
    pallas_call x4 -> x3, Pallas kernels: 44.9 us -> 138 us  [the longest x1 113 us: forward_call(): pl.pallas_call(functools.partial(forward_kernel, small['units']), out_sha...]
    all_gather x12 -> x4, blocking collectives: 123 us -> 37 us  [the longest x2 19.5 us: local(): lax.all_gather(grad_res1.astype(BF16), 'tensor', axis=0, tiled=True)]
    reduce_scatter x14 -> x8, waiting for transfers between devices: 97.8 us -> 12.5 us  [local(): lax.psum_scatter(part.astype(BF16), 'tensor', scatter_dimension=dim, tile...]
    dot_general x22 -> x6, matrix products: 38.1 us -> 2.71 us  [the longest x2 1.19 us: local(): jnp.einsum('hqk,khd->qhd', grad_scores, key_low, preferred_element_type=F32)]
    all_gather x2, waiting for transfers between devices: 26.2 us -> 0.02 us  [local(): branch_all = lax.all_gather(branch_grad, 'tensor', axis=0, tiled=True)]
    slice x9 -> x22, local copies, waits for them, and re-layouts: 7.64 us -> 31 us  [the longest x7 10.2 us: local(): fw['qkv'][i, k, :, :head_cols].reshape(length, heads_here, HD)]
    reduce_sum x23 -> x2, other arithmetic: 24 us -> 2.86 us  [norm_grad(): return (back, jnp.sum(cot * unit, axis=0), jnp.sum(cot, axis=0))]
    another operation x4 -> x19, local copies, waits for them, and re-layouts: 1.02 us -> 14.7 us  [the longest x2 4.68 us: local(): mid_all = fw['mid'][i].reshape(length, model_width)]
  transfers between devices with their start and end apart: 20 -> 12, of which waited for: 9 -> 2; matrix products, arithmetic and copies ran while one was open for 22% -> 24% of each run, Pallas kernels for 5% -> 3%
where the time goes in v2:
time: 741 us; the launch traced here: 729 us
  waiting for transfers between devices  216 us (29%)
  Pallas kernels  138 us (19%)
  local copies, waits for them, and re-layouts  137 us (18%)
  blocking collectives  98.2 us (13%)
  matrix products  60.7 us (8%)
  other arithmetic  49.7 us (7%)
  between operations  16.5 us (2%)
  starting transfers between devices  12.8 us (2%)
    psum x1, waiting for transfers between devices, reduce_weights(): low = lax.psum(tuple((g.astype(jnp.bfloat16) for g in grads)), 'dp')  202 us
    pallas_call x1, Pallas kernels, forward_call(): pl.pallas_call(functools.partial(forward_kernel, small['units']), out_sha...  113 us
    unnamed x219, local copies, waits for them, and re-layouts  42.9 us
    psum x1, blocking collectives, local(): gain_grad, bias_grad = lax.psum((gain_total, bias_total), ('dp', 'tensor'))  39.8 us
    dot_general x14, matrix products, inner_rows(): lax.dot_general(left_rows, right_rows, (((0,), (0,)), ((), ())), preferre...  36.9 us
    pallas_call x2, Pallas kernels, local(): gru_call(gru_bwd_kernel, (jax.ShapeDtypeStruct((char_total, 4 * LANE), BF...  25.2 us
    psum x1, blocking collectives, reduce_weights(): low = lax.psum(tuple((g.astype(jnp.bfloat16) for g in grads)), 'dp')  21.4 us
    dot_general x14, matrix products, times_transposed(): lax.dot_general(left_rows, right_matrix, (((1,), (1,)), ((), ())), prefer...  19.5 us
  transfers between devices with their start and end apart: 12, of which 2 were waited for; matrix products, arithmetic and copies ran while one was open for 24% of the time, Pallas kernels for 3%

profile of v2, /device:TPU:0, one launch (start us, length us, event | category | flops | bytes accessed | tf_op | source)
XLA Modules:
  0.0 729.2 jit_solution(13805427920124078528)
XLA Ops:
  15.9 1.7 pad.58.wout
  25.8 2.0 copy.155
  27.8 3.0 pad_slice_fusion.1
  32.4 2.4 copy.149
  39.8 1.9 pad_maximum_fusion.1.keep
  43.5 113.2 %shard_map.263 = (bf16[2,128,768]{2,1,0:T(8,128)(2,1)}, bf16[2,128,768]{2,1,0:T(8,128)(2,1)}, bf16[2,4,128,768]{3,2,1,0:T(8,128)(2,1)}, bf16[2,4,512,256]{3,2,1,...) custom-call(bf16[2,128,768]{2,1,0:T(8,128)(2,1)} %tokens.1, ...), custom_call_target="tpu_custom_call" | custom-call | tf_op jit(solution)/shard_map/pallas_call | solution.py:743
  156.7 2.5 slice_bitcast_fusion.5
  160.4 3.1 fusion.88
  165.3 2.8 fusion.165
  174.8 2.3 copy.184
  177.1 2.4 copy.181
  179.4 3.2 fusion.159
  184.1 2.1 reshape_squeeze.73
  186.2 3.6 copy.210
  189.8 2.2 reshape_squeeze.71
  192.0 3.6 copy.209
  195.6 2.7 slice_maximum_fusion.1
  199.6 2.0 fusion.52
  208.6 2.0 fusion.55
  214.9 1.7 copy-done.12
  217.6 11.5 %all-reduce.27.cloned.1.call-start = ((), (), s32[]{:S(2)}) async-start(), calls=%async_computation.19 | async-start | bytes 3145728
  229.1 3.1 fusion.27
  232.3 2.0 fusion.29
  236.7 2.2 convert_element_type.443
  238.9 2.2 copy.176
  243.0 2.2 convert_element_type.439
  245.2 2.2 copy.174
  247.5 12.5 %reduce-scatter.9.cloned.1.call-done = bf16[128,768]{1,0:T(8,128)(2,1)} async-done(((bf16[512,768]{1,0:T(8,128)(2,1)}), bf16[128,768]{1,0:T(8,128)(2,1)}) %reduce-scatter.9.cloned.1.call-update) | async-done | bytes 196624 | tf_op jit(solution)/shard_map/reduce_scatter | solution.py:865
  262.6 8.7 %all_gather.19 = bf16[512,768]{1,0:T(8,128)(2,1)S(1)} all-gather(bf16[128,768]{1,0:T(8,128)(2,1)S(1)} %get-tuple-element.259), channel_id=1, replica_groups=mesh['dp'=8,'tensor'=4] {'tensor'}, dimensions={0}, use_global_device_ids=true | all-gather | bytes 983040 | tf_op jit(solution)/shard_map/all_gather | solution.py:878
  274.9 2.4 fusion.164
  277.3 2.0 pad_multiply_fusion.1
  279.3 8.8 %all_gather.22 = bf16[512,768]{1,0:T(8,128)(2,1)S(1)} all-gather(bf16[128,768]{1,0:T(8,128)(2,1)S(1)} %copy-done.79), channel_id=1, replica_groups=mesh['dp'=8,'tensor'=4] {'tensor'}, dimensions={0}, use_global_device_ids=true | all-gather | bytes 983040 | tf_op jit(solution)/shard_map/all_gather | solution.py:878
  291.7 1.9 copy.163
  293.6 1.7 copy.173
  295.3 1.8 copy.170
  300.8 2.1 pad_multiply_fusion
  302.9 4.5 slice_bitcast_fusion.1
  307.4 2.8 copy.205
  316.1 12.6 %shard_map.265 = (bf16[2048,512]{1,0:T(8,128)(2,1)S(1)}, f32[1,256]{1,0:T(1,128)S(1)}) custom-call(bf16[2048,256]{1,0:T(8,128)(2,1)S(1)} %bitcast.392, bf16[256,512]{1,0:T(8,128)(2,1)S(1)} %copy-done, f32[1,256]{1,0:T(1,128)S(1)} %bitcast.397, f32[2048,2]{1,0:T(8,128)S(1)} %copy-done.5, s32[2,512]{1,0:T(2,128)S(1)} %get-tuple-element.286.pick_ref, ...), custom_call_target="tpu_custom_call" | custom-call | tf_op jit(solution)/shard_map/pallas_call | solution.py:913
  331.0 6.2 fusion.1
  337.3 11.8 %fusion = bf16[4608,192]{0,1:T(8,128)(2,1)} fusion(f32[4608,192]{0,1:T(8,128)S(1)} %fusion.1, bf16[512,192]{1,0:T(8,128)(2,1)S(1)} %copy-done.94, bf16[512,1536]{0,1:T(8,128)(2,1)S(1)} %copy-done.51, bf16[512,768]{0,1:T(8,128)(2,1)S(1)} %bitcast.407, bf16[512,768]{0,1:T(8,128)(2,1)S(1)} %copy-done.19, bf16[512,1536]{0,1:T(8,128)(2,1)S(1)} %copy-done.56), kind=kOutput, calls=%fused_computation.1 | convolution fusion | flops 926613504 | bytes 10223616 | tf_op jit(solution)/shard_map/dot_general | solution.py:205
  349.0 5.2 convert_element_type.463
  354.2 2.3 fusion.108
  358.1 1.7 constant_dynamic-slice_fusion.1
  359.8 1.9 copy.212
  363.7 2.4 copy.203
  368.3 12.6 %shard_map.264 = (bf16[2048,512]{1,0:T(8,128)(2,1)S(1)}, f32[1,256]{1,0:T(1,128)S(1)}) custom-call(bf16[2048,256]{1,0:T(8,128)(2,1)S(1)} %bitcast.390, bf16[256,512]{1,0:T(8,128)(2,1)S(1)} %copy-done, f32[1,256]{1,0:T(1,128)S(1)} %bitcast.398, f32[2048,2]{1,0:T(8,128)S(1)} %get-tuple-element.249.keep_ref, s32[2,512]{1,0:T(2,128)S(1)} %get-tuple-element.285.pick_ref, ...), custom_call_target="tpu_custom_call" | custom-call | tf_op jit(solution)/shard_map/pallas_call | solution.py:913
  380.9 2.5 copy.202
  383.4 1.8 convolution_convert_fusion.1
  385.3 2.1 fusion.30
  391.6 8.9 %all_gather.20 = bf16[512,768]{1,0:T(8,128)(2,1)S(1)} all-gather(bf16[128,768]{1,0:T(8,128)(2,1)S(1)} %get-tuple-element.235), channel_id=1, replica_groups=mesh['dp'=8,'tensor'=4] {'tensor'}, dimensions={0}, use_global_device_ids=true | all-gather | bytes 983040 | tf_op jit(solution)/shard_map/all_gather | solution.py:887
  400.5 10.7 %all_gather.23 = bf16[512,768]{1,0:T(8,128)(2,1)S(1)} all-gather(bf16[128,768]{1,0:T(8,128)(2,1)S(1)} %get-tuple-element.277), channel_id=1, replica_groups=mesh['dp'=8,'tensor'=4] {'tensor'}, dimensions={0}, use_global_device_ids=true | all-gather | bytes 983040 | tf_op jit(solution)/shard_map/all_gather | solution.py:887
  419.9 2.3 fusion.175
  422.3 1.9 add_convert_fusion
  428.5 2.1 fusion.174
  430.7 1.9 add_convert_fusion.1
  437.0 21.4 %psum.75 = bf16[2,96]{1,0:T(2,128)(2,1)S(1)} all-reduce(bf16[2,96]{1,0:T(2,128)(2,1)S(1)} %add_convert_fusion.3), channel_id=1, replica_groups=mesh['dp'=8,'tensor'=4] {'dp'}, use_global_device_ids=true, to_apply=%region_43.44 | all-reduce | flops 192 | bytes 768 | tf_op jit(solution)/shard_map/psum | solution.py:763
  459.0 2.1 maximum_convert_fusion
  461.2 39.8 %all-reduce.19 = (f32[4,768]{1,0:T(4,128)}, f32[4,768]{1,0:T(4,128)}) all-reduce(f32[4,768]{1,0:T(4,128)S(1)} %fusion.127, f32[4,768]{1,0:T(4,128)S(1)} %fusion.128), channel_id=1, replica_groups=mesh['dp'=8,'tensor'=4] {'dp','tensor'}, use_global_device_ids=true, to_apply=%region_50.51 | all-reduce | flops 6144 | bytes 49152 | tf_op jit(solution)/shard_map/psum | solution.py:950
  504.0 202.5 %all-reduce.25.cloned.1.call-done = (bf16[256,2,2,96]{0,3,1,2:T(8,128)(2,1)}, bf16[3,1536,192]{1,0,2:T(4,128)(2,1)}, bf16[192,2,768]{2,0,1:T(8,128)(2,1)}, bf16[...) async-done(((bf16[256,2,2,96]{0,3,1,2:T(8,128)(2,1)}, bf16[3,1536,192]{1,0,2:T(4,128)(2,1)}, ...) | async-done | bytes 6094864 | tf_op jit(solution)/shard_map/psum | solution.py:763
  706.4 1.8 copy.190
  708.2 1.8 convert_element_type.448
  710.0 2.8 copy.192
  718.3 2.3 copy.191
  (398 shorter events, 112.4 us)
Async XLA Ops:
  7.2 192.4 %all-gather.7.cloned.1.call-start = ((), (), s32[]{:S(2)}) async-start(), calls=%async_computation.17 | async-start | bytes 1966080 | tf_op jit(solution)/shard_map/all_gather | solution.py:851
  13.6 8.1 %copy-start.88 = (bf16[192,2,768]{2,1,0:T(2,128)(2,1)S(1)}, bf16[192,2,768]{2,1,0:T(2,128)(2,1)}, u32[]{:S(2)}) copy-start(bf16[192,2,768]{2,1,0:T(2,128)(2,1)} %param.39) | copy-start | bytes 1769476
  18.7 4.9 copy-start.66
  25.8 14.0 %copy-start.8 = (f32[2,2048,1]{2,1,0:T(8,128)}, f32[2,2048,1]{2,1,0:T(8,128)S(1)}, u32[]{:S(2)}) copy-start(f32[2,2048,1]{2,1,0:T(8,128)S(1)} %copy.154) | copy-start | bytes 49156
  37.6 2.2 copy-start.10
  156.7 3.7 copy-start.9
  159.2 49.4 %all-gather.5.cloned.1.call-start = ((), (), s32[]{:S(2)}) async-start(), calls=%async_computation.16 | async-start | bytes 1966080 | tf_op jit(solution)/shard_map/all_gather | solution.py:851
  159.9 87.6 %reduce-scatter.15.cloned.1.call-start = ((), (), s32[]{:S(2)}) async-start(), calls=%async_computation.11 | async-start | bytes 983040 | tf_op jit(solution)/shard_map/reduce_scatter | solution.py:865
  165.2 3.0 copy-start.55
  168.1 2.1 copy-start.54
  169.4 2.1 copy-start.53
  179.4 3.2 copy-start.48
  195.6 2.8 copy-start.13
  195.6 2.8 copy-start.17
  208.5 51.5 %reduce-scatter.9.cloned.1.call-start = ((), (), s32[]{:S(2)}) async-start(), calls=%async_computation.8 | async-start | bytes 983040 | tf_op jit(solution)/shard_map/reduce_scatter | solution.py:865
  216.6 12.5 %copy-start.97 = (f32[4,768]{1,0:T(4,128)S(1)}, f32[4,768]{1,0:T(4,128)}, u32[]{:S(2)}) copy-start(f32[4,768]{1,0:T(4,128)} %gain.1) | copy-start | bytes 36868
  216.6 12.5 %copy-start.16 = (bf16[4,512,2,96]{1,3,0,2:T(8,128)(2,1)S(1)}, bf16[4,512,2,96]{1,3,0,2:T(8,128)(2,1)}, u32[]{:S(2)}) copy-start(bf16[4,512,2,96]{1,3,0,2:T(8,128)(2,1)} %copy.209) | copy-start | bytes 2359300
  217.6 14.7 %copy-start.14 = (bf16[4,512,2,96]{1,3,0,2:T(8,128)(2,1)S(1)}, bf16[4,512,2,96]{1,3,0,2:T(8,128)(2,1)}, u32[]{:S(2)}) copy-start(bf16[4,512,2,96]{1,3,0,2:T(8,128)(2,1)} %copy.210) | copy-start | bytes 2359300
  217.6 14.7 %copy-start.18 = (bf16[512,768]{0,1:T(8,128)(2,1)S(1)}, bf16[512,768]{0,1:T(8,128)(2,1)}, u32[]{:S(2)}) copy-start(bf16[512,768]{0,1:T(8,128)(2,1)} %copy.184) | copy-start | bytes 2359300
  217.6 94.1 %all-reduce.27.cloned.1.call-start = ((), (), s32[]{:S(2)}) async-start(), calls=%async_computation.19 | async-start | bytes 3145728
  236.7 4.4 slice-start.1
  243.0 17.0 %copy-start.33 = (f32[2,128,768]{2,1,0:T(8,128)S(1)}, f32[2,128,768]{2,1,0:T(8,128)}, u32[]{:S(2)}) copy-start(f32[2,128,768]{2,1,0:T(8,128)} %get-tuple-element.117) | copy-start | bytes 2359300
  243.0 17.0 %copy-start.34 = (f32[2,128,768]{2,1,0:T(8,128)S(1)}, f32[2,128,768]{2,1,0:T(8,128)}, u32[]{:S(2)}) copy-start(f32[2,128,768]{2,1,0:T(8,128)} %get-tuple-element.114) | copy-start | bytes 2359300
  247.4 141.5 %reduce-scatter.11.cloned.1.call-start = ((), (), s32[]{:S(2)}) async-start(), calls=%async_computation.9 | async-start | bytes 983040 | tf_op jit(solution)/shard_map/reduce_scatter | solution.py:865
  247.5 13.9 %copy-start.75 = (bf16[128,768]{1,0:T(8,128)(2,1)S(1)}, bf16[128,768]{1,0:T(8,128)(2,1)}, u32[]{:S(2)}) copy-start(bf16[128,768]{1,0:T(8,128)(2,1)} %reduce-scatter.15.cloned.1.call-done) | copy-start | bytes 589828
  261.4 9.9 %copy-start.59 = (bf16[768,768]{1,0:T(8,128)(2,1)S(1)}, bf16[768,768]{1,0:T(8,128)(2,1)}, u32[]{:S(2)}) copy-start(bf16[768,768]{1,0:T(8,128)(2,1)} %wdown.1) | copy-start | bytes 3538948
  261.4 9.9 %copy-start.78 = (bf16[1,4,128,768]{3,2,1,0:T(8,128)(2,1)S(1)}, bf16[1,4,128,768]{3,2,1,0:T(8,128)(2,1)}, u32[]{:S(2)}) copy-start(bf16[1,4,128,768]{3,2,1,0:T(8,128)(2,1)} %get-tuple-element.276) | copy-start | bytes 2359300
  274.8 2.5 copy-start.23
  274.8 114.1 %reduce-scatter.17.cloned.1.call-start = ((), (), s32[]{:S(2)}) async-start(), calls=%async_computation.12 | async-start | bytes 983040 | tf_op jit(solution)/shard_map/reduce_scatter | solution.py:865
  277.3 10.8 %copy-start.60 = (bf16[768,768]{1,0:T(8,128)(2,1)S(1)}, bf16[768,768]{1,0:T(8,128)(2,1)}, u32[]{:S(2)}) copy-start(bf16[768,768]{1,0:T(8,128)(2,1)} %wdown.1) | copy-start | bytes 3538948
  277.3 10.8 %copy-start.77 = (bf16[1,4,128,768]{3,2,1,0:T(8,128)(2,1)S(1)}, bf16[1,4,128,768]{3,2,1,0:T(8,128)(2,1)}, u32[]{:S(2)}) copy-start(bf16[1,4,128,768]{3,2,1,0:T(8,128)(2,1)} %get-tuple-element.275) | copy-start | bytes 2359300
  291.6 7.9 %copy-start.100 = (u32[32]{0:T(128)S(1)}, u32[32]{0:T(128)}, u32[]{:S(2)}) copy-start(u32[32]{0:T(128)} %constant.219) | copy-start | bytes 388
  291.6 9.1 %copy-start.22 = (bf16[511,1536]{0,1:T(8,128)(2,1)S(1)}, bf16[511,1536]{0,1:T(8,128)(2,1)}, u32[]{:S(2)}) copy-start(bf16[511,1536]{0,1:T(8,128)(2,1)} %slice_maximum_fusion) | copy-start | bytes 4709380
  291.6 167.3 %reduce-scatter.23.cloned.1.call-start = ((), (), s32[]{:S(2)}) async-start(), calls=%async_computation.15 | async-start | bytes 1310720 | tf_op jit(solution)/shard_map/reduce_scatter | solution.py:865
  307.4 2.8 copy-start.50
  310.1 3.4 copy-start
  310.1 3.4 copy-start.7
  330.5 128.5 %reduce-scatter.21.cloned.1.call-start = ((), (), s32[]{:S(2)}) async-start(), calls=%async_computation.14 | async-start | bytes 1310720 | tf_op jit(solution)/shard_map/reduce_scatter | solution.py:865
  331.0 6.3 copy-start.15
  331.0 6.3 copy-start.19
  331.0 6.3 copy-start.51
  331.0 6.3 copy-start.56
  331.0 6.3 copy-start.94
  354.2 2.3 copy-start.24
  354.2 2.4 copy-start.89
  385.3 2.3 copy-start.2
  385.3 115.8 %reduce-scatter.19.cloned.1.call-start = ((), (), s32[]{:S(2)}) async-start(), calls=%async_computation.13 | async-start | bytes 983040 | tf_op jit(solution)/shard_map/reduce_scatter | solution.py:865
  385.3 2.4 copy-start.49
  390.5 20.7 %copy-start.38 = (bf16[192,768]{1,0:T(8,128)(2,1)S(1)}, bf16[192,768]{1,0:T(8,128)(2,1)}, u32[]{:S(2)}) copy-start(bf16[192,768]{1,0:T(8,128)(2,1)} %param.33) | copy-start | bytes 884740
  391.6 19.9 %copy-start.74 = (bf16[1,1,512,192]{2,3,1,0:T(8,128)(2,1)S(1)}, bf16[1,1,512,192]{2,3,1,0:T(8,128)(2,1)}, u32[]{:S(2)}) copy-start(bf16[1,1,512,192]{2,3,1,0:T(8,128)(2,1)} %copy.170) | copy-start | bytes 589828
  419.9 82.2 %reduce-scatter.13.cloned.1.call-start = ((), (), s32[]{:S(2)}) async-start(), calls=%async_computation.10 | async-start | bytes 983040 | tf_op jit(solution)/shard_map/reduce_scatter | solution.py:865
  419.9 2.3 copy-start.29
  419.9 2.3 copy-start.31
  422.3 2.3 copy-start.81
  428.2 278.2 %all-reduce.25.cloned.1.call-start = ((), (), s32[]{:S(2)}) async-start(), calls=%async_computation.18 | async-start | bytes 13369344 | tf_op jit(solution)/shard_map/psum | solution.py:763
  428.5 2.1 copy-start.28
  428.5 2.1 copy-start.71
  436.2 64.8 %copy-start.58 = (f32[128,768]{1,0:T(8,128)S(1)}, f32[128,768]{1,0:T(8,128)}, u32[]{:S(2)}) copy-start(f32[128,768]{1,0:T(8,128)} %get-tuple-element.278) | copy-start | bytes 1179652
  436.3 65.8 %copy-start.57 = (f32[128,768]{1,0:T(8,128)S(1)}, f32[128,768]{1,0:T(8,128)}, u32[]{:S(2)}) copy-start(f32[128,768]{1,0:T(8,128)} %get-tuple-element.236) | copy-start | bytes 1179652
  706.4 6.4 copy-start.69
  710.0 4.1 copy-start.64
  715.7 2.5 copy-start.45
  718.3 2.4 copy-start.92
  718.3 3.1 copy-start.91
  (51 other events, 73.8 us)
Sparse Core Ops, SparseCore 0:
  159.3 21.3 all-gather.6
  182.3 19.6 all-gather.4
  208.7 24.8 reduce-scatter.14
  236.7 23.2 reduce-scatter.8
  262.2 43.7 all-reduce.26
  309.0 23.2 reduce-scatter.10
  335.0 23.2 reduce-scatter.16
  360.8 24.8 reduce-scatter.22
  388.5 26.4 reduce-scatter.20
  420.0 25.5 reduce-scatter.18
  448.8 23.5 reduce-scatter.12
  478.8 227.5 all-reduce.24

commit v3 on v2

v3 whole, which is shorter than its diff:
```python
import functools

import jax
import jax.numpy as jnp
from jax import lax
from jax.experimental import pallas as pl
from jax.experimental.pallas import tpu as pltpu
from jax.sharding import PartitionSpec as P

HD = 64


NORM_EPSILON = 1e-06
MASK_VALUE = -1e30
HIGH_PRECISION = lax.Precision.HIGHEST


def layout(doc_sizes, char_counts, char_total):
    length = char_counts.shape[0]
    docs = doc_sizes.shape[0]
    doc_ids = jnp.arange(docs, dtype=jnp.int32)
    doc_ends = jnp.sum(
        jnp.where(doc_ids[None, :] <= doc_ids[:, None], doc_sizes[None, :], 0), axis=1
    )
    positions = jnp.arange(length, dtype=jnp.int32)
    segment = jnp.sum(
        (positions[:, None] >= doc_ends[None, :]).astype(jnp.int32), axis=1, dtype=jnp.int32
    )
    token_ends = jnp.sum(
        jnp.where(positions[None, :] <= positions[:, None], char_counts[None, :], 0), axis=1
    )
    last_char = token_ends - 1
    first_char = token_ends - char_counts
    char_ends = jnp.sum(
        jnp.where(positions[None, :] < doc_ends[:, None], char_counts[None, :], 0), axis=1
    )
    char_positions = jnp.arange(char_total, dtype=jnp.int32)
    starts = char_ends - jnp.sum(
        jnp.where(
            (positions[None, :] < doc_ends[:, None])
            & (positions[None, :] >= (doc_ends - doc_sizes)[:, None]),
            char_counts[None, :],
            0,
        ),
        axis=1,
    )
    keep_forward = 1.0 - jnp.any(char_positions[:, None] == starts[None, :], axis=1).astype(
        jnp.float32
    )
    keep_backward = 1.0 - jnp.any(
        char_positions[:, None] == (char_ends - 1)[None, :], axis=1
    ).astype(jnp.float32)
    token_starts = doc_ends - doc_sizes
    prev_ok = 1.0 - jnp.any(positions[:, None] == token_starts[None, :], axis=1).astype(
        jnp.float32
    )
    next_ok = 1.0 - jnp.any(positions[:, None] == (doc_ends - 1)[None, :], axis=1).astype(
        jnp.float32
    )
    return (segment, first_char, last_char, keep_forward, keep_backward, prev_ok, next_ok)


F32 = jnp.float32
BF16 = jnp.bfloat16
LANE = 128
CHUNKS = 32
MIB = 1024 * 1024
VMEM = pl.BlockSpec(memory_space=pltpu.VMEM)


def gru_weights(w_gru, gate_bias):
    width, _, _, units = w_gru.shape
    matrix = jnp.pad(jnp.swapaxes(w_gru, 1, 2), ((0, 0), (0, 0), (0, 0), (0, LANE - units)))
    bias = jnp.pad(gate_bias, ((0, 0), (0, LANE - units)))
    return matrix.reshape(width, 4 * LANE), bias.reshape(1, 2 * LANE)


def nn(left, right):
    return jnp.dot(left, right, preferred_element_type=F32)


def nt(left, right):
    return lax.dot_general(left, right, (((1,), (1,)), ((), ())), preferred_element_type=F32)


def tn(left, right):
    return lax.dot_general(left, right, (((0,), (0,)), ((), ())), preferred_element_type=F32)


def gelu_pair(values):
    cdf = 0.5 * (1.0 + lax.erf(values * 0.7071067811865476))
    density = 0.3989422804014327 * jnp.exp(-0.5 * values * values)
    return values * cdf, cdf + values * density


def normalize(rows):
    centered = rows - jnp.mean(rows, axis=-1, keepdims=True)
    scale = lax.rsqrt(jnp.mean(centered * centered, axis=-1, keepdims=True) + NORM_EPSILON)
    return centered * scale, scale


def normalize_back(unit, scale, grad_unit):
    return scale * (
        grad_unit
        - jnp.mean(grad_unit, axis=-1, keepdims=True)
        - unit * jnp.mean(grad_unit * unit, axis=-1, keepdims=True)
    )


def roll_lanes(value, shift):
    return pltpu.roll(value, shift % value.shape[1], axis=1)


def unpack3(packed, size):
    room = -(-size // LANE) * LANE
    lane = lax.broadcasted_iota(jnp.int32, (packed.shape[0], room), 1)
    parts = []
    for k in range(3):
        first = k * size // LANE * LANE
        inner = k * size - first
        part = packed[:, first : min(first + room + LANE, packed.shape[1])]
        if inner:
            part = roll_lanes(part, -inner)
        parts.append(jnp.where(lane < size, part[:, :room], 0.0))
    return parts


def pack3(parts, size):
    room = parts[0].shape[1]
    columns = -(-3 * size // LANE) * LANE
    tiles = [None] * (columns // LANE)
    for k in range(3):
        first, inner = divmod(k * size, LANE)
        part = parts[k]
        if inner:
            part = jnp.concatenate([part, jnp.zeros_like(part[:, :LANE])], axis=1)
            part = roll_lanes(part, inner)
        for j in range(part.shape[1] // LANE):
            if first + j < len(tiles) and (first + j) * LANE < (k + 1) * size:
                tile = part[:, j * LANE : (j + 1) * LANE]
                old = tiles[first + j]
                tiles[first + j] = tile if old is None else old + tile
    return jnp.concatenate(tiles, axis=1)


class Group:
    def __init__(self, send, recv, seqs):
        self.me = lax.axis_index("tensor")
        self.low = self.me % 2
        self.high = self.me // 2
        self.pair = self.high * 2 + (1 - self.low)
        self.far = (1 - self.high) * 2 + self.low
        self.send, self.recv, self.seqs, self.used = send, recv, seqs, 0

    def block(self, turn):
        left = 3 - turn
        return ((self.high + left // 2) % 2) * 2 + (self.low + left % 2) % 2

    def slots(self, count):
        first = self.used
        self.used += count
        return [first + i for i in range(count)]

    def copy(self, slot, seq, source, target, peer):
        index = slot * self.seqs + seq
        return pltpu.make_async_remote_copy(
            src_ref=source,
            dst_ref=target,
            send_sem=self.send.at[index],
            recv_sem=self.recv.at[index],
            device_id={"tensor": peer},
            device_id_type=pl.DeviceIdType.MESH,
        )

    def greet(self):
        barrier = pltpu.get_barrier_semaphore()
        for peer in (self.pair, self.far):
            pl.semaphore_signal(
                barrier, inc=1, device_id={"tensor": peer}, device_id_type=pl.DeviceIdType.MESH
            )
        pl.semaphore_wait(barrier, 2)


class Gather:
    def __init__(self, group, buf, source=None, place=None):
        self.group, self.source = group, source
        self.at = place or (lambda seq, t: buf.at[seq, t])
        self.near, self.over, self.fwd = group.slots(3)

    def own(self, seq):
        return self.at(seq, self.group.me) if self.source is None else self.source.at[seq]

    def near_copy(self, seq):
        g = self.group
        return g.copy(self.near, seq, self.own(seq), self.at(seq, g.me), g.pair)

    def over_copy(self, seq):
        g = self.group
        return g.copy(self.over, seq, self.own(seq), self.at(seq, g.me), g.far)

    def fwd_copy(self, seq):
        g = self.group
        other = self.at(seq, g.far)
        return g.copy(self.fwd, seq, other, other, g.pair)

    def start(self, seq):
        self.over_copy(seq).start()
        self.near_copy(seq).start()

    def forward(self, seq):
        self.over_copy(seq).wait_recv()
        self.fwd_copy(seq).start()

    def finish(self, seq):
        near = self.near_copy(seq)
        fwd = self.fwd_copy(seq)
        near.wait_recv()
        fwd.wait_recv()
        near.wait_send()
        self.over_copy(seq).wait_send()
        fwd.wait_send()


class Scatter:
    def __init__(self, group, stage, got, own, temp):
        self.group, self.stage, self.got, self.held, self.temp = group, stage, got, own, temp
        self.names = group.slots(3)

    def copies(self, seq):
        g = self.group
        peers = (g.pair, g.pair, g.far)
        return [
            g.copy(self.names[i], seq, self.stage(seq, i), self.got(seq, i), peers[i])
            for i in range(3)
        ]

    def start(self, seq, part):
        mine, other, over = self.copies(seq)

        def turn(step, carry):
            part(self.group.block(step), self.temp)

            @pl.when(step == 0)
            def _():
                self.stage(seq, 1)[...] = self.temp[...].astype(BF16)
                other.start()

            @pl.when(step == 1)
            def _():
                other.wait_recv()
                self.stage(seq, 2)[...] = (self.temp[...] + self.got(seq, 1)[...]).astype(BF16)
                over.start()

            @pl.when(step == 2)
            def _():
                self.stage(seq, 0)[...] = self.temp[...].astype(BF16)
                mine.start()

            @pl.when(step == 3)
            def _():
                self.held(seq)[...] = self.temp[...]

            return carry

        lax.fori_loop(0, 4, turn, 0)

    def finish(self, seq):
        mine, other, over = self.copies(seq)
        mine.wait_recv()
        over.wait_recv()
        total = self.held(seq)[...] + self.got(seq, 0)[...] + self.got(seq, 2)[...]
        mine.wait_send()
        other.wait_send()
        over.wait_send()
        return total


def recur(ups, decays, drives, outs, steps, offsets=(0, 0)):
    def rows(tile, step, offset=0):
        row = step if ups[tile] else steps - 1 - step
        return pl.ds(row + offset, CHUNKS, stride=steps)

    zero = jnp.zeros((CHUNKS, LANE), F32)
    one = jnp.ones((CHUNKS, LANE), F32)

    def summary(step, carry):
        new = []
        for tile in range(2):
            state, mult = carry[2 * tile], carry[2 * tile + 1]
            decay = decays[tile, rows(tile, step, offsets[tile]), :]
            new += [decay * state + drives[tile, rows(tile, step), :], decay * mult]
        return tuple(new)

    ends = lax.fori_loop(0, steps, summary, (zero, one, zero, one), unroll=4)
    starts = []
    for tile in range(2):
        final, mult = ends[2 * tile], ends[2 * tile + 1]
        order = range(CHUNKS) if ups[tile] else range(CHUNKS - 1, -1, -1)
        carry = jnp.zeros((1, LANE), F32)
        heads = [None] * CHUNKS
        for chunk in order:
            heads[chunk] = carry
            carry = mult[chunk : chunk + 1] * carry + final[chunk : chunk + 1]
        starts.append(jnp.concatenate(heads, axis=0))

    def write(step, carry):
        new = []
        for tile in range(2):
            here = rows(tile, step)
            decay = decays[tile, rows(tile, step, offsets[tile]), :]
            state = decay * carry[tile] + drives[tile, here, :]
            outs[tile, here, :] = state
            new.append(state)
        return tuple(new)

    lax.fori_loop(0, steps, write, tuple(starts), unroll=4)


def forward_kernel(
    units, channels, tokens, chars, wq, wout, win, wdown, wg, gate_bias, wc, wm, gain, bias, cot_t, cot_c,
    segc, segr, pickc, keep, edges,
    token_out, char_out, o_x, o_c, o_qkv, o_p, o_ctx, o_h, o_act, o_dact, o_mid, o_st, o_mg,
    o_dmg, o_states, o_decay, o_unit0, o_unit1, o_scale, o_res3, o_res4, o_branch, norm_grads,
    x, c, qkv, p, ctx, h, act, dact, mid, st, mg, dmg, states, decays, unit0, unit1, scale, res3, res4, branch,
    hidden, middle, outs_t, outs_c, drive, taps, perm,
    stage, got, held, temp, send, recv, local,
):
    seqs, length = tokens.shape[0], segr.shape[2]
    shard, width = tokens.shape[1], tokens.shape[2]
    block_chars = chars.shape[1]
    heads = p.shape[1] // 4
    g = Group(send, recv, seqs)
    me = g.me
    saves = []

    def keep_out(seq, source, target):
        saves.append((source, target, len(saves)))

    def local_copy(number, seq, source, target):
        return pltpu.make_async_copy(source, target, local.at[number * seqs + seq])

    gx, gc = Gather(g, x, tokens), Gather(g, c, chars)
    gh, gm, gs = Gather(g, h), Gather(g, mid), Gather(g, st)
    narrow = lambda ref: (lambda s, i: ref.at[s, i, :, pl.ds(0, width)])
    wide = lambda ref: (lambda s, i: ref.at[s, i])
    own_n = lambda s: held.at[s, :, pl.ds(0, width)]
    own_w = lambda s: held.at[s]
    thin = temp.at[:, pl.ds(0, width)]
    s_attn = Scatter(g, narrow(stage), narrow(got), own_n, thin)
    s_ffn = Scatter(g, narrow(stage), narrow(got), own_n, thin)
    s_branch = Scatter(g, wide(stage), wide(got), own_w, temp)

    def own_x(seq):
        return local_copy(0, seq, tokens.at[seq], x.at[seq, me])

    def own_c(seq):
        return local_copy(1, seq, chars.at[seq], c.at[seq, me])

    plan = [
        (x, o_x), (c, o_c), (qkv, o_qkv), (p, o_p), (ctx, o_ctx), (h, o_h), (act, o_act),
        (dact, o_dact), (mid, o_mid), (st, o_st), (mg, o_mg), (dmg, o_dmg), (states, o_states),
        (decays, o_decay), (res4, o_res4), (unit0, o_unit0), (unit1, o_unit1), (scale, o_scale), (res3, o_res3), (branch, o_branch),
        (outs_t, token_out), (outs_c, char_out),
    ]

    def save(seq, *names):
        for name in names:
            for number, (source, target) in enumerate(plan):
                if source is name:
                    local_copy(2 + number, seq, source.at[seq], target.at[seq]).start()

    def each(body):
        def run(seq, carry):
            body(seq)
            return carry

        lax.fori_loop(0, seqs, run, 0)

    each(lambda s: (own_x(s).start(), own_c(s).start()))
    g.greet()
    each(gx.start)
    each(gc.start)

    for t in range(4):
        for d in range(2):
            row = lax.broadcasted_iota(jnp.int32, (LANE, width), 0)
            col = lax.broadcasted_iota(jnp.int32, (LANE, width), 1)
            first = d * 4 * units + t * units
            hit = (col - first == row) & (row < units)
            perm[pl.ds((2 * t + d) * LANE, LANE), :] = hit.astype(F32).astype(BF16)
    taps[...] = jnp.zeros_like(taps)
    norm_grads[...] = jnp.zeros_like(norm_grads)

    lane = lax.broadcasted_iota(jnp.int32, (shard, LANE), 1)
    left = lane < HD

    def attention(s):
        gx.forward(s)
        gx.finish(s)
        own_x(s).wait()
        save(s, x)

        def project(t, carry):
            rows = pl.ds(pl.multiple_of(t * shard, shard), shard)
            first, second, third = unpack3(nn(x[s, t], wq[...]), HD * heads)
            qkv[s, 0, rows, :] = (first * 0.125).astype(BF16)
            qkv[s, 1, rows, :] = second.astype(BF16)
            qkv[s, 2, rows, :] = third.astype(BF16)
            return carry

        lax.fori_loop(0, 4, project, 0)
        save(s, qkv)

        def part(b, out):
            rows = pl.ds(pl.multiple_of(b * shard, shard), shard)
            same = segc[s, rows, :] == segr[s]
            for tile in range(qkv.shape[3] // LANE):
                cols = pl.ds(tile * LANE, LANE)
                result = None
                for half in range(2):
                    head = 2 * tile + half
                    if head >= heads:
                        continue
                    query = qkv[s, 0, rows, cols]
                    if 2 * tile + 1 < heads:
                        query = jnp.where(left if half == 0 else ~left, query, jnp.zeros_like(query))
                    scores = jnp.where(same, nt(query, qkv[s, 1, :, cols]), MASK_VALUE)
                    power = jnp.exp(scores - jnp.max(scores, axis=-1, keepdims=True))
                    probs = (power * (1.0 / jnp.sum(power, axis=-1, keepdims=True))).astype(BF16)
                    p[s, head * 4 + b] = probs
                    mixed = nn(probs, qkv[s, 2, :, cols])
                    result = mixed if result is None else jnp.where(left, result, mixed)
                ctx[s, rows, cols] = result.astype(BF16)
            out[...] = nn(ctx[s, rows, :], wout[...])

        s_attn.start(s, part)
        save(s, p, ctx)

    each(attention)

    def first_norm(s):
        total = x[s, me].astype(F32) + s_attn.finish(s)
        unit, spread = normalize(total)
        unit0[s] = unit
        scale[s, 0] = jnp.broadcast_to(spread, (shard, LANE))
        hidden[s] = unit * gain[0:1] + bias[0:1]
        h[s, me] = hidden[s].astype(BF16)
        gh.start(s)
        save(s, unit0)

    def gru(s):
        gc.forward(s)
        gc.finish(s)
        own_c(s).wait()
        save(s, c)

        def gates(t, carry):
            rows = pl.ds(pl.multiple_of(t * LANE, LANE), LANE)
            per = block_chars // LANE
            inner = pl.ds(pl.multiple_of((t % per) * LANE, LANE), LANE)
            proj = nn(c[s, t // per, inner, :], wg[...])
            for tile in range(2):
                cols = slice(tile * LANE, (tile + 1) * LANE)
                gate = jax.nn.sigmoid(proj[:, cols] + gate_bias_pad(tile))
                cand = proj[:, (2 + tile) * LANE : (3 + tile) * LANE]
                decays[s, tile, rows, :] = (1.0 - gate) * keep[s, rows, tile : tile + 1]
                drive[tile, rows, :] = gate * cand
            return carry

        def gate_bias_pad(tile):
            return gate_bias[:, tile * LANE : (tile + 1) * LANE]

        total = 4 * block_chars
        lax.fori_loop(0, total // LANE, gates, 0)
        recur((True, False), decays.at[s], drive, states.at[s], total // CHUNKS)
        save(s, decays)

        def pick(t, carry):
            rows = pl.ds(pl.multiple_of(t * shard, shard), shard)
            for tile in range(2):
                ids = lax.broadcasted_iota(jnp.int32, (shard, total), 1)
                hot = (ids == pickc[s, rows, tile : tile + 1]).astype(F32).astype(BF16)
                out = nn(hot, states[s, tile].astype(BF16))
                st[s, me, rows, pl.ds(tile * LANE, LANE)] = out.astype(BF16)
            return carry

        lax.fori_loop(0, 4, pick, 0)
        gs.start(s)
        save(s, states)

    def norm_and_gru(s):
        first_norm(s)
        gru(s)

    each(norm_and_gru)

    def ffn(s):
        gh.forward(s)
        gh.finish(s)
        save(s, h)

        def part(b, out):
            value, slope = gelu_pair(nn(h[s, b], win[...]))
            act[s, b] = value.astype(BF16)
            dact[s, b] = slope.astype(BF16)
            out[...] = nn(act[s, b], wdown[...])

        s_ffn.start(s, part)
        save(s, act, dact)

    each(ffn)

    def second_norm(s):
        unit, spread = normalize(hidden[s] + s_ffn.finish(s))
        unit1[s] = unit
        scale[s, 1] = jnp.broadcast_to(spread, (shard, LANE))
        middle[s] = unit * gain[1:2] + bias[1:2]
        mid[s, me] = middle[s].astype(BF16)
        gm.start(s)
        save(s, unit1, scale)

    each(second_norm)

    def merge(s):
        gs.forward(s)
        gm.forward(s)
        gs.finish(s)
        gm.finish(s)
        save(s, mid, st)
        def mix(t, carry):
            rows = pl.ds(pl.multiple_of(t * shard, shard), shard)
            total = nn(mid[s, t], wc[pl.ds(0, width), :])
            for u in range(4):
                weights = wc[pl.ds(width + u * 2 * LANE, 2 * LANE), :]
                total = total + nn(st[s, u, rows, :], weights)
            taps[pl.ds(pl.multiple_of(8 + t * shard, 8), shard), :] = total
            return carry

        lax.fori_loop(0, 4, mix, 0)

        def shifted(t, carry):
            rows = pl.ds(pl.multiple_of(t * shard, shard), shard)
            window = taps[pl.ds(pl.multiple_of(t * shard, 8), shard + 16), :]
            before = unpack3(window[7 : 7 + shard], channels)[0]
            center = unpack3(window[8 : 8 + shard], channels)[1]
            after = unpack3(window[9 : 9 + shard], channels)[2]
            value, slope = gelu_pair(
                before * edges[s, rows, 0:1] + center + after * edges[s, rows, 1:2]
            )
            mg[s, rows, :] = value.astype(BF16)
            dmg[s, rows, :] = slope.astype(BF16)
            return carry

        lax.fori_loop(0, 4, shifted, 0)

        def part(b, out):
            rows = pl.ds(pl.multiple_of(b * shard, shard), shard)
            out[...] = nn(mg[s, rows, :], wm[...])

        s_branch.start(s, part)
        save(s, mg, dmg)

    each(merge)

    def put_branch(s, first, value):
        span = branch.shape[3]
        at = 0
        while at < width:
            part, inner = divmod(first + at, span)
            size = min(span - inner, width - at)
            branch[s, part, :, pl.ds(inner, size)] = value[:, at : at + size]
            at += size

    def last_norms(s):
        total = s_branch.finish(s)
        rows = pl.ds(pl.multiple_of(me * shard, shard), shard)
        unit, spread = normalize(middle[s] + total[:, :width])
        outs_t[s] = (unit * gain[2:3] + bias[2:3]).astype(BF16)
        cot = cot_t[s]
        norm_grads[0:1] += jnp.sum(cot * unit, axis=0, keepdims=True)
        norm_grads[2:3] += jnp.sum(cot, axis=0, keepdims=True)
        back = normalize_back(unit, spread, cot * gain[2:3])
        res3[s] = back
        put_branch(s, 0, back.astype(BF16))
        mine = total[:, width:]
        for u in range(4):
            mine = mine + nn(st[s, u, rows, :], perm[pl.ds(u * 2 * LANE, 2 * LANE), :])
        unit, spread = normalize(mine)
        outs_c[s] = (unit * gain[3:4] + bias[3:4]).astype(BF16)
        cot = cot_c[s]
        norm_grads[1:2] += jnp.sum(cot * unit, axis=0, keepdims=True)
        norm_grads[3:4] += jnp.sum(cot, axis=0, keepdims=True)
        back = normalize_back(unit, spread, cot * gain[3:4]).astype(BF16)
        put_branch(s, width, back)
        for u in range(4):
            res4[s, u] = nt(back, perm[pl.ds(u * 2 * LANE, 2 * LANE), :]).astype(BF16)
        save(s, outs_t, outs_c, res3, res4, branch)

    each(last_norms)

    def drain(s):
        for number, (source, target) in enumerate(plan):
            local_copy(2 + number, s, source.at[s], target.at[s]).wait()

    each(drain)


def forward_call(tokens, chars, weights, small, group_slots=27):
    seqs, shard, width = tokens.shape
    length, block_chars = shard * 4, chars.shape[1]
    total = block_chars * 4
    wq, wout, win, wdown, wg, gate_bias, wc, wm = weights
    cols = wout.shape[0]
    heads = small["heads"]
    sds = jax.ShapeDtypeStruct
    big = {
        "x": ((seqs, 4, shard, width), BF16),
        "c": ((seqs, 4, block_chars, chars.shape[2]), BF16),
        "qkv": ((seqs, 3, length, cols), BF16),
        "p": ((seqs, heads * 4, shard, length), BF16),
        "ctx": ((seqs, length, cols), BF16),
        "h": ((seqs, 4, shard, width), BF16),
        "act": ((seqs, 4, shard, win.shape[1]), BF16),
        "dact": ((seqs, 4, shard, win.shape[1]), BF16),
        "mid": ((seqs, 4, shard, width), BF16),
        "st": ((seqs, 4, length, 2 * LANE), BF16),
        "mg": ((seqs, length, wm.shape[0]), BF16),
        "dmg": ((seqs, length, wm.shape[0]), BF16),
        "states": ((seqs, 2, total, LANE), F32),
        "decay": ((seqs, 2, total, LANE), F32),
        "unit0": ((seqs, shard, width), F32),
        "unit1": ((seqs, shard, width), F32),
        "scale": ((seqs, 2, shard, LANE), F32),
        "res3": ((seqs, shard, width), F32),
        "res4": ((seqs, 4, shard, 2 * LANE), BF16),
        "branch": ((seqs, 2 * width // length, shard, length), BF16),
    }
    rows = ((seqs, shard, width), F32)
    low_rows = ((seqs, shard, width), BF16)
    scratch = list(big.values()) + [
        rows, rows, low_rows, low_rows,
        ((2, total, LANE), F32),
        ((length + 16, wc.shape[1]), F32),
        ((8 * LANE, width), BF16),
        ((seqs, 3, shard, 2 * width), BF16), ((seqs, 3, shard, 2 * width), BF16),
        ((seqs, shard, 2 * width), F32), ((shard, 2 * width), F32),
    ]
    anyspace = pl.BlockSpec(memory_space=pl.ANY)
    vmem = pl.BlockSpec(memory_space=pltpu.VMEM)
    out_shapes = [sds(low_rows[0], BF16)] * 2 + [sds(*v) for v in big.values()]
    ins = (
        tokens, chars, wq, wout, win, wdown, wg, gate_bias, wc, wm, small["gain"], small["bias"],
        small["cot_t"], small["cot_c"], small["segc"], small["segr"], small["pickc"],
        small["keep"], small["edges"],
    )
    outs = pl.pallas_call(
        functools.partial(forward_kernel, small["units"], small["channels"]),
        out_shape=out_shapes + [sds((4, width), F32)],
        in_specs=[anyspace] * 2 + [vmem] * (len(ins) - 2),
        out_specs=[anyspace] * len(out_shapes) + [vmem],
        scratch_shapes=[pltpu.VMEM(*v) for v in scratch]
        + [
            pltpu.SemaphoreType.DMA((group_slots * seqs,)),
            pltpu.SemaphoreType.DMA((group_slots * seqs,)),
            pltpu.SemaphoreType.DMA((26 * seqs,)),
        ],
        compiler_params=pltpu.CompilerParams(
            collective_id=0, has_side_effects=True, vmem_limit_bytes=62 * MIB
        ),
    )(*ins)
    names = ["token_out", "char_out"] + list(big) + ["norm_grads"]
    return dict(zip(names, outs))


class Reduce:
    def __init__(self, net, buf, out, first, land, land_first, rows, order):
        self.net, self.buf, self.out, self.land, self.order = net, buf, out, land, order
        self.first, self.land_first, self.rows = first, land_first, rows
        self.slots = net.take(2 * len(order))
        self.mark = net.mark()

    def start_of(self, level):
        start = self.first
        for i in range(level):
            start = start + self.net.bit(self.order[i]) * (self.rows >> (i + 1))
        return start

    def half(self, level):
        return self.rows >> (level + 1)

    def view(self, start, size, ref=None):
        ref = self.buf if ref is None else ref
        return ref.at[pl.ds(pl.multiple_of(start, 16), size), :]

    def keep(self):
        levels = len(self.order)
        start, size = self.start_of(levels), self.rows >> levels
        return pltpu.make_async_copy(
            self.view(start, size), self.view(start, size, self.out), self.mark
        )

    def landing(self, level):
        start = self.land_first + self.rows - (self.rows >> level)
        return self.land.at[pl.ds(start, self.half(level)), :]

    def down(self, level):
        bit = self.net.bit(self.order[level])
        other = self.start_of(level) + (1 - bit) * self.half(level)
        return self.net.copy(
            self.slots[level],
            self.view(other, self.half(level)),
            self.landing(level),
            self.order[level],
        )

    def up(self, level):
        start, size = self.start_of(level + 1), self.half(level)
        target = self.view(start, size, self.out)
        source = self.view(start, size) if level == len(self.order) - 1 else target
        return self.net.copy(
            self.slots[len(self.order) + level], source, target, self.order[level]
        )

    def step(self, number):
        levels = len(self.order)
        if 0 < number <= levels:
            level = number - 1
            self.down(level).wait()
            start = self.start_of(level + 1)
            start_land = self.land_first + self.rows - (self.rows >> level)

            def add(i, carry):
                rows = pl.ds(pl.multiple_of(start + i * 16, 16), 16)
                more = pl.ds(pl.multiple_of(start_land + i * 16, 16), 16)
                total = self.buf[rows, :].astype(F32) + self.land[more, :].astype(F32)
                self.buf[rows, :] = total.astype(BF16)
                return carry

            lax.fori_loop(0, self.half(level) // 16, add, 0)
            if number == levels:
                self.keep().start()
        elif number > levels:
            self.up(2 * levels - number).wait()
            if number == levels + 1:
                self.keep().wait()
        if number < levels:
            self.down(number).start()
        elif number < 2 * levels:
            self.up(2 * levels - 1 - number).start()


class Plane:
    def __init__(self, send, recv, marks):
        self.index = lax.axis_index("dp")
        self.send, self.recv, self.marks, self.used, self.marked = send, recv, marks, 0, 0

    def mark(self):
        self.marked += 1
        return self.marks.at[self.marked - 1]

    def bit(self, number):
        return (self.index // (1 << number)) % 2

    def peer(self, number):
        return self.index + (1 - 2 * self.bit(number)) * (1 << number)

    def take(self, count):
        first = self.used
        self.used += count
        return [first + i for i in range(count)]

    def copy(self, slot, source, target, number):
        return pltpu.make_async_remote_copy(
            src_ref=source,
            dst_ref=target,
            send_sem=self.send.at[slot],
            recv_sem=self.recv.at[slot],
            device_id={"dp": self.peer(number)},
            device_id_type=pl.DeviceIdType.MESH,
        )


SAVED = (
    "branch", "mg", "dmg", "mid", "st", "res3", "res4", "unit0", "unit1", "scale", "act", "dact",
    "h", "p", "qkv", "ctx", "x", "c", "states", "decay",
)
GRADS = ("merge", "conv", "down", "in", "gru", "out", "qkv")


def backward_kernel(units, channels, dp_size, *refs):
    refs = list(refs)
    take = lambda count: [refs.pop(0) for _ in range(count)]
    hbm = dict(zip(SAVED, take(len(SAVED))))
    wq, wout, win, wdown, wg, gate_bias, wc, wm, gain, pickr, edges, norm_in = take(12)
    grad_tokens, grad_chars = take(2)
    grads_out = dict(zip(GRADS, take(len(GRADS))))
    (small_out,) = take(1)
    names = [n for n in SAVED if n not in ("branch", "states", "decay", "p", "x")]
    v = dict(zip(names, take(len(names))))
    (pb, states, decay, drive, dpre, dyk, fg, gtok, dproj, gru_acc, res2, res1, ds, parts,
     stage, got, held, temp, cstage, cgot, cheld, ctemp) = take(22)
    land = dict(zip(GRADS, take(len(GRADS))))
    big = dict(zip(GRADS, take(len(GRADS))))
    small, small_land, send, recv, dsend, drecv, local, marks = take(8)

    seqs, shard, width = grad_tokens.shape
    length = 4 * shard
    block_chars = grad_chars.shape[1]
    total = 4 * block_chars
    heads = pb.shape[1] // 4
    cols = v["ctx"].shape[2]
    g = Group(send, recv, seqs)
    me = g.me
    inside = dp_size == 8
    plane = Plane(dsend, drecv, marks)

    def each(body):
        def run(seq, carry):
            body(seq)
            return carry

        lax.fori_loop(0, seqs, run, 0)

    def load(name):
        index = names.index(name)
        return pltpu.make_async_copy(hbm[name], v[name], local.at[index])

    spare = len(names)
    p_copy = lambda: pltpu.make_async_copy(hbm["p"], pb, local.at[spare])
    x_copy = lambda: pltpu.make_async_copy(hbm["x"], v["h"], local.at[39])

    def states_copy(s):
        return pltpu.make_async_copy(hbm["states"].at[s], states, local.at[spare + 1])

    def decay_copy(s, tile):
        return pltpu.make_async_copy(
            hbm["decay"].at[s, tile], decay.at[tile, pl.ds(8, total), :], local.at[spare + 2 + tile]
        )

    def out_copy(kind, s):
        source, target = ((res1, grad_tokens), (cheld, grad_chars))[kind]
        return pltpu.make_async_copy(
            source.at[s], target.at[s], local.at[spare + 4 + kind * seqs + s]
        )

    pieces = 2 * width // length
    gb = Gather(
        g, pb, hbm["branch"], place=lambda s, t: pb.at[s, pl.ds(t * pieces, pieces)]
    )
    gf, ga = Gather(g, fg), Gather(g, v["mid"])
    pick = lambda ref: (lambda s, i: ref.at[s, i])
    own = lambda ref: (lambda s: ref.at[s])
    s_mid = Scatter(g, pick(stage), pick(got), own(held), temp)
    s_hid = Scatter(g, pick(stage), pick(got), own(held), temp)
    s_tok = Scatter(g, pick(stage), pick(got), own(held), temp)
    s_chr = Scatter(g, pick(cstage), pick(cgot), own(cheld), ctemp)
    s_cout = Scatter(g, pick(cstage), pick(cgot), own(cheld), ctemp)

    def own_branch(s):
        return pltpu.make_async_copy(
            hbm["branch"].at[s], gb.at(s, me), local.at[spare + 4 + 2 * seqs + s]
        )

    each(lambda s: own_branch(s).start())
    for name in ("dmg", "res4", "mg", "mid", "st"):
        load(name).start()
    states_copy(0).start()
    for tile in range(2):
        decay_copy(0, tile).start()
    for name in names:
        if name not in ("dmg", "res4", "mg", "mid", "st"):
            load(name).start()

    barrier = pltpu.get_barrier_semaphore()
    places = [{"tensor": g.pair}, {"tensor": g.far}]
    if inside:
        places += [{"dp": plane.peer(k)} for k in range(3)]
    for place in places:
        pl.semaphore_signal(barrier, inc=1, device_id=place, device_id_type=pl.DeviceIdType.MESH)
    pl.semaphore_wait(barrier, len(places))
    each(gb.start)
    dpre[...] = jnp.zeros_like(dpre)
    for tile in range(2):
        decay[tile, pl.ds(0, 8), :] = jnp.zeros((8, LANE), F32)
        decay[tile, pl.ds(total + 8, 8), :] = jnp.zeros((8, LANE), F32)
    small[...] = jnp.zeros_like(small)
    small[0, pl.ds(0, 4), :] = norm_in[...]
    lane = lax.broadcasted_iota(jnp.int32, (shard, LANE), 1)
    left = lane < HD
    for name in ("dmg", "res4"):
        load(name).wait()

    def block_rows(t, size):
        return pl.ds(pl.multiple_of(t * size, size), size)

    def merge_back(s):
        gb.forward(s)
        gb.finish(s)
        own_branch(s).wait()

        def inner(t, carry):
            rows = block_rows(t, shard)
            back = None
            for j in range(pieces):
                piece = nt(pb[s, t * pieces + j], wm[:, j * length : (j + 1) * length])
                back = piece if back is None else back + piece
            dpre[pl.ds(pl.multiple_of(8 + t * shard, 8), shard), :] = (
                (back * v["dmg"][s, rows, :].astype(F32)).astype(BF16).astype(F32)
            )
            return carry

        lax.fori_loop(0, 4, inner, 0)

        def taps(t, carry):
            rows = block_rows(t, shard)
            window = dpre[pl.ds(pl.multiple_of(t * shard, 8), shard + 16), :]
            marks = edges[s, rows, :]
            before = window[9 : 9 + shard] * marks[:, 2:3]
            after = window[7 : 7 + shard] * marks[:, 3:4]
            dyk[s, rows, :] = pack3(
                [before, window[8 : 8 + shard], after], channels
            ).astype(BF16)
            return carry

        lax.fori_loop(0, 4, taps, 0)

        def mid_part(b, out):
            out[...] = nt(dyk[s, block_rows(b, shard), :], wc[pl.ds(0, width), :])

        s_mid.start(s, mid_part)

        def char_part(b, out):
            first = pl.multiple_of(width + b * 2 * LANE, 2 * LANE)
            out[...] = nt(dyk[s], wc[pl.ds(first, 2 * LANE), :])
            out[block_rows(me, shard), :] += v["res4"][s, b].astype(F32)

        s_chr.start(s, char_part)

    each(merge_back)
    for name in ("mg", "mid", "st"):
        load(name).wait()

    tokens = seqs * length
    half_w = width
    for j in range(pieces):
        right = jnp.concatenate(
            [pb[s, t * pieces + j] for s in range(seqs) for t in range(4)], axis=0
        )
        out = tn(v["mg"][...].reshape(tokens, -1), right)[:channels].astype(BF16)
        at = 0
        while at < length:
            part, inside_at = divmod(j * length + at, half_w)
            size = min(length - at, half_w - inside_at)
            big["merge"][pl.ds(part * channels, channels), pl.ds(inside_at, size)] = out[
                :, at : at + size
            ]
            at += size
    step_w = 2 * LANE

    def conv_mid(j, carry):
        colsj = pl.ds(pl.multiple_of(j * step_w, step_w), step_w)
        out = tn(v["mid"][:, :, :, colsj].reshape(tokens, step_w), dyk[...].reshape(tokens, -1))
        big["conv"][block_rows(j, step_w), :] = out.astype(BF16)
        return carry

    lax.fori_loop(0, width // step_w, conv_mid, 0)

    def conv_char(t, carry):
        out = tn(v["st"][:, t].reshape(tokens, 2 * LANE), dyk[...].reshape(tokens, -1))
        for d in range(2):
            first = pl.multiple_of(width + d * 4 * units + t * units, 16)
            big["conv"][pl.ds(first, units), :] = out[d * LANE : d * LANE + units].astype(BF16)
        return carry

    lax.fori_loop(0, 4, conv_char, 0)
    p_copy().start()

    near, along = (0, 1, 2), (1, 2, 0)

    def split(name, head):
        rows = big[name].shape[0]
        result = []
        if head:
            result.append(
                Reduce(plane, big[name], grads_out[name], 0, land[name], 0, head, near)
            )
        if rows > head:
            result.append(
                Reduce(
                    plane, big[name], grads_out[name], head, land[name], head * 7 // 8,
                    rows - head, along,
                )
            )
        return result

    if inside:
        first_sums = split("conv", 1024) + split("merge", 0)
        second_sums = split("down", big["down"].shape[0]) + split("in", 256)
        third_sums = split("qkv", 512) + split("out", 0) + split("gru", big["gru"].shape[0])
    else:
        first_sums, second_sums, third_sums = [], [], []

    def advance(sums, number):
        for one in sums:
            one.step(number)

    advance(first_sums, 0)

    def second_back(s):
        incoming = v["res3"][s] + s_mid.finish(s)
        unit = v["unit1"][s]
        small[0, 5:6] += jnp.sum(incoming * unit, axis=0, keepdims=True)
        small[0, 7:8] += jnp.sum(incoming, axis=0, keepdims=True)
        spread = v["scale"][s, 1][:, 0:1]
        res2[s] = normalize_back(unit, spread, incoming * gain[1:2])
        fg[s, me] = res2[s].astype(BF16)
        gtok[s] = s_chr.finish(s).astype(BF16)
        gf.start(s)

    for name in ("res3", "unit1", "scale"):
        load(name).wait()
    each(second_back)
    load("c").wait()

    def gru_back(s):
        def spread_out(t, carry):
            rows = block_rows(t, LANE)
            for tile in range(2):
                ids = lax.broadcasted_iota(jnp.int32, (LANE, length), 0) + t * LANE
                hot = (ids == pickr[s, tile : tile + 1, :]).astype(F32).astype(BF16)
                drive[tile, rows, :] = nn(hot, gtok[s, :, pl.ds(tile * LANE, LANE)])
            return carry

        lax.fori_loop(0, total // LANE, spread_out, 0)
        for tile in range(2):
            decay_copy(s, tile).wait()
        recur((False, True), decay, drive, drive, total // CHUNKS, (9, 7))
        states_copy(s).wait()

        def finish(t, sums):
            rows = block_rows(t, LANE)
            per = block_chars // LANE
            inner = block_rows(t % per, LANE)
            proj = nn(v["c"][s, t // per, inner, :], wg[...])
            new = []
            for tile in range(2):
                colst = slice(tile * LANE, (tile + 1) * LANE)
                gate = jax.nn.sigmoid(proj[:, colst] + gate_bias[:, colst])
                cand = proj[:, (2 + tile) * LANE : (3 + tile) * LANE]
                flow = drive[tile, rows, :] * gate
                logit = flow * (cand - states[tile, rows, :])
                dproj[rows, pl.ds(tile * LANE, LANE)] = logit.astype(BF16)
                dproj[rows, pl.ds((2 + tile) * LANE, LANE)] = flow.astype(BF16)
                new.append(sums[tile] + jnp.sum(logit, axis=0, keepdims=True))
            return tuple(new)

        zero = jnp.zeros((1, LANE), F32)
        sums = lax.fori_loop(0, total // LANE, finish, (zero, zero))
        for tile in range(2):
            small[0, 8:9, pl.ds(tile * LANE, LANE)] += sums[tile]

        @pl.when(s + 1 < seqs)
        def _():
            states_copy(s + 1).start()
            for tile in range(2):
                decay_copy(s + 1, tile).start()

        def part(b, out):
            out[...] = nt(dproj[block_rows(b, block_chars), :], wg[...])

        gf.forward(s)
        gf.finish(s)
        s_cout.start(s, part)
        grad = tn(v["c"][s].reshape(total, -1), dproj[...])

        @pl.when(s == 0)
        def _():
            gru_acc[...] = grad

        @pl.when(s > 0)
        def _():
            gru_acc[...] += grad

    each(gru_back)
    big["gru"][...] = gru_acc[...].astype(BF16)
    advance(first_sums, 1)
    for name in ("dact", "act", "h"):
        load(name).wait()

    def ffn_back(s):
        def part(b, out):
            back = nt(fg[s, b], wdown[...]) * v["dact"][s, b].astype(F32)
            v["dact"][s, b] = back.astype(BF16)
            out[...] = nt(v["dact"][s, b], win[...])

        s_hid.start(s, part)

    each(ffn_back)
    advance(first_sums, 2)

    def ffn_weights(j, carry):
        colsj = pl.ds(pl.multiple_of(j * step_w, step_w), step_w)
        out = tn(v["act"][:, :, :, colsj].reshape(tokens, step_w), fg[...].reshape(tokens, width))
        big["down"][block_rows(j, step_w), :] = out.astype(BF16)
        return carry

    lax.fori_loop(0, big["down"].shape[0] // step_w, ffn_weights, 0)

    def in_weights(j, carry):
        colsj = pl.ds(pl.multiple_of(j * step_w, step_w), step_w)
        out = tn(
            v["h"][:, :, :, colsj].reshape(tokens, step_w), v["dact"][...].reshape(tokens, -1)
        )
        big["in"][block_rows(j, step_w), :] = out.astype(BF16)
        return carry

    lax.fori_loop(0, width // step_w, in_weights, 0)
    x_copy().start()
    advance(second_sums, 0)
    load("unit0").wait()

    def first_back(s):
        incoming = res2[s] + s_hid.finish(s)
        unit = v["unit0"][s]
        small[0, 4:5] += jnp.sum(incoming * unit, axis=0, keepdims=True)
        small[0, 6:7] += jnp.sum(incoming, axis=0, keepdims=True)
        spread = v["scale"][s, 0][:, 0:1]
        res1[s] = normalize_back(unit, spread, incoming * gain[0:1])
        v["mid"][s, me] = res1[s].astype(BF16)
        ga.start(s)

    each(first_back)
    hops = [("t", g.pair), ("t", g.far)] + ([("d", k) for k in range(3)] if inside else [])
    slots_t, slots_d = g.slots(2), plane.take(3)

    def small_copy(number):
        kind, where = hops[number]
        source, target = small.at[number], small_land.at[number]
        if kind == "t":
            return g.copy(slots_t[number], 0, source, target, where)
        return plane.copy(slots_d[where], source, target, where)

    def small_step(number):
        if number > 0:
            small_copy(number - 1).wait()
            keep_rows = 8 if number <= 2 else 16
            value, more = small[number - 1], small_land[number - 1]
            small[number, pl.ds(0, 8), :] = value[:8] + more[:8]
            small[number, pl.ds(8, 8), :] = value[8:] if number <= 2 else value[8:] + more[8:]
        if number < len(hops):
            small_copy(number).start()

    if not inside:
        hops = []
    small_step(0) if hops else None
    advance(first_sums, 3)
    for name in ("qkv", "ctx"):
        load(name).wait()
    p_copy().wait()

    def attention_back(s):
        ga.forward(s)
        ga.finish(s)
        dctx = v["dmg"]

        def context(t, carry):
            dctx[s, block_rows(t, shard), :] = nt(v["mid"][s, t], wout[...]).astype(BF16)
            return carry

        lax.fori_loop(0, 4, context, 0)
        for tile in range(cols // LANE):
            lanes = pl.ds(tile * LANE, LANE)
            for half in range(2):
                head = 2 * tile + half
                if head >= heads:
                    continue
                paired = 2 * tile + 1 < heads

                def rows_of(b, carry):
                    rows = block_rows(b, shard)
                    grad = dctx[s, rows, lanes]
                    if paired:
                        grad = jnp.where(left if half == 0 else ~left, grad, jnp.zeros_like(grad))
                    back = nt(grad, v["qkv"][s, 2, :, lanes])
                    probs = pb[s, head * 4 + b].astype(F32)
                    row_dot = jnp.sum(probs * back, axis=-1, keepdims=True)
                    ds[b] = (probs * (back - row_dot)).astype(BF16)
                    out = nn(ds[b], v["qkv"][s, 1, :, lanes])
                    if half == 1:
                        out = jnp.where(left, ctemp[rows, lanes], out)
                    ctemp[rows, lanes] = out
                    return carry

                lax.fori_loop(0, 4, rows_of, 0)
                keys = tn(ds[...].reshape(length, length), v["qkv"][s, 0, :, lanes])
                values = tn(
                    pb[s, pl.ds(head * 4, 4)].reshape(length, length), dctx[s, :, lanes]
                )
                if half == 1:
                    wide_left = lax.broadcasted_iota(jnp.int32, (length, LANE), 1) < HD
                    keys = jnp.where(wide_left, parts[0, :, lanes], keys)
                    values = jnp.where(wide_left, parts[1, :, lanes], values)
                parts[0, :, lanes] = keys
                parts[1, :, lanes] = values

        def pack(t, carry):
            rows = block_rows(t, shard)
            query = ctemp[rows, :].astype(BF16).astype(F32) * 0.125
            dyk[s, rows, :] = pack3(
                [query, parts[0, rows, :], parts[1, rows, :]], HD * heads
            ).astype(BF16)
            return carry

        lax.fori_loop(0, 4, pack, 0)

        def part(b, out):
            out[...] = nt(dyk[s, block_rows(b, shard), :], wq[...])

        s_tok.start(s, part)

    each(attention_back)
    advance(first_sums, 4)
    advance(second_sums, 1)

    x_copy().wait()

    def qkv_weights(j, carry):
        colsj = pl.ds(pl.multiple_of(j * step_w, step_w), step_w)
        out = tn(v["h"][:, :, :, colsj].reshape(tokens, step_w), dyk[...].reshape(tokens, -1))
        big["qkv"][block_rows(j, step_w), :] = out.astype(BF16)
        return carry

    lax.fori_loop(0, width // step_w, qkv_weights, 0)
    big["out"][...] = tn(
        v["ctx"][...].reshape(tokens, -1), v["mid"][...].reshape(tokens, width)
    ).astype(BF16)
    advance(third_sums, 0)
    if hops:
        small_step(1)

    def last(s):
        res1[s] = res1[s] + s_tok.finish(s)
        out_copy(0, s).start()
        cheld[s] = s_cout.finish(s)
        out_copy(1, s).start()

    each(last)

    def emit(name):
        return pltpu.make_async_copy(
            big[name], grads_out[name], local.at[spare + 4 + 3 * seqs + GRADS.index(name)]
        )

    if inside:
        small_step(2)
        advance(second_sums, 2)
        advance(first_sums, 5)
        advance(third_sums, 1)
        small_step(3)
        advance(second_sums, 3)
        advance(third_sums, 2)
        advance(first_sums, 6)
        small_step(4)
        advance(second_sums, 4)
        advance(third_sums, 3)
        small_step(5)
        advance(second_sums, 5)
        advance(third_sums, 4)
        advance(second_sums, 6)
        advance(third_sums, 5)
        advance(third_sums, 6)
    else:
        for name in GRADS:
            emit(name).start()
        for name in GRADS:
            emit(name).wait()
    small_out[...] = small[len(hops)]
    each(lambda s: (out_copy(0, s).wait(), out_copy(1, s).wait()))


def backward_call(saved, weights, small, dp_size):
    wq, wout, win, wdown, wg, gate_bias, wc, wm = weights
    sds = jax.ShapeDtypeStruct
    seqs, shard, width = saved["res3"].shape
    length = shard * 4
    block_chars, char_width = saved["c"].shape[2:]
    total = 4 * block_chars
    cols, packed = wout.shape[0], wc.shape[1]
    channels = small["channels"]
    saved_in = [saved[n] for n in SAVED]
    names = [n for n in SAVED if n not in ("branch", "states", "decay", "p", "x")]
    shapes = [(saved[n].shape, saved[n].dtype) for n in names]
    grads = {
        "merge": (2 * channels, width), "conv": (2 * width, packed),
        "down": (win.shape[1], width), "in": (width, win.shape[1]),
        "gru": (char_width, 4 * LANE), "out": (cols, width), "qkv": (width, wq.shape[1]),
    }
    pad = (seqs, 3, shard, width)
    cpad = (seqs, 3, length, 2 * LANE)
    scratch = shapes + [
        (saved["p"].shape, BF16),
        ((2, total, LANE), F32),
        ((2, total + 16, LANE), F32),
        ((2, total, LANE), F32),
        ((length + 16, wm.shape[0]), F32),
        ((seqs, length, packed), BF16),
        ((seqs, 4, shard, width), BF16),
        ((seqs, length, 2 * LANE), BF16),
        ((total, 4 * LANE), BF16),
        ((char_width, 4 * LANE), F32),
        ((seqs, shard, width), F32),
        ((seqs, shard, width), F32),
        ((4, shard, length), BF16),
        ((2, length, cols), F32),
        (pad, BF16), (pad, BF16), ((seqs, shard, width), F32), ((shard, width), F32),
        (cpad, BF16), (cpad, BF16), ((seqs, length, 2 * LANE), F32), ((length, 2 * LANE), F32),
    ]
    scratch += [((rows * 7 // 8 if dp_size == 8 else 16, last), BF16) for rows, last in grads.values()]
    scratch += [(shape, BF16) for shape in grads.values()]
    scratch += [((6, 16, width), F32), ((6, 16, width), F32)]
    anyspace = pl.BlockSpec(memory_space=pl.ANY)
    vmem = pl.BlockSpec(memory_space=pltpu.VMEM)
    ins = saved_in + list(weights) + [small["gain"], small["pickr"], small["edges"], saved["norm_grads"]]
    outs = pl.pallas_call(
        functools.partial(backward_kernel, small["units"], channels, dp_size),
        out_shape=[sds((seqs, shard, width), F32), sds((seqs, block_chars, char_width), F32)]
        + [sds(shape, BF16) for shape in grads.values()]
        + [sds((16, width), F32)],
        in_specs=[anyspace] * len(saved_in) + [vmem] * (len(ins) - len(saved_in)),
        out_specs=[anyspace] * (2 + len(grads)) + [vmem],
        scratch_shapes=[pltpu.VMEM(*one) for one in scratch]
        + [
            pltpu.SemaphoreType.DMA((32 * seqs,)),
            pltpu.SemaphoreType.DMA((32 * seqs,)),
            pltpu.SemaphoreType.DMA((72,)),
            pltpu.SemaphoreType.DMA((72,)),
            pltpu.SemaphoreType.DMA((40,)),
            pltpu.SemaphoreType.DMA((12,)),
        ],
        compiler_params=pltpu.CompilerParams(
            collective_id=1, has_side_effects=True, vmem_limit_bytes=63 * MIB
        ),
    )(*ins)
    names = ["grad_tokens", "grad_chars"] + list(grads) + ["small"]
    return dict(zip(names, outs))


def local(
    tokens,
    characters,
    doc_lengths,
    token_chars,
    w_qkv,
    w_out,
    w_in,
    w_down,
    w_gru,
    gate_bias,
    w_conv,
    w_merge,
    norm_gain,
    norm_bias,
    token_cot,
    char_cot,
):
    micro_count = tokens.shape[0]
    shard_len = tokens.shape[1]
    model_width = tokens.shape[2]
    char_width = characters.shape[2]
    group_size = lax.axis_size("tensor")
    group_rank = lax.axis_index("tensor")
    length = shard_len * group_size
    char_total = characters.shape[1] * group_size
    head_cols = w_qkv.shape[2]
    heads_here = head_cols // HD
    units_here = w_gru.shape[3]
    merge_here = w_conv.shape[2]
    gru_matrix, gru_bias = gru_weights(w_gru, gate_bias)
    spare = -head_cols % LANE
    more = -merge_here % LANE
    wq = jnp.pad(
        w_qkv.reshape(model_width, 3 * head_cols), ((0, 0), (0, -3 * head_cols % LANE))
    )
    wout = jnp.pad(w_out, ((0, spare), (0, 0)))
    wm = jnp.pad(w_merge.reshape(merge_here, 2 * model_width), ((0, more), (0, 0)))
    conv = jnp.swapaxes(w_conv, 0, 1).reshape(2 * model_width, 3 * merge_here)
    conv = jnp.pad(conv, ((0, 0), (0, -3 * merge_here % LANE)))
    conv_char = conv[model_width:].reshape(2, group_size, units_here, -1)
    conv_char = jnp.pad(
        jnp.swapaxes(conv_char, 0, 1), ((0, 0), (0, 0), (0, LANE - units_here), (0, 0))
    )
    wc = jnp.concatenate(
        [conv[:model_width], conv_char.reshape(group_size * 2 * LANE, -1)], axis=0
    )
    layouts = [layout(doc_lengths[i], token_chars[i], char_total) for i in range(micro_count)]
    stacked_layout = [jnp.stack(parts) for parts in zip(*layouts)]
    segment, first_char, last_char, keep_forward, keep_backward, prev_ok, next_ok = stacked_layout
    keep = jnp.stack([keep_forward, keep_backward], axis=2)
    picks = jnp.stack([last_char, first_char], axis=2)
    zero = jnp.zeros_like(prev_ok[:, :1])
    small = dict(
        gain=norm_gain, bias=norm_bias, cot_t=token_cot, cot_c=char_cot,
        segc=segment[:, :, None], segr=segment[:, None, :], pickc=picks, keep=keep,
        pickr=jnp.swapaxes(picks, 1, 2),
        edges=jnp.stack(
            [
                prev_ok,
                next_ok,
                jnp.concatenate([prev_ok[:, 1:], zero], axis=1),
                jnp.concatenate([zero, next_ok[:, :-1]], axis=1),
            ],
            axis=2,
        ),
        heads=heads_here, units=units_here, channels=merge_here,
    )
    weights = (wq, wout, w_in, w_down, gru_matrix, gru_bias, wc, wm)
    fw = forward_call(tokens, characters, weights, small)
    dp_size = lax.axis_size("dp")
    bw = backward_call(fw, weights, small, dp_size)
    rows = bw["small"]
    gate_row = rows[8, : 2 * LANE]
    grads = {name: bw[name] for name in GRADS}
    if dp_size != 8:
        grads, gate_row = lax.psum((grads, gate_row), "dp")
        rows = lax.psum(rows, ("dp", "tensor"))
    grads = {name: value.astype(F32) for name, value in grads.items()}
    packed = 3 * merge_here
    grad_conv = grads["conv"][:, :packed].reshape(2 * model_width, 3, merge_here)
    grad_merge = grads["merge"].reshape(2, merge_here, model_width)
    grad_gru = grads["gru"].reshape(char_width, 2, 2, LANE)[..., :units_here]
    return (
        fw["token_out"],
        fw["char_out"],
        bw["grad_tokens"],
        bw["grad_chars"],
        grads["qkv"][:, : 3 * head_cols].reshape(model_width, 3, head_cols),
        grads["out"][:head_cols],
        grads["in"],
        grads["down"],
        jnp.swapaxes(grad_gru, 1, 2),
        gate_row.reshape(2, LANE)[:, :units_here],
        jnp.swapaxes(grad_conv, 0, 1),
        jnp.swapaxes(grad_merge, 0, 1),
        jnp.concatenate([rows[4:6], rows[0:2]], axis=0),
        jnp.concatenate([rows[6:8], rows[2:4]], axis=0),
    )


def solution(mesh):
    return jax.shard_map(
        local,
        mesh=mesh,
        in_specs=(
            P("dp", "tensor", None),
            P("dp", "tensor", None),
            P("dp", None),
            P("dp", None),
            P(None, None, "tensor"),
            P("tensor", None),
            P(None, "tensor"),
            P("tensor", None),
            P(None, None, None, "tensor"),
            P(None, "tensor"),
            P(None, None, "tensor"),
            P("tensor", None, None),
            P(),
            P(),
            P("dp", "tensor", None),
            P("dp", "tensor", None),
        ),
        out_specs=(
            P("dp", "tensor", None),
            P("dp", "tensor", None),
            P("dp", "tensor", None),
            P("dp", "tensor", None),
            P(None, None, "tensor"),
            P("tensor", None),
            P(None, "tensor"),
            P("tensor", None),
            P(None, None, None, "tensor"),
            P(None, "tensor"),
            P(None, None, "tensor"),
            P("tensor", None, None),
            P(),
            P(),
        ),
        check_vma=False,
    )
```

time: 741 us -> 424 us (0.57); the launches traced: 729 us -> 423 us
  Pallas kernels: 138 us -> 367 us
  waiting for transfers between devices: 216 us -> 0 us
  local copies, waits for them, and re-layouts: 137 us -> 34.2 us
  blocking collectives: 98.2 us -> 0 us
  matrix products: 60.7 us -> 0 us
  other arithmetic: 49.7 us -> 20.5 us
  between operations: 16.5 us -> 0.95 us
  starting transfers between devices: 12.8 us -> 0 us
    pallas_call x3 -> x2, Pallas kernels: 138 us -> 367 us  [the longest x1 253 us: backward_call(): pl.pallas_call(functools.partial(backward_kernel, small['units'], channel...]
    psum x1 -> x0, waiting for transfers between devices: 202 us -> none  [reduce_weights(): low = lax.psum(tuple((g.astype(jnp.bfloat16) for g in grads)), 'dp')]
    psum x2 -> x0, blocking collectives: 61.2 us -> none  [the longest x1 39.8 us: local(): gain_grad, bias_grad = lax.psum((gain_total, bias_total), ('dp', 'tensor'))]
    dot_general x36 -> x0, matrix products: 60.7 us -> none  [the longest x14 36.9 us: inner_rows(): lax.dot_general(left_rows, right_rows, (((0,), (0,)), ((), ())), preferre...]
    unnamed x219 -> x31, local copies, waits for them, and re-layouts: 42.9 us -> 5.59 us
    all_gather x4 -> x0, blocking collectives: 37 us -> none  [the longest x2 19.5 us: local(): lax.all_gather(grad_res1.astype(BF16), 'tensor', axis=0, tiled=True)]
    slice x29 -> x3, local copies, waits for them, and re-layouts: 32.7 us -> 2.4 us  [the longest x1 1.32 us: local(): gate_row = rows[8, :2 * LANE]]
    convert_element_type x5 -> x0, local copies, waits for them, and re-layouts: 13.9 us -> none  [the longest x4 8.73 us: local(): part.astype(BF16)]
  transfers between devices with their start and end apart: 12 -> 0, of which waited for: 2 -> 0; matrix products, arithmetic and copies ran while one was open for 24% -> 0% of each run, Pallas kernels for 3% -> 0%
where the time goes in v3:
time: 424 us; the launch traced here: 423 us
  Pallas kernels  367 us (87%)
  local copies, waits for them, and re-layouts  34.2 us (8%)
  other arithmetic  20.5 us (5%)
    pallas_call x1, Pallas kernels, backward_call(): pl.pallas_call(functools.partial(backward_kernel, small['units'], channel...  253 us
    pallas_call x1, Pallas kernels, forward_call(): pl.pallas_call(functools.partial(forward_kernel, small['units'], small['c...  114 us

profile of v3, /device:TPU:0, one launch (start us, length us, event | category | flops | bytes accessed | tf_op | source)
XLA Modules:
  0.0 423.1 jit_solution(7498628654175631686)
XLA Ops:
  0.7 1.3 pad.33
  1.9 0.8 slice_bitcast_fusion.1
  2.7 0.1 select_reduce_fusion.6
  2.8 0.8 fusion.14
  3.6 0.1 fusion.7
  3.7 0.1 fusion.6
  4.0 0.8 fusion.16
  4.7 0.1 fusion.9
  5.1 0.6 broadcast_in_dim.122.segr
  5.7 0.8 fusion.21
  6.5 0.2 select_reduce_fusion.2
  6.7 0.2 select_reduce_fusion
  6.9 0.2 select_reduce_fusion.4
  7.1 0.2 select_reduce_fusion.1
  7.3 0.1 fusion
  7.4 0.1 fusion.1
  7.5 0.1 fusion.2
  7.6 0.1 fusion.3
  7.7 0.8 slice_subtract_fusion.1
  8.6 0.6 fusion.19
  9.2 1.1 copy.130
  10.3 0.3 pad.32.clone
  10.6 0.8 reshape.230.wg.refs_24_
  11.4 0.8 pad.31.wout.refs_21_
  12.2 0.2 copy.121
  12.4 0.2 copy.119
  12.6 0.2 copy.122
  12.9 0.2 copy.120
  13.1 1.3 pad_maximum_fusion.2.edges.refs_30_
  14.4 1.0 copy.124.pickc
  15.4 1.0 copy.123.segc
  16.5 0.9 pad.36.wm.refs_27_
  17.4 0.6 copy.112
  18.1 1.0 pad.30.wq.refs_20_
  19.1 2.7 copy.114
  21.8 0.2 pad_slice_fusion.1
  22.1 0.1 pad.35
  22.3 1.6 pad_maximum_fusion.wc.refs_26_
  23.8 0.6 copy.117
  24.5 2.0 copy.118
  26.5 3.5 pad_maximum_fusion.1.keep
  30.0 113.9 %shard_map.263 = (bf16[2,128,768]{2,1,0:T(8,128)(2,1)}, bf16[2,128,768]{2,1,0:T(8,128)(2,1)}, bf16[2,4,128,768]{3,2,1,0:T(8,128)(2,1)}, bf16[2,4,512,256]{3,2,1,...) custom-call(bf16[2,128,768]{2,1,0:T(8,128)(2,1)} %tokens.1, ...), custom_call_target="tpu_custom_call" | custom-call | tf_op jit(solution)/shard_map/pallas_call | solution.py:656
  143.9 253.5 %shard_map.264 = (f32[2,128,768]{2,1,0:T(8,128)}, f32[2,512,256]{2,1,0:T(8,128)}, bf16[384,768]{1,0:T(8,128)(2,1)}, bf16[1536,640]{1,0:T(8,128)(2,1)}, bf16[768,...) custom-call(bf16[2,3,128,512]{3,2,1,0:T(8,128)(2,1)} %get-tuple-elem, ...), custom_call_target="tpu_custom_call" | custom-call | tf_op jit(solution)/shard_map/pallas_call | solution.py:1324
  397.4 1.3 slice.72
  398.7 0.9 fusion.20
  399.6 0.6 pad_maximum_fusion.4
  400.2 0.6 pad_maximum_fusion.3
  400.8 1.1 reshape.238
  401.9 0.1 copy.129
  402.1 0.8 convert_bitcast_fusion
  402.9 1.8 slice_convert_fusion.2
  404.7 1.6 copy.134
  406.3 0.1 slice_convert_fusion.1
  406.4 1.7 copy.125
  408.2 1.6 convert_element_type.129
  409.7 0.1 copy-done.1
  409.8 1.6 convert_element_type.130
  411.4 0.8 copy-done
  412.2 2.1 slice_convert_fusion
  414.4 5.4 %copy.127 = f32[1536,576]{0,1:T(8,128)} copy(f32[1536,576]{1,0:T(8,128)} %slice_convert_fusion) | data formatting | bytes 7077888 | tf_op jit(solution)/shard_map/transpose | solution.py:1442
  419.8 0.7 copy.140
  420.5 0.7 copy.141
  421.3 0.9 copy.142
  422.1 1.0 copy.143
  (50 shorter events, 0.8 us)
Async XLA Ops:
  0.6 10.7 %copy-start.11 = (bf16[192,768]{1,0:T(8,128)(2,1)S(1)}, bf16[192,768]{1,0:T(8,128)(2,1)}, u32[]{:S(2)}) copy-start(bf16[192,768]{1,0:T(8,128)(2,1)} %param.21) | copy-start | bytes 884740
  12.9 3.6 copy-start.8
  14.4 3.1 copy-start.5
  397.4 7.3 %copy-start.7 = (bf16[384,768]{1,0:T(8,128)(2,1)S(1)}, bf16[384,768]{1,0:T(8,128)(2,1)}, u32[]{:S(2)}) copy-start(bf16[384,768]{1,0:T(8,128)(2,1)} %get-tuple-element.79) | copy-start | bytes 1769476
  400.8 5.5 %copy-start.4 = (bf16[768,640]{1,0:T(8,128)(2,1)S(1)}, bf16[768,640]{1,0:T(8,128)(2,1)}, u32[]{:S(2)}) copy-start(bf16[768,640]{1,0:T(8,128)(2,1)} %get-tuple-element.72) | copy-start | bytes 2949124
  406.4 1.7 copy-start.2
  408.1 1.7 copy-start.1
  409.8 2.4 copy-start
  414.4 5.4 %copy-start.10 = (bf16[2,128,768]{2,1,0:T(8,128)(2,1)S(1)}, bf16[2,128,768]{2,1,0:T(8,128)(2,1)}, u32[]{:S(2)}) copy-start(bf16[2,128,768]{2,1,0:T(8,128)(2,1)} %get-tuple-element.142) | copy-start | bytes 1179652
  414.4 6.2 %copy-start.9 = (bf16[2,128,768]{2,1,0:T(8,128)(2,1)S(1)}, bf16[2,128,768]{2,1,0:T(8,128)(2,1)}, u32[]{:S(2)}) copy-start(bf16[2,128,768]{2,1,0:T(8,128)(2,1)} %get-tuple-element.143) | copy-start | bytes 1179652
  414.4 6.9 %copy-start.6 = (f32[2,128,768]{2,1,0:T(8,128)S(1)}, f32[2,128,768]{2,1,0:T(8,128)}, u32[]{:S(2)}) copy-start(f32[2,128,768]{2,1,0:T(8,128)} %get-tuple-element.144) | copy-start | bytes 2359300
  419.8 2.4 copy-start.3

commit v4 on v3

--- a/solution.py
+++ b/solution.py
@@ -1,4 +1,5 @@
 import functools
+from types import SimpleNamespace
 
 import jax
 import jax.numpy as jnp
@@ -63,7 +64,6 @@
 F32 = jnp.float32
 BF16 = jnp.bfloat16
 LANE = 128
-CHUNKS = 32
 MIB = 1024 * 1024
 VMEM = pl.BlockSpec(memory_space=pltpu.VMEM)
 
@@ -275,42 +275,55 @@
         return total
 
 
-def recur(ups, decays, drives, outs, steps, offsets=(0, 0)):
-    def rows(tile, step, offset=0):
+def shift_rows(value, count, up, fill):
+    edge = jnp.full((count, value.shape[1]), fill, value.dtype)
+    if up:
+        return jnp.concatenate([edge, value[:-count]], axis=0)
+    return jnp.concatenate([value[count:], edge], axis=0)
+
+
+def recur(ups, decays, drives, outs, block, back=False):
+    steps = block // 8
+    pairs = [(tile, t) for tile in range(2) for t in range(4)]
+
+    def rows(tile, t, step):
         row = step if ups[tile] else steps - 1 - step
-        return pl.ds(row + offset, CHUNKS, stride=steps)
-
-    zero = jnp.zeros((CHUNKS, LANE), F32)
-    one = jnp.ones((CHUNKS, LANE), F32)
+        return pl.ds(pl.multiple_of(t * block + row * 8, 8), 8)
 
     def summary(step, carry):
         new = []
-        for tile in range(2):
-            state, mult = carry[2 * tile], carry[2 * tile + 1]
-            decay = decays[tile, rows(tile, step, offsets[tile]), :]
-            new += [decay * state + drives[tile, rows(tile, step), :], decay * mult]
+        for i, (tile, t) in enumerate(pairs):
+            state, mult = carry[2 * i], carry[2 * i + 1]
+            here = rows(tile, t, step)
+            decay, drive = decays[tile, here, :], drives[tile, here, :]
+            state = decay * (state + drive) if back else decay * state + drive
+            new += [state, decay * mult]
         return tuple(new)
 
-    ends = lax.fori_loop(0, steps, summary, (zero, one, zero, one), unroll=4)
+    zero, one = jnp.zeros((8, LANE), F32), jnp.ones((8, LANE), F32)
+    ends = lax.fori_loop(0, steps, summary, (zero, one) * 8, unroll=4)
     starts = []
     for tile in range(2):
-        final, mult = ends[2 * tile], ends[2 * tile + 1]
-        order = range(CHUNKS) if ups[tile] else range(CHUNKS - 1, -1, -1)
-        carry = jnp.zeros((1, LANE), F32)
-        heads = [None] * CHUNKS
-        for chunk in order:
-            heads[chunk] = carry
-            carry = mult[chunk : chunk + 1] * carry + final[chunk : chunk + 1]
-        starts.append(jnp.concatenate(heads, axis=0))
+        state = jnp.concatenate([ends[2 * (4 * tile + t)] for t in range(4)], axis=0)
+        mult = jnp.concatenate([ends[2 * (4 * tile + t) + 1] for t in range(4)], axis=0)
+        for count in (1, 2, 4, 8, 16):
+            state = mult * shift_rows(state, count, ups[tile], 0.0) + state
+            mult = mult * shift_rows(mult, count, ups[tile], 1.0)
+        state = shift_rows(state, 1, ups[tile], 0.0)
+        starts += [state[8 * t : 8 * t + 8] for t in range(4)]
 
     def write(step, carry):
         new = []
-        for tile in range(2):
-            here = rows(tile, step)
-            decay = decays[tile, rows(tile, step, offsets[tile]), :]
-            state = decay * carry[tile] + drives[tile, here, :]
-            outs[tile, here, :] = state
-            new.append(state)
+        for i, (tile, t) in enumerate(pairs):
+            here = rows(tile, t, step)
+            decay, drive = decays[tile, here, :], drives[tile, here, :]
+            if back:
+                value = drive + carry[i]
+                new.append(decay * value)
+            else:
+                value = decay * carry[i] + drive
+                new.append(value)
+            outs[tile, here, :] = value
         return tuple(new)
 
     lax.fori_loop(0, steps, write, tuple(starts), unroll=4)
@@ -321,8 +334,8 @@
     segc, segr, pickc, keep, edges,
     token_out, char_out, o_x, o_c, o_qkv, o_p, o_ctx, o_h, o_act, o_dact, o_mid, o_st, o_mg,
     o_dmg, o_states, o_decay, o_unit0, o_unit1, o_scale, o_res3, o_res4, o_branch, norm_grads,
-    x, c, qkv, p, ctx, h, act, dact, mid, st, mg, dmg, states, decays, unit0, unit1, scale, res3, res4, branch,
-    hidden, middle, outs_t, outs_c, drive, taps, perm,
+    x, c, qkv, p, ctx, h, act, dact, mid, st, mg, dmg, low_states, decays, unit0, unit1, scale, res3, res4, branch,
+    hidden, middle, outs_t, outs_c, states, drive, taps, perm,
     stage, got, held, temp, send, recv, local,
 ):
     seqs, length = tokens.shape[0], segr.shape[2]
@@ -358,7 +371,7 @@
 
     plan = [
         (x, o_x), (c, o_c), (qkv, o_qkv), (p, o_p), (ctx, o_ctx), (h, o_h), (act, o_act),
-        (dact, o_dact), (mid, o_mid), (st, o_st), (mg, o_mg), (dmg, o_dmg), (states, o_states),
+        (dact, o_dact), (mid, o_mid), (st, o_st), (mg, o_mg), (dmg, o_dmg), (low_states, o_states),
         (decays, o_decay), (res4, o_res4), (unit0, o_unit0), (unit1, o_unit1), (scale, o_scale), (res3, o_res3), (branch, o_branch),
         (outs_t, token_out), (outs_c, char_out),
     ]
@@ -472,21 +485,24 @@
 
         total = 4 * block_chars
         lax.fori_loop(0, total // LANE, gates, 0)
-        recur((True, False), decays.at[s], drive, states.at[s], total // CHUNKS)
+        recur((True, False), decays.at[s], drive, states, block_chars)
         save(s, decays)
+
+        for tile in range(2):
+            low_states[s, tile] = states[tile].astype(BF16)
 
         def pick(t, carry):
             rows = pl.ds(pl.multiple_of(t * shard, shard), shard)
             for tile in range(2):
                 ids = lax.broadcasted_iota(jnp.int32, (shard, total), 1)
                 hot = (ids == pickc[s, rows, tile : tile + 1]).astype(F32).astype(BF16)
-                out = nn(hot, states[s, tile].astype(BF16))
+                out = nn(hot, low_states[s, tile])
                 st[s, me, rows, pl.ds(tile * LANE, LANE)] = out.astype(BF16)
             return carry
 
         lax.fori_loop(0, 4, pick, 0)
         gs.start(s)
-        save(s, states)
+        save(s, low_states)
 
     def norm_and_gru(s):
         first_norm(s)
@@ -626,7 +642,7 @@
         "st": ((seqs, 4, length, 2 * LANE), BF16),
         "mg": ((seqs, length, wm.shape[0]), BF16),
         "dmg": ((seqs, length, wm.shape[0]), BF16),
-        "states": ((seqs, 2, total, LANE), F32),
+        "states": ((seqs, 2, total, LANE), BF16),
         "decay": ((seqs, 2, total, LANE), F32),
         "unit0": ((seqs, shard, width), F32),
         "unit1": ((seqs, shard, width), F32),
@@ -639,6 +655,7 @@
     low_rows = ((seqs, shard, width), BF16)
     scratch = list(big.values()) + [
         rows, rows, low_rows, low_rows,
+        ((2, total, LANE), F32),
         ((2, total, LANE), F32),
         ((length + 16, wc.shape[1]), F32),
         ((8 * LANE, width), BF16),
@@ -672,135 +689,266 @@
     return dict(zip(names, outs))
 
 
-class Reduce:
-    def __init__(self, net, buf, out, first, land, land_first, rows, order):
-        self.net, self.buf, self.out, self.land, self.order = net, buf, out, land, order
-        self.first, self.land_first, self.rows = first, land_first, rows
-        self.slots = net.take(2 * len(order))
-        self.mark = net.mark()
-
-    def start_of(self, level):
-        start = self.first
-        for i in range(level):
-            start = start + self.net.bit(self.order[i]) * (self.rows >> (i + 1))
-        return start
-
-    def half(self, level):
-        return self.rows >> (level + 1)
-
-    def view(self, start, size, ref=None):
-        ref = self.buf if ref is None else ref
-        return ref.at[pl.ds(pl.multiple_of(start, 16), size), :]
-
-    def keep(self):
-        levels = len(self.order)
-        start, size = self.start_of(levels), self.rows >> levels
-        return pltpu.make_async_copy(
-            self.view(start, size), self.view(start, size, self.out), self.mark
-        )
-
-    def landing(self, level):
-        start = self.land_first + self.rows - (self.rows >> level)
-        return self.land.at[pl.ds(start, self.half(level)), :]
-
-    def down(self, level):
-        bit = self.net.bit(self.order[level])
-        other = self.start_of(level) + (1 - bit) * self.half(level)
-        return self.net.copy(
-            self.slots[level],
-            self.view(other, self.half(level)),
-            self.landing(level),
-            self.order[level],
-        )
-
-    def up(self, level):
-        start, size = self.start_of(level + 1), self.half(level)
-        target = self.view(start, size, self.out)
-        source = self.view(start, size) if level == len(self.order) - 1 else target
-        return self.net.copy(
-            self.slots[len(self.order) + level], source, target, self.order[level]
-        )
-
-    def step(self, number):
-        levels = len(self.order)
-        if 0 < number <= levels:
-            level = number - 1
-            self.down(level).wait()
-            start = self.start_of(level + 1)
-            start_land = self.land_first + self.rows - (self.rows >> level)
-
-            def add(i, carry):
-                rows = pl.ds(pl.multiple_of(start + i * 16, 16), 16)
-                more = pl.ds(pl.multiple_of(start_land + i * 16, 16), 16)
-                total = self.buf[rows, :].astype(F32) + self.land[more, :].astype(F32)
-                self.buf[rows, :] = total.astype(BF16)
-                return carry
-
-            lax.fori_loop(0, self.half(level) // 16, add, 0)
-            if number == levels:
-                self.keep().start()
-        elif number > levels:
-            self.up(2 * levels - number).wait()
-            if number == levels + 1:
-                self.keep().wait()
-        if number < levels:
-            self.down(number).start()
-        elif number < 2 * levels:
-            self.up(2 * levels - 1 - number).start()
-
-
 class Plane:
     def __init__(self, send, recv, marks):
         self.index = lax.axis_index("dp")
+        self.x, self.z = self.index % 2, self.index // 2
         self.send, self.recv, self.marks, self.used, self.marked = send, recv, marks, 0, 0
 
     def mark(self):
         self.marked += 1
         return self.marks.at[self.marked - 1]
-
-    def bit(self, number):
-        return (self.index // (1 << number)) % 2
-
-    def peer(self, number):
-        return self.index + (1 - 2 * self.bit(number)) * (1 << number)
 
     def take(self, count):
         first = self.used
         self.used += count
         return [first + i for i in range(count)]
 
-    def copy(self, slot, source, target, number):
+    def peer(self, way):
+        if way == "x":
+            return self.index + 1 - 2 * self.x
+        return (self.index + (2 if way == "up" else 6)) % 8
+
+    def pair(self, bit):
+        digit = self.index // (1 << bit) % 2
+        return self.index + (1 - 2 * digit) * (1 << bit)
+
+    def copy(self, slot, source, target, peer):
         return pltpu.make_async_remote_copy(
             src_ref=source,
             dst_ref=target,
             send_sem=self.send.at[slot],
             recv_sem=self.recv.at[slot],
-            device_id={"dp": self.peer(number)},
+            device_id={"dp": peer},
             device_id_type=pl.DeviceIdType.MESH,
         )
+
+
+class Reduce:
+    steps = 9
+
+    def __init__(self, plane, buf, out, land, first, land_first, rows, x_first):
+        self.plane, self.buf, self.out, self.land = plane, buf, out, land
+        self.first, self.land_first, self.rows, self.x_first = first, land_first, rows, x_first
+        self.slots = plane.take(14)
+        self.mark = plane.mark()
+        x, z = plane.x, plane.z
+        if x_first:
+            self.quarter, self.half = rows // 8, rows // 2
+            self.z_base, self.x_base = first + x * self.half, first
+        else:
+            self.quarter, self.half = rows // 4, rows // 8
+            self.z_base, self.x_base = first, first + z * self.quarter
+        self.x_land = land_first + 5 * self.quarter
+
+    @staticmethod
+    def landing_rows(rows, x_first):
+        return 5 * rows // 8 + rows // 2 if x_first else 5 * rows // 4 + rows // 8
+
+    def rows_of(self, ref, start, size):
+        return ref.at[pl.ds(pl.multiple_of(start, 16), size), :]
+
+    def add(self, start, land_start, size):
+        def one(i, carry):
+            rows = pl.ds(pl.multiple_of(start + i * 16, 16), 16)
+            more = pl.ds(pl.multiple_of(land_start + i * 16, 16), 16)
+            total = self.buf[rows, :].astype(F32) + self.land[more, :].astype(F32)
+            self.buf[rows, :] = total.astype(BF16)
+            return carry
+
+        lax.fori_loop(0, size // 16, one, 0)
+
+    def gather_copy(self, way, step, z):
+        piece = 3 - step + z if way == "up" else step - 3 + z
+        slot = piece if way == "up" else piece + (4 - piece) * (step // 2)
+        return self.plane.copy(
+            self.slots[step if way == "up" else 3 + step],
+            self.rows_of(self.buf, self.z_base + piece * self.quarter, self.quarter),
+            self.rows_of(self.land, self.land_first + slot * self.quarter, self.quarter),
+            self.plane.peer(way),
+        )
+
+    def gather_send(self, step):
+        z = self.plane.z
+        pl.when(step >= z)(lambda: self.gather_copy("up", step, z).start())
+        pl.when(step >= 3 - z)(lambda: self.gather_copy("down", step, z).start())
+
+    def gather_wait(self, step):
+        z = self.plane.z
+
+        @pl.when((z >= 1) & (step >= z - 1))
+        def _():
+            self.gather_copy("up", step, z - 1).wait_recv()
+            piece = 3 - step + z - 1
+            self.add(
+                self.z_base + piece * self.quarter,
+                self.land_first + piece * self.quarter,
+                self.quarter,
+            )
+
+        @pl.when((z <= 2) & (step >= 2 - z))
+        def _():
+            self.gather_copy("down", step, z + 1).wait_recv()
+            piece = step - 3 + z + 1
+            slot = piece if step < 2 else 4
+            self.add(
+                self.z_base + piece * self.quarter,
+                self.land_first + slot * self.quarter,
+                self.quarter,
+            )
+
+        pl.when(step >= z)(lambda: self.gather_copy("up", step, z).wait_send())
+        pl.when(step >= 3 - z)(lambda: self.gather_copy("down", step, z).wait_send())
+
+    def spread_copy(self, way, step, z):
+        piece = z - step if way == "up" else z + step
+        start = self.z_base + piece * self.quarter
+        target = self.rows_of(self.out, start, self.quarter)
+        source = target
+        if self.x_first and step == 0:
+            source = self.rows_of(self.buf, start, self.quarter)
+        slot = self.slots[6 + step if way == "up" else 9 + step]
+        return self.plane.copy(slot, source, target, self.plane.peer(way))
+
+    def spread_send(self, step):
+        z = self.plane.z
+        pl.when((z <= 2) & (step <= z))(lambda: self.spread_copy("up", step, z).start())
+        pl.when((z >= 1) & (step <= 3 - z))(lambda: self.spread_copy("down", step, z).start())
+
+    def spread_wait(self, step):
+        z = self.plane.z
+        pl.when((z >= 1) & (step <= z - 1))(lambda: self.spread_copy("up", step, z - 1).wait_recv())
+        pl.when((z <= 2) & (step <= 2 - z))(lambda: self.spread_copy("down", step, z + 1).wait_recv())
+        pl.when((z <= 2) & (step <= z))(lambda: self.spread_copy("up", step, z).wait_send())
+        pl.when((z >= 1) & (step <= 3 - z))(lambda: self.spread_copy("down", step, z).wait_send())
+
+    def halve(self):
+        other = self.x_base + (1 - self.plane.x) * self.half
+        return self.plane.copy(
+            self.slots[12],
+            self.rows_of(self.buf, other, self.half),
+            self.rows_of(self.land, self.x_land, self.half),
+            self.plane.peer("x"),
+        )
+
+    def halve_wait(self):
+        self.halve().wait()
+        self.add(self.x_base + self.plane.x * self.half, self.x_land, self.half)
+
+    def double(self):
+        start = self.x_base + self.plane.x * self.half
+        target = self.rows_of(self.out, start, self.half)
+        source = target if self.x_first else self.rows_of(self.buf, start, self.half)
+        return self.plane.copy(self.slots[13], source, target, self.plane.peer("x"))
+
+    def keep(self):
+        if self.x_first:
+            start, size = self.z_base + self.plane.z * self.quarter, self.quarter
+        else:
+            start, size = self.x_base + self.plane.x * self.half, self.half
+        return pltpu.make_async_copy(
+            self.rows_of(self.buf, start, size), self.rows_of(self.out, start, size), self.mark
+        )
+
+    def step(self, number):
+        if self.x_first:
+            if number == 0:
+                self.halve().start()
+            elif number == 1:
+                self.halve_wait()
+                self.gather_send(0)
+            elif number <= 3:
+                self.gather_wait(number - 2)
+                self.gather_send(number - 1)
+            elif number == 4:
+                self.gather_wait(2)
+                self.keep().start()
+                self.spread_send(0)
+            elif number <= 6:
+                self.spread_wait(number - 5)
+                self.spread_send(number - 4)
+            elif number == 7:
+                self.spread_wait(2)
+                self.keep().wait()
+                self.double().start()
+            else:
+                self.double().wait()
+        else:
+            if number == 0:
+                self.gather_send(0)
+            elif number <= 2:
+                self.gather_wait(number - 1)
+                self.gather_send(number)
+            elif number == 3:
+                self.gather_wait(2)
+                self.halve().start()
+            elif number == 4:
+                self.halve_wait()
+                self.keep().start()
+                self.double().start()
+            elif number == 5:
+                self.double().wait()
+                self.keep().wait()
+                self.spread_send(0)
+            elif number <= 7:
+                self.spread_wait(number - 6)
+                self.spread_send(number - 5)
+            else:
+                self.spread_wait(2)
 
 
 SAVED = (
     "branch", "mg", "dmg", "mid", "st", "res3", "res4", "unit0", "unit1", "scale", "act", "dact",
     "h", "p", "qkv", "ctx", "x", "c", "states", "decay",
 )
-GRADS = ("merge", "conv", "down", "in", "gru", "out", "qkv")
+GRADS = ("merge", "conv", "down", "win", "gru", "out", "qkv")
+HEADS_OF = dict(zip(GRADS, (0, 1024, 768, 256, 0, 0, 512)))
+SCHEDULE = (
+    (0, 10, 20,),
+    (),
+    (1, 21,),
+    (2, 11,),
+    (22,),
+    (30, 3,),
+    (40, 50, 12,),
+    (),
+    (23,),
+    (),
+    (51,),
+    (13, 31,),
+    (4,),
+    (52, 41,),
+    (24, 14, 5,),
+    (32,),
+    (25,),
+    (70, 80, 90, 53, 15, 42, 6,),
+    (33, 71, 26,),
+    (91, 43, 16,),
+    (81, 34, 7, 54, 72, 92, 27, 44,),
+    (82, 17,),
+    (55, 73, 35, 93,),
+    (60, 83, 8, 28,),
+    (45, 61,),
+    (84, 56, 18, 62, 74, 36,),
+    (94, 46, 85, 63, 75, 95,),
+    (64, 57, 65, 37, 47, 86, 76, 96, 58, 66, 87, 38, 77, 97, 67, 48, 78, 98, 68, 88,),
+)
 
 
 def backward_kernel(units, channels, dp_size, *refs):
     refs = list(refs)
     take = lambda count: [refs.pop(0) for _ in range(count)]
-    hbm = dict(zip(SAVED, take(len(SAVED))))
+    hbm = SimpleNamespace(**dict(zip(SAVED, take(len(SAVED)))))
     wq, wout, win, wdown, wg, gate_bias, wc, wm, gain, pickr, edges, norm_in = take(12)
     grad_tokens, grad_chars = take(2)
     grads_out = dict(zip(GRADS, take(len(GRADS))))
     (small_out,) = take(1)
     names = [n for n in SAVED if n not in ("branch", "states", "decay", "p", "x")]
-    v = dict(zip(names, take(len(names))))
+    v = SimpleNamespace(**dict(zip(names, take(len(names)))))
     (pb, states, decay, drive, dpre, dyk, fg, gtok, dproj, gru_acc, res2, res1, ds, parts,
      stage, got, held, temp, cstage, cgot, cheld, ctemp) = take(22)
     land = dict(zip(GRADS, take(len(GRADS))))
-    big = dict(zip(GRADS, take(len(GRADS))))
+    big = SimpleNamespace(**dict(zip(GRADS, take(len(GRADS)))))
     small, small_land, send, recv, dsend, drecv, local, marks = take(8)
 
     seqs, shard, width = grad_tokens.shape
@@ -808,7 +956,7 @@
     block_chars = grad_chars.shape[1]
     total = 4 * block_chars
     heads = pb.shape[1] // 4
-    cols = v["ctx"].shape[2]
+    cols = v.ctx.shape[2]
     g = Group(send, recv, seqs)
     me = g.me
     inside = dp_size == 8
@@ -823,18 +971,18 @@
 
     def load(name):
         index = names.index(name)
-        return pltpu.make_async_copy(hbm[name], v[name], local.at[index])
+        return pltpu.make_async_copy(getattr(hbm, name), getattr(v, name), local.at[index])
 
     spare = len(names)
-    p_copy = lambda: pltpu.make_async_copy(hbm["p"], pb, local.at[spare])
-    x_copy = lambda: pltpu.make_async_copy(hbm["x"], v["h"], local.at[39])
+    p_copy = lambda: pltpu.make_async_copy(hbm.p, pb, local.at[spare])
+    x_copy = lambda: pltpu.make_async_copy(hbm.x, v.h, local.at[39])
 
     def states_copy(s):
-        return pltpu.make_async_copy(hbm["states"].at[s], states, local.at[spare + 1])
+        return pltpu.make_async_copy(hbm.states.at[s], states, local.at[spare + 1])
 
     def decay_copy(s, tile):
         return pltpu.make_async_copy(
-            hbm["decay"].at[s, tile], decay.at[tile, pl.ds(8, total), :], local.at[spare + 2 + tile]
+            hbm.decay.at[s, tile], decay.at[tile], local.at[spare + 2 + tile]
         )
 
     def out_copy(kind, s):
@@ -845,9 +993,9 @@
 
     pieces = 2 * width // length
     gb = Gather(
-        g, pb, hbm["branch"], place=lambda s, t: pb.at[s, pl.ds(t * pieces, pieces)]
-    )
-    gf, ga = Gather(g, fg), Gather(g, v["mid"])
+        g, pb, hbm.branch, place=lambda s, t: pb.at[s, pl.ds(t * pieces, pieces)]
+    )
+    gf, ga = Gather(g, fg), Gather(g, v.mid)
     pick = lambda ref: (lambda s, i: ref.at[s, i])
     own = lambda ref: (lambda s: ref.at[s])
     s_mid = Scatter(g, pick(stage), pick(got), own(held), temp)
@@ -858,7 +1006,7 @@
 
     def own_branch(s):
         return pltpu.make_async_copy(
-            hbm["branch"].at[s], gb.at(s, me), local.at[spare + 4 + 2 * seqs + s]
+            hbm.branch.at[s], gb.at(s, me), local.at[spare + 4 + 2 * seqs + s]
         )
 
     each(lambda s: own_branch(s).start())
@@ -874,15 +1022,13 @@
     barrier = pltpu.get_barrier_semaphore()
     places = [{"tensor": g.pair}, {"tensor": g.far}]
     if inside:
-        places += [{"dp": plane.peer(k)} for k in range(3)]
+        places += [{"dp": plane.peer(way)} for way in ("x", "up", "down")]
+        places += [{"dp": plane.pair(2)}]
     for place in places:
         pl.semaphore_signal(barrier, inc=1, device_id=place, device_id_type=pl.DeviceIdType.MESH)
     pl.semaphore_wait(barrier, len(places))
     each(gb.start)
     dpre[...] = jnp.zeros_like(dpre)
-    for tile in range(2):
-        decay[tile, pl.ds(0, 8), :] = jnp.zeros((8, LANE), F32)
-        decay[tile, pl.ds(total + 8, 8), :] = jnp.zeros((8, LANE), F32)
     small[...] = jnp.zeros_like(small)
     small[0, pl.ds(0, 4), :] = norm_in[...]
     lane = lax.broadcasted_iota(jnp.int32, (shard, LANE), 1)
@@ -905,7 +1051,7 @@
                 piece = nt(pb[s, t * pieces + j], wm[:, j * length : (j + 1) * length])
                 back = piece if back is None else back + piece
             dpre[pl.ds(pl.multiple_of(8 + t * shard, 8), shard), :] = (
-                (back * v["dmg"][s, rows, :].astype(F32)).astype(BF16).astype(F32)
+                (back * v.dmg[s, rows, :].astype(F32)).astype(BF16).astype(F32)
             )
             return carry
 
@@ -932,7 +1078,7 @@
         def char_part(b, out):
             first = pl.multiple_of(width + b * 2 * LANE, 2 * LANE)
             out[...] = nt(dyk[s], wc[pl.ds(first, 2 * LANE), :])
-            out[block_rows(me, shard), :] += v["res4"][s, b].astype(F32)
+            out[block_rows(me, shard), :] += v.res4[s, b].astype(F32)
 
         s_chr.start(s, char_part)
 
@@ -946,12 +1092,12 @@
         right = jnp.concatenate(
             [pb[s, t * pieces + j] for s in range(seqs) for t in range(4)], axis=0
         )
-        out = tn(v["mg"][...].reshape(tokens, -1), right)[:channels].astype(BF16)
+        out = tn(v.mg[...].reshape(tokens, -1), right)[:channels].astype(BF16)
         at = 0
         while at < length:
             part, inside_at = divmod(j * length + at, half_w)
             size = min(length - at, half_w - inside_at)
-            big["merge"][pl.ds(part * channels, channels), pl.ds(inside_at, size)] = out[
+            big.merge[pl.ds(part * channels, channels), pl.ds(inside_at, size)] = out[
                 :, at : at + size
             ]
             at += size
@@ -959,175 +1105,113 @@
 
     def conv_mid(j, carry):
         colsj = pl.ds(pl.multiple_of(j * step_w, step_w), step_w)
-        out = tn(v["mid"][:, :, :, colsj].reshape(tokens, step_w), dyk[...].reshape(tokens, -1))
-        big["conv"][block_rows(j, step_w), :] = out.astype(BF16)
+        out = tn(v.mid[:, :, :, colsj].reshape(tokens, step_w), dyk[...].reshape(tokens, -1))
+        big.conv[block_rows(j, step_w), :] = out.astype(BF16)
         return carry
 
     lax.fori_loop(0, width // step_w, conv_mid, 0)
 
     def conv_char(t, carry):
-        out = tn(v["st"][:, t].reshape(tokens, 2 * LANE), dyk[...].reshape(tokens, -1))
+        out = tn(v.st[:, t].reshape(tokens, 2 * LANE), dyk[...].reshape(tokens, -1))
         for d in range(2):
             first = pl.multiple_of(width + d * 4 * units + t * units, 16)
-            big["conv"][pl.ds(first, units), :] = out[d * LANE : d * LANE + units].astype(BF16)
+            big.conv[pl.ds(first, units), :] = out[d * LANE : d * LANE + units].astype(BF16)
         return carry
 
     lax.fori_loop(0, 4, conv_char, 0)
     p_copy().start()
 
-    near, along = (0, 1, 2), (1, 2, 0)
-
-    def split(name, head):
-        rows = big[name].shape[0]
-        result = []
-        if head:
-            result.append(
-                Reduce(plane, big[name], grads_out[name], 0, land[name], 0, head, near)
-            )
-        if rows > head:
-            result.append(
-                Reduce(
-                    plane, big[name], grads_out[name], head, land[name], head * 7 // 8,
-                    rows - head, along,
+    sums = []
+    for name in GRADS if inside else ():
+        height, at = getattr(big, name).shape[0], 0
+        pieces_of = ((0, HEADS_OF[name], True), (HEADS_OF[name], height - HEADS_OF[name], False))
+        for first, size, x_first in pieces_of:
+            if size:
+                sums.append(
+                    Reduce(
+                        plane, getattr(big, name), grads_out[name], land[name], first, at, size,
+                        x_first,
+                    )
                 )
-            )
-        return result
-
-    if inside:
-        first_sums = split("conv", 1024) + split("merge", 0)
-        second_sums = split("down", big["down"].shape[0]) + split("in", 256)
-        third_sums = split("qkv", 512) + split("out", 0) + split("gru", big["gru"].shape[0])
-    else:
-        first_sums, second_sums, third_sums = [], [], []
-
-    def advance(sums, number):
-        for one in sums:
-            one.step(number)
-
-    advance(first_sums, 0)
+                at += Reduce.landing_rows(size, x_first)
+    fired = [0] * len(sums)
+
+    def fire(hook):
+        for entry in SCHEDULE[hook] if inside else ():
+            which, number = divmod(entry, 10)
+            fired[which] += 1
+            sums[which].step(number)
+
+    def fire_in(seq, hook, stride):
+        for k in range(2):
+            pl.when(seq == k)(functools.partial(fire, hook + k * stride))
+
+    fire(0)
 
     def second_back(s):
-        incoming = v["res3"][s] + s_mid.finish(s)
-        unit = v["unit1"][s]
+        incoming = v.res3[s] + s_mid.finish(s)
+        unit = v.unit1[s]
         small[0, 5:6] += jnp.sum(incoming * unit, axis=0, keepdims=True)
         small[0, 7:8] += jnp.sum(incoming, axis=0, keepdims=True)
-        spread = v["scale"][s, 1][:, 0:1]
+        spread = v.scale[s, 1][:, 0:1]
         res2[s] = normalize_back(unit, spread, incoming * gain[1:2])
         fg[s, me] = res2[s].astype(BF16)
         gtok[s] = s_chr.finish(s).astype(BF16)
         gf.start(s)
+        fire_in(s, 1, 1)
 
     for name in ("res3", "unit1", "scale"):
         load(name).wait()
     each(second_back)
-    load("c").wait()
-
-    def gru_back(s):
-        def spread_out(t, carry):
-            rows = block_rows(t, LANE)
-            for tile in range(2):
-                ids = lax.broadcasted_iota(jnp.int32, (LANE, length), 0) + t * LANE
-                hot = (ids == pickr[s, tile : tile + 1, :]).astype(F32).astype(BF16)
-                drive[tile, rows, :] = nn(hot, gtok[s, :, pl.ds(tile * LANE, LANE)])
-            return carry
-
-        lax.fori_loop(0, total // LANE, spread_out, 0)
-        for tile in range(2):
-            decay_copy(s, tile).wait()
-        recur((False, True), decay, drive, drive, total // CHUNKS, (9, 7))
-        states_copy(s).wait()
-
-        def finish(t, sums):
-            rows = block_rows(t, LANE)
-            per = block_chars // LANE
-            inner = block_rows(t % per, LANE)
-            proj = nn(v["c"][s, t // per, inner, :], wg[...])
-            new = []
-            for tile in range(2):
-                colst = slice(tile * LANE, (tile + 1) * LANE)
-                gate = jax.nn.sigmoid(proj[:, colst] + gate_bias[:, colst])
-                cand = proj[:, (2 + tile) * LANE : (3 + tile) * LANE]
-                flow = drive[tile, rows, :] * gate
-                logit = flow * (cand - states[tile, rows, :])
-                dproj[rows, pl.ds(tile * LANE, LANE)] = logit.astype(BF16)
-                dproj[rows, pl.ds((2 + tile) * LANE, LANE)] = flow.astype(BF16)
-                new.append(sums[tile] + jnp.sum(logit, axis=0, keepdims=True))
-            return tuple(new)
-
-        zero = jnp.zeros((1, LANE), F32)
-        sums = lax.fori_loop(0, total // LANE, finish, (zero, zero))
-        for tile in range(2):
-            small[0, 8:9, pl.ds(tile * LANE, LANE)] += sums[tile]
-
-        @pl.when(s + 1 < seqs)
-        def _():
-            states_copy(s + 1).start()
-            for tile in range(2):
-                decay_copy(s + 1, tile).start()
-
-        def part(b, out):
-            out[...] = nt(dproj[block_rows(b, block_chars), :], wg[...])
-
+    for name in ("dact", "act", "h"):
+        load(name).wait()
+
+    def ffn_back(s):
         gf.forward(s)
         gf.finish(s)
-        s_cout.start(s, part)
-        grad = tn(v["c"][s].reshape(total, -1), dproj[...])
-
-        @pl.when(s == 0)
-        def _():
-            gru_acc[...] = grad
-
-        @pl.when(s > 0)
-        def _():
-            gru_acc[...] += grad
-
-    each(gru_back)
-    big["gru"][...] = gru_acc[...].astype(BF16)
-    advance(first_sums, 1)
-    for name in ("dact", "act", "h"):
-        load(name).wait()
-
-    def ffn_back(s):
+
         def part(b, out):
-            back = nt(fg[s, b], wdown[...]) * v["dact"][s, b].astype(F32)
-            v["dact"][s, b] = back.astype(BF16)
-            out[...] = nt(v["dact"][s, b], win[...])
+            back = nt(fg[s, b], wdown[...]) * v.dact[s, b].astype(F32)
+            v.dact[s, b] = back.astype(BF16)
+            out[...] = nt(v.dact[s, b], win[...])
 
         s_hid.start(s, part)
+        fire_in(s, 3, 1)
 
     each(ffn_back)
-    advance(first_sums, 2)
 
     def ffn_weights(j, carry):
         colsj = pl.ds(pl.multiple_of(j * step_w, step_w), step_w)
-        out = tn(v["act"][:, :, :, colsj].reshape(tokens, step_w), fg[...].reshape(tokens, width))
-        big["down"][block_rows(j, step_w), :] = out.astype(BF16)
+        out = tn(v.act[:, :, :, colsj].reshape(tokens, step_w), fg[...].reshape(tokens, width))
+        big.down[block_rows(j, step_w), :] = out.astype(BF16)
         return carry
 
-    lax.fori_loop(0, big["down"].shape[0] // step_w, ffn_weights, 0)
+    lax.fori_loop(0, big.down.shape[0] // step_w, ffn_weights, 0)
+    fire(5)
 
     def in_weights(j, carry):
         colsj = pl.ds(pl.multiple_of(j * step_w, step_w), step_w)
         out = tn(
-            v["h"][:, :, :, colsj].reshape(tokens, step_w), v["dact"][...].reshape(tokens, -1)
+            v.h[:, :, :, colsj].reshape(tokens, step_w), v.dact[...].reshape(tokens, -1)
         )
-        big["in"][block_rows(j, step_w), :] = out.astype(BF16)
+        big.win[block_rows(j, step_w), :] = out.astype(BF16)
         return carry
 
     lax.fori_loop(0, width // step_w, in_weights, 0)
     x_copy().start()
-    advance(second_sums, 0)
+    fire(6)
     load("unit0").wait()
 
     def first_back(s):
         incoming = res2[s] + s_hid.finish(s)
-        unit = v["unit0"][s]
+        unit = v.unit0[s]
         small[0, 4:5] += jnp.sum(incoming * unit, axis=0, keepdims=True)
         small[0, 6:7] += jnp.sum(incoming, axis=0, keepdims=True)
-        spread = v["scale"][s, 0][:, 0:1]
+        spread = v.scale[s, 0][:, 0:1]
         res1[s] = normalize_back(unit, spread, incoming * gain[0:1])
-        v["mid"][s, me] = res1[s].astype(BF16)
+        v.mid[s, me] = res1[s].astype(BF16)
         ga.start(s)
+        fire_in(s, 7, 1)
 
     each(first_back)
     hops = [("t", g.pair), ("t", g.far)] + ([("d", k) for k in range(3)] if inside else [])
@@ -1138,22 +1222,21 @@
         source, target = small.at[number], small_land.at[number]
         if kind == "t":
             return g.copy(slots_t[number], 0, source, target, where)
-        return plane.copy(slots_d[where], source, target, where)
+        return plane.copy(slots_d[where], source, target, plane.pair(where))
 
     def small_step(number):
         if number > 0:
             small_copy(number - 1).wait()
-            keep_rows = 8 if number <= 2 else 16
             value, more = small[number - 1], small_land[number - 1]
             small[number, pl.ds(0, 8), :] = value[:8] + more[:8]
-            small[number, pl.ds(8, 8), :] = value[8:] if number <= 2 else value[8:] + more[8:]
+            rest = small[6, pl.ds(0, 8), :] if number <= 2 else value[8:] + more[8:]
+            small[number, pl.ds(8, 8), :] = rest
         if number < len(hops):
             small_copy(number).start()
 
     if not inside:
         hops = []
     small_step(0) if hops else None
-    advance(first_sums, 3)
     for name in ("qkv", "ctx"):
         load(name).wait()
     p_copy().wait()
@@ -1161,10 +1244,10 @@
     def attention_back(s):
         ga.forward(s)
         ga.finish(s)
-        dctx = v["dmg"]
+        dctx = v.dmg
 
         def context(t, carry):
-            dctx[s, block_rows(t, shard), :] = nt(v["mid"][s, t], wout[...]).astype(BF16)
+            dctx[s, block_rows(t, shard), :] = nt(v.mid[s, t], wout[...]).astype(BF16)
             return carry
 
         lax.fori_loop(0, 4, context, 0)
@@ -1181,18 +1264,18 @@
                     grad = dctx[s, rows, lanes]
                     if paired:
                         grad = jnp.where(left if half == 0 else ~left, grad, jnp.zeros_like(grad))
-                    back = nt(grad, v["qkv"][s, 2, :, lanes])
+                    back = nt(grad, v.qkv[s, 2, :, lanes])
                     probs = pb[s, head * 4 + b].astype(F32)
                     row_dot = jnp.sum(probs * back, axis=-1, keepdims=True)
                     ds[b] = (probs * (back - row_dot)).astype(BF16)
-                    out = nn(ds[b], v["qkv"][s, 1, :, lanes])
+                    out = nn(ds[b], v.qkv[s, 1, :, lanes])
                     if half == 1:
                         out = jnp.where(left, ctemp[rows, lanes], out)
                     ctemp[rows, lanes] = out
                     return carry
 
                 lax.fori_loop(0, 4, rows_of, 0)
-                keys = tn(ds[...].reshape(length, length), v["qkv"][s, 0, :, lanes])
+                keys = tn(ds[...].reshape(length, length), v.qkv[s, 0, :, lanes])
                 values = tn(
                     pb[s, pl.ds(head * 4, 4)].reshape(length, length), dctx[s, :, lanes]
                 )
@@ -1202,6 +1285,7 @@
                     values = jnp.where(wide_left, parts[1, :, lanes], values)
                 parts[0, :, lanes] = keys
                 parts[1, :, lanes] = values
+                fire_in(s, 9 + head, 4)
 
         def pack(t, carry):
             rows = block_rows(t, shard)
@@ -1218,25 +1302,87 @@
 
         s_tok.start(s, part)
 
+        fire_in(s, 12, 4)
+
     each(attention_back)
-    advance(first_sums, 4)
-    advance(second_sums, 1)
+    small_step(1) if hops else None
 
     x_copy().wait()
 
     def qkv_weights(j, carry):
         colsj = pl.ds(pl.multiple_of(j * step_w, step_w), step_w)
-        out = tn(v["h"][:, :, :, colsj].reshape(tokens, step_w), dyk[...].reshape(tokens, -1))
-        big["qkv"][block_rows(j, step_w), :] = out.astype(BF16)
+        out = tn(v.h[:, :, :, colsj].reshape(tokens, step_w), dyk[...].reshape(tokens, -1))
+        big.qkv[block_rows(j, step_w), :] = out.astype(BF16)
         return carry
 
     lax.fori_loop(0, width // step_w, qkv_weights, 0)
-    big["out"][...] = tn(
-        v["ctx"][...].reshape(tokens, -1), v["mid"][...].reshape(tokens, width)
+    big.out[...] = tn(
+        v.ctx[...].reshape(tokens, -1), v.mid[...].reshape(tokens, width)
     ).astype(BF16)
-    advance(third_sums, 0)
-    if hops:
-        small_step(1)
+    fire(17)
+
+    load("c").wait()
+
+    def gru_back(s):
+        def spread_out(t, carry):
+            rows = block_rows(t, LANE)
+            for tile in range(2):
+                ids = lax.broadcasted_iota(jnp.int32, (LANE, length), 0) + t * LANE
+                hot = (ids == pickr[s, tile : tile + 1, :]).astype(F32).astype(BF16)
+                drive[tile, rows, :] = nn(hot, gtok[s, :, pl.ds(tile * LANE, LANE)])
+            return carry
+
+        lax.fori_loop(0, total // LANE, spread_out, 0)
+        fire_in(s, 18, 3)
+        for tile in range(2):
+            decay_copy(s, tile).wait()
+        recur((False, True), decay, drive, drive, block_chars, back=True)
+        fire_in(s, 19, 3)
+        states_copy(s).wait()
+
+        @pl.when(s == 0)
+        def _():
+            gru_acc[...] = jnp.zeros_like(gru_acc)
+
+        def part(b, out):
+            def finish(t, sums):
+                inner = block_rows(t, LANE)
+                rows = pl.ds(pl.multiple_of(b * block_chars + t * LANE, LANE), LANE)
+                proj = nn(v.c[s, b, inner, :], wg[...])
+                new = []
+                for tile in range(2):
+                    colst = slice(tile * LANE, (tile + 1) * LANE)
+                    gate = jax.nn.sigmoid(proj[:, colst] + gate_bias[:, colst])
+                    cand = proj[:, (2 + tile) * LANE : (3 + tile) * LANE]
+                    flow = drive[tile, rows, :] * gate
+                    logit = flow * (cand - states[tile, rows, :].astype(F32))
+                    dproj[inner, pl.ds(tile * LANE, LANE)] = logit.astype(BF16)
+                    dproj[inner, pl.ds((2 + tile) * LANE, LANE)] = flow.astype(BF16)
+                    new.append(sums[tile] + jnp.sum(logit, axis=0, keepdims=True))
+                return tuple(new)
+
+            zero = jnp.zeros((1, LANE), F32)
+            sums = lax.fori_loop(0, block_chars // LANE, finish, (zero, zero))
+            for tile in range(2):
+                small[6, 0:1, pl.ds(tile * LANE, LANE)] += sums[tile]
+            out[...] = nt(dproj[...], wg[...])
+            gru_acc[...] += tn(v.c[s, b], dproj[...])
+
+        s_cout.start(s, part)
+
+        @pl.when(s + 1 < seqs)
+        def _():
+            states_copy(s + 1).start()
+            for tile in range(2):
+                decay_copy(s + 1, tile).start()
+
+        if seqs > 1:
+            pl.when(s == 0)(functools.partial(fire, 20))
+
+    each(gru_back)
+    big.gru[...] = gru_acc[...].astype(BF16)
+    small_step(2) if hops else None
+    fire(23)
 
     def last(s):
         res1[s] = res1[s] + s_tok.finish(s)
@@ -1248,33 +1394,26 @@
 
     def emit(name):
         return pltpu.make_async_copy(
-            big[name], grads_out[name], local.at[spare + 4 + 3 * seqs + GRADS.index(name)]
+            getattr(big, name), grads_out[name], local.at[spare + 4 + 3 * seqs + GRADS.index(name)]
         )
 
     if inside:
-        small_step(2)
-        advance(second_sums, 2)
-        advance(first_sums, 5)
-        advance(third_sums, 1)
+        fire(24)
         small_step(3)
-        advance(second_sums, 3)
-        advance(third_sums, 2)
-        advance(first_sums, 6)
+        fire(25)
         small_step(4)
-        advance(second_sums, 4)
-        advance(third_sums, 3)
+        fire(26)
         small_step(5)
-        advance(second_sums, 5)
-        advance(third_sums, 4)
-        advance(second_sums, 6)
-        advance(third_sums, 5)
-        advance(third_sums, 6)
+        fire(27)
+        assert all(count == Reduce.steps for count in fired)
     else:
         for name in GRADS:
             emit(name).start()
         for name in GRADS:
             emit(name).wait()
     small_out[...] = small[len(hops)]
+    if not inside:
+        small_out[pl.ds(8, 8), :] = small[6, pl.ds(0, 8), :]
     each(lambda s: (out_copy(0, s).wait(), out_copy(1, s).wait()))
 
 
@@ -1292,21 +1431,21 @@
     shapes = [(saved[n].shape, saved[n].dtype) for n in names]
     grads = {
         "merge": (2 * channels, width), "conv": (2 * width, packed),
-        "down": (win.shape[1], width), "in": (width, win.shape[1]),
+        "down": (win.shape[1], width), "win": (width, win.shape[1]),
         "gru": (char_width, 4 * LANE), "out": (cols, width), "qkv": (width, wq.shape[1]),
     }
     pad = (seqs, 3, shard, width)
     cpad = (seqs, 3, length, 2 * LANE)
     scratch = shapes + [
         (saved["p"].shape, BF16),
+        ((2, total, LANE), BF16),
         ((2, total, LANE), F32),
-        ((2, total + 16, LANE), F32),
         ((2, total, LANE), F32),
         ((length + 16, wm.shape[0]), F32),
         ((seqs, length, packed), BF16),
         ((seqs, 4, shard, width), BF16),
         ((seqs, length, 2 * LANE), BF16),
-        ((total, 4 * LANE), BF16),
+        ((block_chars, 4 * LANE), BF16),
         ((char_width, 4 * LANE), F32),
         ((seqs, shard, width), F32),
         ((seqs, shard, width), F32),
@@ -1315,9 +1454,12 @@
         (pad, BF16), (pad, BF16), ((seqs, shard, width), F32), ((shard, width), F32),
         (cpad, BF16), (cpad, BF16), ((seqs, length, 2 * LANE), F32), ((length, 2 * LANE), F32),
     ]
-    scratch += [((rows * 7 // 8 if dp_size == 8 else 16, last), BF16) for rows, last in grads.values()]
+    for name, (rows, last) in grads.items():
+        head = HEADS_OF[name]
+        landing = Reduce.landing_rows(head, True) + Reduce.landing_rows(rows - head, False)
+        scratch.append(((landing if dp_size == 8 else 16, last), BF16))
     scratch += [(shape, BF16) for shape in grads.values()]
-    scratch += [((6, 16, width), F32), ((6, 16, width), F32)]
+    scratch += [((7, 16, width), F32), ((5, 16, width), F32)]
     anyspace = pl.BlockSpec(memory_space=pl.ANY)
     vmem = pl.BlockSpec(memory_space=pltpu.VMEM)
     ins = saved_in + list(weights) + [small["gain"], small["pickr"], small["edges"], saved["norm_grads"]]
@@ -1332,8 +1474,8 @@
         + [
             pltpu.SemaphoreType.DMA((32 * seqs,)),
             pltpu.SemaphoreType.DMA((32 * seqs,)),
-            pltpu.SemaphoreType.DMA((72,)),
-            pltpu.SemaphoreType.DMA((72,)),
+            pltpu.SemaphoreType.DMA((160,)),
+            pltpu.SemaphoreType.DMA((160,)),
             pltpu.SemaphoreType.DMA((40,)),
             pltpu.SemaphoreType.DMA((12,)),
         ],
@@ -1395,8 +1537,17 @@
     layouts = [layout(doc_lengths[i], token_chars[i], char_total) for i in range(micro_count)]
     stacked_layout = [jnp.stack(parts) for parts in zip(*layouts)]
     segment, first_char, last_char, keep_forward, keep_backward, prev_ok, next_ok = stacked_layout
-    keep = jnp.stack([keep_forward, keep_backward], axis=2)
+    block_chars = characters.shape[1]
+    steps = block_chars // 8
+
+    def reorder(rows):
+        split = rows.reshape(micro_count, -1, 8, steps, rows.shape[-1])
+        return jnp.swapaxes(split, 2, 3).reshape(rows.shape)
+
+    keep = reorder(jnp.stack([keep_forward, keep_backward], axis=2))
     picks = jnp.stack([last_char, first_char], axis=2)
+    inner = picks % block_chars
+    picks = picks - inner + inner % steps * 8 + inner // steps
     zero = jnp.zeros_like(prev_ok[:, :1])
     small = dict(
         gain=norm_gain, bias=norm_bias, cot_t=token_cot, cot_c=char_cot,
@@ -1414,7 +1565,7 @@
         heads=heads_here, units=units_here, channels=merge_here,
     )
     weights = (wq, wout, w_in, w_down, gru_matrix, gru_bias, wc, wm)
-    fw = forward_call(tokens, characters, weights, small)
+    fw = forward_call(tokens, reorder(characters), weights, small)
     dp_size = lax.axis_size("dp")
     bw = backward_call(fw, weights, small, dp_size)
     rows = bw["small"]
@@ -1424,22 +1575,26 @@
         grads, gate_row = lax.psum((grads, gate_row), "dp")
         rows = lax.psum(rows, ("dp", "tensor"))
     grads = {name: value.astype(F32) for name, value in grads.items()}
-    packed = 3 * merge_here
-    grad_conv = grads["conv"][:, :packed].reshape(2 * model_width, 3, merge_here)
+    grad_conv = jnp.stack(
+        [grads["conv"][:, k * merge_here : (k + 1) * merge_here] for k in range(3)], axis=0
+    )
     grad_merge = grads["merge"].reshape(2, merge_here, model_width)
     grad_gru = grads["gru"].reshape(char_width, 2, 2, LANE)[..., :units_here]
+    grad_chars = jnp.swapaxes(
+        bw["grad_chars"].reshape(micro_count, steps, 8, char_width), 1, 2
+    )
     return (
         fw["token_out"],
         fw["char_out"],
         bw["grad_tokens"],
-        bw["grad_chars"],
+        grad_chars.reshape(bw["grad_chars"].shape),
         grads["qkv"][:, : 3 * head_cols].reshape(model_width, 3, head_cols),
         grads["out"][:head_cols],
-        grads["in"],
+        grads["win"],
         grads["down"],
         jnp.swapaxes(grad_gru, 1, 2),
         gate_row.reshape(2, LANE)[:, :units_here],
-        jnp.swapaxes(grad_conv, 0, 1),
+        grad_conv,
         jnp.swapaxes(grad_merge, 0, 1),
         jnp.concatenate([rows[4:6], rows[0:2]], axis=0),
         jnp.concatenate([rows[6:8], rows[2:4]], axis=0),

time: 424 us -> 354 us (0.83)
  Pallas kernels: 367 us -> 300 us
    pallas_call x1, Pallas kernels: 253 us -> 198 us  [backward_call(): pl.pallas_call(functools.partial(backward_kernel, small['units'], channel...]
    pallas_call x1, Pallas kernels: 114 us -> 102 us  [forward_call(): pl.pallas_call(functools.partial(forward_kernel, small['units'], small['c...]
    unnamed x31 -> x35, local copies, waits for them, and re-layouts: 5.59 us -> 10.3 us
where the time goes in v4:
time: 354 us
  Pallas kernels  300 us (85%)
  local copies, waits for them, and re-layouts  34.9 us (10%)
  other arithmetic  17.9 us (5%)
    pallas_call x1, Pallas kernels, backward_call(): pl.pallas_call(functools.partial(backward_kernel, small['units'], channel...  198 us
    pallas_call x1, Pallas kernels, forward_call(): pl.pallas_call(functools.partial(forward_kernel, small['units'], small['c...  102 us
    unnamed x35, local copies, waits for them, and re-layouts  10.3 us

profile of v4, /device:TPU:0, one launch (start us, length us, event | category | flops | bytes accessed | tf_op | source)
XLA Modules:
  0.0 353.6 jit_solution(11532498721402534052)
XLA Ops:
  0.7 1.3 pad.33
  1.9 0.8 slice_bitcast_fusion.4
  2.7 0.1 select_reduce_fusion.6
  2.8 0.8 fusion.18
  3.6 0.1 fusion.7
  3.7 0.1 fusion.6
  4.0 0.8 fusion.20
  4.7 0.1 fusion.9
  4.8 0.1 fusion.8
  5.1 0.6 broadcast_in_dim.122.segr
  5.7 0.8 fusion.24
  6.5 0.2 select_reduce_fusion.2
  6.7 0.2 select_reduce_fusion
  6.9 0.2 select_reduce_fusion.4
  7.1 0.2 select_reduce_fusion.1
  7.3 0.1 fusion
  7.4 0.1 fusion.1
  7.5 0.1 fusion.2
  7.6 0.1 fusion.3
  7.7 0.8 slice_subtract_fusion.1
  8.8 0.7 fusion.27.refs_29_
  9.6 1.1 copy.136
  10.7 0.3 pad.32.clone
  10.9 0.8 reshape.264.wg.refs_24_
  11.7 0.8 pad.31.wout.refs_21_
  12.5 1.0 copy.129.pickc
  13.5 0.2 copy.126
  13.8 0.2 copy.124
  14.0 0.2 copy.127
  14.3 0.2 copy.125
  14.5 1.3 pad_maximum_fusion.2.edges.refs_30_
  15.8 1.0 copy.128.segc
  16.8 1.1 copy.143
  17.9 0.9 pad.36.wm.refs_27_
  18.9 0.6 copy.118
  19.5 1.0 pad.30.wq.refs_20_
  20.6 2.7 copy.120
  23.3 0.2 pad_slice_fusion.1
  23.6 0.1 pad.35
  23.7 1.6 pad_maximum_fusion.1.wc.refs_26_
  25.3 2.0 copy.123
  27.3 101.8 %shard_map.263 = (bf16[2,128,768]{2,1,0:T(8,128)(2,1)}, bf16[2,128,768]{2,1,0:T(8,128)(2,1)}, bf16[2,4,128,768]{3,2,1,0:T(8,128)(2,1)}, bf16[2,4,512,256]{3,2,1,...) custom-call(bf16[2,128,768]{2,1,0:T(8,128)(2,1)} %tokens.1, ...), custom_call_target="tpu_custom_call" | custom-call | tf_op jit(solution)/shard_map/pallas_call | solution.py:673
  129.1 198.1 %shard_map.264 = (f32[2,128,768]{2,1,0:T(8,128)}, f32[2,512,256]{2,1,0:T(8,128)}, bf16[384,768]{1,0:T(8,128)(2,1)}, bf16[1536,640]{1,0:T(8,128)(2,1)}, bf16[768,...) custom-call(bf16[2,3,128,512]{3,2,1,0:T(8,128)(2,1)} %get-tuple-elem, ...), custom_call_target="tpu_custom_call" | custom-call | tf_op jit(solution)/shard_map/pallas_call | solution.py:1466
  327.2 2.6 copy.130
  329.8 0.6 slice.77
  330.4 0.6 pad_maximum_fusion.4
  331.0 0.6 pad_maximum_fusion.3
  331.7 0.1 copy.135
  331.8 0.8 convert_bitcast_fusion
  332.6 0.9 slice_convert_fusion.1
  333.5 1.6 copy.141
  335.1 1.3 slice_convert_fusion
  336.4 1.7 copy.131
  338.1 1.6 convert_element_type.135
  339.7 0.1 copy-done.1
  339.8 1.6 convert_element_type.136
  341.4 0.8 copy-done
  342.2 0.3 convert_element_type.137
  342.5 0.6 slice_bitcast_fusion.2
  343.1 2.4 pad_maximum_fusion
  345.5 5.7 %copy.134 = f32[3,1536,192]{1,2,0:T(8,128)} copy(f32[3,1536,192]{2,1,0:T(8,128)} %pad_maximum_fusion) | data formatting | bytes 7077888
  351.2 0.7 copy.147
  352.0 0.7 copy.148
  352.7 0.9 copy.149
  (59 shorter events, 1.1 us)
Async XLA Ops:
  0.6 11.1 %copy-start.10 = (bf16[192,768]{1,0:T(8,128)(2,1)S(1)}, bf16[192,768]{1,0:T(8,128)(2,1)}, u32[]{:S(2)}) copy-start(bf16[192,768]{1,0:T(8,128)(2,1)} %param.21) | copy-start | bytes 884740
  14.2 2.6 copy-start.7
  14.5 3.4 copy-start.6
  15.8 3.1 copy-start.3
  327.2 2.6 copy-start.13
  327.2 4.4 %copy-start.11 = (bf16[256,512]{1,0:T(8,128)(2,1)S(1)}, bf16[256,512]{1,0:T(8,128)(2,1)}, u32[]{:S(2)}) copy-start(bf16[256,512]{1,0:T(8,128)(2,1)} %get-tuple-element.76) | copy-start | bytes 786436
  327.2 5.4 %copy-start.12 = (bf16[256,768]{1,0:T(8,128)(2,1)S(1)}, bf16[256,768]{1,0:T(8,128)(2,1)}, u32[]{:S(2)}) copy-start(bf16[256,768]{1,0:T(8,128)(2,1)} %get-tuple-element.73) | copy-start | bytes 1179652
  327.2 6.3 %copy-start.5 = (bf16[384,768]{1,0:T(8,128)(2,1)S(1)}, bf16[384,768]{1,0:T(8,128)(2,1)}, u32[]{:S(2)}) copy-start(bf16[384,768]{1,0:T(8,128)(2,1)} %get-tuple-element.79) | copy-start | bytes 1769476
  336.4 1.7 copy-start.2
  338.1 1.7 copy-start.1
  339.8 2.4 copy-start
  345.5 5.7 %copy-start.9 = (bf16[2,128,768]{2,1,0:T(8,128)(2,1)S(1)}, bf16[2,128,768]{2,1,0:T(8,128)(2,1)}, u32[]{:S(2)}) copy-start(bf16[2,128,768]{2,1,0:T(8,128)(2,1)} %get-tuple-element.213) | copy-start | bytes 1179652
  345.5 6.4 %copy-start.8 = (bf16[2,128,768]{2,1,0:T(8,128)(2,1)S(1)}, bf16[2,128,768]{2,1,0:T(8,128)(2,1)}, u32[]{:S(2)}) copy-start(bf16[2,128,768]{2,1,0:T(8,128)(2,1)} %get-tuple-element.214) | copy-start | bytes 1179652
  351.2 1.5 copy-start.4

commit v5 on v4

--- a/solution.py
+++ b/solution.py
@@ -902,36 +902,51 @@
     "h", "p", "qkv", "ctx", "x", "c", "states", "decay",
 )
 GRADS = ("merge", "conv", "down", "win", "gru", "out", "qkv")
-HEADS_OF = dict(zip(GRADS, (0, 1024, 768, 256, 0, 0, 512)))
+PIECES = (
+    (0, 384, True),
+    (1, 640, False),
+    (1, 768, True),
+    (1, 128, True),
+    (2, 384, True),
+    (2, 384, True),
+    (3, 768, True),
+    (4, 128, True),
+    (4, 128, True),
+    (5, 256, False),
+    (6, 512, True),
+    (6, 256, False),
+)
 SCHEDULE = (
-    (0, 10, 20,),
     (),
-    (1, 21,),
-    (2, 11,),
-    (22,),
-    (30, 3,),
+    (0, 10, 20, 30,),
+    (),
+    (11,),
+    (1,),
+    (),
     (40, 50, 12,),
+    (60, 2,),
+    (21,),
+    (31,),
+    (13,),
+    (3, 22, 41, 32,),
+    (4,),
+    (51, 23, 42, 33,),
+    (5,),
+    (52, 24,),
+    (43, 34, 6, 61, 53, 14,),
+    (25, 44, 35, 7,),
+    (15, 62,),
+    (90, 100, 110, 54, 26, 45, 36,),
+    (8, 16,),
     (),
-    (23,),
-    (),
-    (51,),
-    (13, 31,),
-    (4,),
-    (52, 41,),
-    (24, 14, 5,),
-    (32,),
-    (25,),
-    (70, 80, 90, 53, 15, 42, 6,),
-    (33, 71, 26,),
-    (91, 43, 16,),
-    (81, 34, 7, 54, 72, 92, 27, 44,),
-    (82, 17,),
-    (55, 73, 35, 93,),
-    (60, 83, 8, 28,),
-    (45, 61,),
-    (84, 56, 18, 62, 74, 36,),
-    (94, 46, 85, 63, 75, 95,),
-    (64, 57, 65, 37, 47, 86, 76, 96, 58, 66, 87, 38, 77, 97, 67, 48, 78, 98, 68, 88,),
+    (63, 91, 27, 111, 101, 37, 46, 55, 17,),
+    (64,),
+    (47, 92, 112,),
+    (70, 80, 56, 102, 18, 28, 38, 65, 93,),
+    (113, 103, 57, 48,),
+    (71, 81, 66, 94, 104, 114, 72,),
+    (82, 67, 73, 83, 105, 58, 95,),
+    (74, 115, 84, 106, 96, 75, 116, 85, 107, 97, 76, 68, 117, 86, 98, 77, 118, 87, 108, 78, 88,),
 )
 
 
@@ -949,7 +964,7 @@
      stage, got, held, temp, cstage, cgot, cheld, ctemp) = take(22)
     land = dict(zip(GRADS, take(len(GRADS))))
     big = SimpleNamespace(**dict(zip(GRADS, take(len(GRADS)))))
-    small, small_land, send, recv, dsend, drecv, local, marks = take(8)
+    small, small_land, send, recv, dsend, drecv, local, marks, credit = take(9)
 
     seqs, shard, width = grad_tokens.shape
     length = 4 * shard
@@ -1075,65 +1090,17 @@
 
         s_mid.start(s, mid_part)
 
-        def char_part(b, out):
-            first = pl.multiple_of(width + b * 2 * LANE, 2 * LANE)
-            out[...] = nt(dyk[s], wc[pl.ds(first, 2 * LANE), :])
-            out[block_rows(me, shard), :] += v.res4[s, b].astype(F32)
-
-        s_chr.start(s, char_part)
-
     each(merge_back)
-    for name in ("mg", "mid", "st"):
-        load(name).wait()
-
-    tokens = seqs * length
-    half_w = width
-    for j in range(pieces):
-        right = jnp.concatenate(
-            [pb[s, t * pieces + j] for s in range(seqs) for t in range(4)], axis=0
+    sums, marks_at = [], {}
+    for which, height, x_first in PIECES if inside else ():
+        name = GRADS[which]
+        first, at = marks_at.get(name, (0, 0))
+        sums.append(
+            Reduce(
+                plane, getattr(big, name), grads_out[name], land[name], first, at, height, x_first
+            )
         )
-        out = tn(v.mg[...].reshape(tokens, -1), right)[:channels].astype(BF16)
-        at = 0
-        while at < length:
-            part, inside_at = divmod(j * length + at, half_w)
-            size = min(length - at, half_w - inside_at)
-            big.merge[pl.ds(part * channels, channels), pl.ds(inside_at, size)] = out[
-                :, at : at + size
-            ]
-            at += size
-    step_w = 2 * LANE
-
-    def conv_mid(j, carry):
-        colsj = pl.ds(pl.multiple_of(j * step_w, step_w), step_w)
-        out = tn(v.mid[:, :, :, colsj].reshape(tokens, step_w), dyk[...].reshape(tokens, -1))
-        big.conv[block_rows(j, step_w), :] = out.astype(BF16)
-        return carry
-
-    lax.fori_loop(0, width // step_w, conv_mid, 0)
-
-    def conv_char(t, carry):
-        out = tn(v.st[:, t].reshape(tokens, 2 * LANE), dyk[...].reshape(tokens, -1))
-        for d in range(2):
-            first = pl.multiple_of(width + d * 4 * units + t * units, 16)
-            big.conv[pl.ds(first, units), :] = out[d * LANE : d * LANE + units].astype(BF16)
-        return carry
-
-    lax.fori_loop(0, 4, conv_char, 0)
-    p_copy().start()
-
-    sums = []
-    for name in GRADS if inside else ():
-        height, at = getattr(big, name).shape[0], 0
-        pieces_of = ((0, HEADS_OF[name], True), (HEADS_OF[name], height - HEADS_OF[name], False))
-        for first, size, x_first in pieces_of:
-            if size:
-                sums.append(
-                    Reduce(
-                        plane, getattr(big, name), grads_out[name], land[name], first, at, size,
-                        x_first,
-                    )
-                )
-                at += Reduce.landing_rows(size, x_first)
+        marks_at[name] = (first + height, at + Reduce.landing_rows(height, x_first))
     fired = [0] * len(sums)
 
     def fire(hook):
@@ -1146,7 +1113,45 @@
         for k in range(2):
             pl.when(seq == k)(functools.partial(fire, hook + k * stride))
 
-    fire(0)
+    tokens = seqs * length
+    step_w = 2 * LANE
+
+    def merge_weights():
+        for name in ("mg", "mid", "st"):
+            load(name).wait()
+
+        half_w = width
+        for j in range(pieces):
+            right = jnp.concatenate(
+                [pb[s, t * pieces + j] for s in range(seqs) for t in range(4)], axis=0
+            )
+            out = tn(v.mg[...].reshape(tokens, -1), right)[:channels].astype(BF16)
+            at = 0
+            while at < length:
+                part, inside_at = divmod(j * length + at, half_w)
+                size = min(length - at, half_w - inside_at)
+                big.merge[pl.ds(part * channels, channels), pl.ds(inside_at, size)] = out[
+                    :, at : at + size
+                ]
+                at += size
+        def conv_mid(j, carry):
+            colsj = pl.ds(pl.multiple_of(j * step_w, step_w), step_w)
+            out = tn(v.mid[:, :, :, colsj].reshape(tokens, step_w), dyk[...].reshape(tokens, -1))
+            big.conv[block_rows(j, step_w), :] = out.astype(BF16)
+            return carry
+
+        lax.fori_loop(0, width // step_w, conv_mid, 0)
+
+        def conv_char(t, carry):
+            out = tn(v.st[:, t].reshape(tokens, 2 * LANE), dyk[...].reshape(tokens, -1))
+            for d in range(2):
+                first = pl.multiple_of(width + d * 4 * units + t * units, 16)
+                big.conv[pl.ds(first, units), :] = out[d * LANE : d * LANE + units].astype(BF16)
+            return carry
+
+        lax.fori_loop(0, 4, conv_char, 0)
+        p_copy().start()
+        fire(1)
 
     def second_back(s):
         incoming = v.res3[s] + s_mid.finish(s)
@@ -1156,9 +1161,9 @@
         spread = v.scale[s, 1][:, 0:1]
         res2[s] = normalize_back(unit, spread, incoming * gain[1:2])
         fg[s, me] = res2[s].astype(BF16)
-        gtok[s] = s_chr.finish(s).astype(BF16)
         gf.start(s)
-        fire_in(s, 1, 1)
+        fire_in(s, 0, 2)
+        pl.when(s == 0)(merge_weights)
 
     for name in ("res3", "unit1", "scale"):
         load(name).wait()
@@ -1180,26 +1185,28 @@
 
     each(ffn_back)
 
-    def ffn_weights(j, carry):
-        colsj = pl.ds(pl.multiple_of(j * step_w, step_w), step_w)
-        out = tn(v.act[:, :, :, colsj].reshape(tokens, step_w), fg[...].reshape(tokens, width))
-        big.down[block_rows(j, step_w), :] = out.astype(BF16)
-        return carry
-
-    lax.fori_loop(0, big.down.shape[0] // step_w, ffn_weights, 0)
-    fire(5)
-
-    def in_weights(j, carry):
-        colsj = pl.ds(pl.multiple_of(j * step_w, step_w), step_w)
-        out = tn(
-            v.h[:, :, :, colsj].reshape(tokens, step_w), v.dact[...].reshape(tokens, -1)
-        )
-        big.win[block_rows(j, step_w), :] = out.astype(BF16)
-        return carry
-
-    lax.fori_loop(0, width // step_w, in_weights, 0)
-    x_copy().start()
-    fire(6)
+    def all_ffn_weights():
+        def ffn_weights(j, carry):
+            colsj = pl.ds(pl.multiple_of(j * step_w, step_w), step_w)
+            out = tn(v.act[:, :, :, colsj].reshape(tokens, step_w), fg[...].reshape(tokens, width))
+            big.down[block_rows(j, step_w), :] = out.astype(BF16)
+            return carry
+
+        lax.fori_loop(0, big.down.shape[0] // step_w, ffn_weights, 0)
+        fire(6)
+
+        def in_weights(j, carry):
+            colsj = pl.ds(pl.multiple_of(j * step_w, step_w), step_w)
+            out = tn(
+                v.h[:, :, :, colsj].reshape(tokens, step_w), v.dact[...].reshape(tokens, -1)
+            )
+            big.win[block_rows(j, step_w), :] = out.astype(BF16)
+            return carry
+
+        lax.fori_loop(0, width // step_w, in_weights, 0)
+        x_copy().start()
+        fire(7)
+
     load("unit0").wait()
 
     def first_back(s):
@@ -1211,9 +1218,21 @@
         res1[s] = normalize_back(unit, spread, incoming * gain[0:1])
         v.mid[s, me] = res1[s].astype(BF16)
         ga.start(s)
-        fire_in(s, 7, 1)
+        fire_in(s, 5, 3)
+        pl.when(s == 0)(all_ffn_weights)
 
     each(first_back)
+
+    def chars_back(s):
+        def char_part(b, out):
+            first = pl.multiple_of(width + b * 2 * LANE, 2 * LANE)
+            out[...] = nt(dyk[s], wc[pl.ds(first, 2 * LANE), :])
+            out[block_rows(me, shard), :] += v.res4[s, b].astype(F32)
+
+        s_chr.start(s, char_part)
+        fire_in(s, 9, 1)
+
+    each(chars_back)
     hops = [("t", g.pair), ("t", g.far)] + ([("d", k) for k in range(3)] if inside else [])
     slots_t, slots_d = g.slots(2), plane.take(3)
 
@@ -1285,7 +1304,7 @@
                     values = jnp.where(wide_left, parts[1, :, lanes], values)
                 parts[0, :, lanes] = keys
                 parts[1, :, lanes] = values
-                fire_in(s, 9 + head, 4)
+                fire_in(s, 11 + head, 4)
 
         def pack(t, carry):
             rows = block_rows(t, shard)
@@ -1302,7 +1321,7 @@
 
         s_tok.start(s, part)
 
-        fire_in(s, 12, 4)
+        fire_in(s, 14, 4)
 
     each(attention_back)
     small_step(1) if hops else None
@@ -1319,25 +1338,31 @@
     big.out[...] = tn(
         v.ctx[...].reshape(tokens, -1), v.mid[...].reshape(tokens, width)
     ).astype(BF16)
-    fire(17)
+    fire(19)
 
     load("c").wait()
 
     def gru_back(s):
+        gtok[...] = s_chr.finish(s).astype(BF16)
+        for peer in (g.pair, g.far):
+            pl.semaphore_signal(
+                credit.at[s], inc=1, device_id={"tensor": peer},
+                device_id_type=pl.DeviceIdType.MESH,
+            )
         def spread_out(t, carry):
             rows = block_rows(t, LANE)
             for tile in range(2):
                 ids = lax.broadcasted_iota(jnp.int32, (LANE, length), 0) + t * LANE
                 hot = (ids == pickr[s, tile : tile + 1, :]).astype(F32).astype(BF16)
-                drive[tile, rows, :] = nn(hot, gtok[s, :, pl.ds(tile * LANE, LANE)])
+                drive[tile, rows, :] = nn(hot, gtok[:, pl.ds(tile * LANE, LANE)])
             return carry
 
         lax.fori_loop(0, total // LANE, spread_out, 0)
-        fire_in(s, 18, 3)
+        fire_in(s, 20, 3)
         for tile in range(2):
             decay_copy(s, tile).wait()
         recur((False, True), decay, drive, drive, block_chars, back=True)
-        fire_in(s, 19, 3)
+        fire_in(s, 21, 3)
         states_copy(s).wait()
 
         @pl.when(s == 0)
@@ -1368,6 +1393,7 @@
             out[...] = nt(dproj[...], wg[...])
             gru_acc[...] += tn(v.c[s, b], dproj[...])
 
+        pl.semaphore_wait(credit.at[s], 2)
         s_cout.start(s, part)
 
         @pl.when(s + 1 < seqs)
@@ -1377,12 +1403,12 @@
                 decay_copy(s + 1, tile).start()
 
         if seqs > 1:
-            pl.when(s == 0)(functools.partial(fire, 20))
+            pl.when(s == 0)(functools.partial(fire, 22))
 
     each(gru_back)
     big.gru[...] = gru_acc[...].astype(BF16)
     small_step(2) if hops else None
-    fire(23)
+    fire(25)
 
     def last(s):
         res1[s] = res1[s] + s_tok.finish(s)
@@ -1398,13 +1424,13 @@
         )
 
     if inside:
-        fire(24)
+        fire(26)
         small_step(3)
-        fire(25)
+        fire(27)
         small_step(4)
-        fire(26)
+        fire(28)
         small_step(5)
-        fire(27)
+        fire(29)
         assert all(count == Reduce.steps for count in fired)
     else:
         for name in GRADS:
@@ -1444,7 +1470,7 @@
         ((length + 16, wm.shape[0]), F32),
         ((seqs, length, packed), BF16),
         ((seqs, 4, shard, width), BF16),
-        ((seqs, length, 2 * LANE), BF16),
+        ((length, 2 * LANE), BF16),
         ((block_chars, 4 * LANE), BF16),
         ((char_width, 4 * LANE), F32),
         ((seqs, shard, width), F32),
@@ -1454,10 +1480,9 @@
         (pad, BF16), (pad, BF16), ((seqs, shard, width), F32), ((shard, width), F32),
         (cpad, BF16), (cpad, BF16), ((seqs, length, 2 * LANE), F32), ((length, 2 * LANE), F32),
     ]
-    for name, (rows, last) in grads.items():
-        head = HEADS_OF[name]
-        landing = Reduce.landing_rows(head, True) + Reduce.landing_rows(rows - head, False)
-        scratch.append(((landing if dp_size == 8 else 16, last), BF16))
+    for which, name in enumerate(GRADS):
+        landing = sum(Reduce.landing_rows(n, way) for k, n, way in PIECES if k == which)
+        scratch.append(((landing if dp_size == 8 else 16, grads[name][1]), BF16))
     scratch += [(shape, BF16) for shape in grads.values()]
     scratch += [((7, 16, width), F32), ((5, 16, width), F32)]
     anyspace = pl.BlockSpec(memory_space=pl.ANY)
@@ -1474,10 +1499,11 @@
         + [
             pltpu.SemaphoreType.DMA((32 * seqs,)),
             pltpu.SemaphoreType.DMA((32 * seqs,)),
-            pltpu.SemaphoreType.DMA((160,)),
-            pltpu.SemaphoreType.DMA((160,)),
+            pltpu.SemaphoreType.DMA((14 * len(PIECES) + 4,)),
+            pltpu.SemaphoreType.DMA((14 * len(PIECES) + 4,)),
             pltpu.SemaphoreType.DMA((40,)),
-            pltpu.SemaphoreType.DMA((12,)),
+            pltpu.SemaphoreType.DMA((len(PIECES),)),
+            pltpu.SemaphoreType.REGULAR((seqs,)),
         ],
         compiler_params=pltpu.CompilerParams(
             collective_id=1, has_side_effects=True, vmem_limit_bytes=63 * MIB

time: 354 us -> 331 us (0.935)
  Pallas kernels: 300 us -> 277 us
    pallas_call x1, Pallas kernels: 198 us -> 175 us  [backward_call(): pl.pallas_call(functools.partial(backward_kernel, small['units'], channel...]
where the time goes in v5:
time: 331 us; the launch traced here: 330 us
  Pallas kernels  277 us (84%)
  local copies, waits for them, and re-layouts  34.9 us (11%)
  other arithmetic  17.9 us (5%)
    pallas_call x1, Pallas kernels, backward_call(): pl.pallas_call(functools.partial(backward_kernel, small['units'], channel...  175 us
    pallas_call x1, Pallas kernels, forward_call(): pl.pallas_call(functools.partial(forward_kernel, small['units'], small['c...  102 us
    unnamed x35, local copies, waits for them, and re-layouts  10.3 us

profile of v5, /device:TPU:0, one launch (start us, length us, event | category | flops | bytes accessed | tf_op | source)
XLA Modules:
  0.0 330.3 jit_solution(13070169732625671442)
XLA Ops:
  0.7 1.3 pad.33
  1.9 0.8 slice_bitcast_fusion.4
  2.7 0.1 select_reduce_fusion.6
  2.8 0.8 fusion.18
  3.6 0.1 fusion.7
  3.7 0.1 fusion.6
  4.0 0.8 fusion.20
  4.7 0.1 fusion.9
  4.8 0.1 fusion.8
  5.1 0.6 broadcast_in_dim.122.segr
  5.7 0.8 fusion.24
  6.5 0.2 select_reduce_fusion.2
  6.7 0.2 select_reduce_fusion
  6.9 0.2 select_reduce_fusion.4
  7.1 0.2 select_reduce_fusion.1
  7.3 0.1 fusion
  7.4 0.1 fusion.1
  7.5 0.1 fusion.2
  7.6 0.1 fusion.3
  7.7 0.8 slice_subtract_fusion.1
  8.8 0.7 fusion.27.refs_29_
  9.6 1.1 copy.136
  10.7 0.3 pad.32.clone
  10.9 0.8 reshape.264.wg.refs_24_
  11.7 0.8 pad.31.wout.refs_21_
  12.5 1.0 copy.129.pickc
  13.5 0.2 copy.126
  13.8 0.2 copy.124
  14.0 0.2 copy.127
  14.3 0.2 copy.125
  14.5 1.3 pad_maximum_fusion.2.edges.refs_30_
  15.8 1.0 copy.128.segc
  16.8 1.1 copy.143
  17.9 0.9 pad.36.wm.refs_27_
  18.9 0.6 copy.118
  19.5 1.0 pad.30.wq.refs_20_
  20.6 2.7 copy.120
  23.3 0.2 pad_slice_fusion.1
  23.6 0.1 pad.35
  23.7 1.6 pad_maximum_fusion.1.wc.refs_26_
  25.3 2.0 copy.123
  27.3 101.8 %shard_map.263 = (bf16[2,128,768]{2,1,0:T(8,128)(2,1)}, bf16[2,128,768]{2,1,0:T(8,128)(2,1)}, bf16[2,4,128,768]{3,2,1,0:T(8,128)(2,1)}, bf16[2,4,512,256]{3,2,1,...) custom-call(bf16[2,128,768]{2,1,0:T(8,128)(2,1)} %tokens.1, ...), custom_call_target="tpu_custom_call" | custom-call | tf_op jit(solution)/shard_map/pallas_call | solution.py:673
  129.1 174.8 %shard_map.264 = (f32[2,128,768]{2,1,0:T(8,128)}, f32[2,512,256]{2,1,0:T(8,128)}, bf16[384,768]{1,0:T(8,128)(2,1)}, bf16[1536,640]{1,0:T(8,128)(2,1)}, bf16[768,...) custom-call(bf16[2,3,128,512]{3,2,1,0:T(8,128)(2,1)} %get-tuple-elem, ...), custom_call_target="tpu_custom_call" | custom-call | tf_op jit(solution)/shard_map/pallas_call | solution.py:1491
  303.9 2.6 copy.130
  306.5 0.6 slice.77
  307.1 0.6 pad_maximum_fusion.4
  307.7 0.6 pad_maximum_fusion.3
  308.4 0.1 copy.135
  308.5 0.8 convert_bitcast_fusion
  309.3 0.9 slice_convert_fusion.1
  310.2 1.6 copy.141
  311.8 1.3 slice_convert_fusion
  313.1 1.7 copy.131
  314.9 1.6 convert_element_type.135
  316.4 0.1 copy-done.1
  316.5 1.6 convert_element_type.136
  318.1 0.8 copy-done
  318.9 0.3 convert_element_type.137
  319.2 0.6 slice_bitcast_fusion.2
  319.8 2.4 pad_maximum_fusion
  322.2 5.7 %copy.134 = f32[3,1536,192]{1,2,0:T(8,128)} copy(f32[3,1536,192]{2,1,0:T(8,128)} %pad_maximum_fusion) | data formatting | bytes 7077888
  327.9 0.7 copy.147
  328.7 0.7 copy.148
  329.4 0.9 copy.149
  (59 shorter events, 1.1 us)
Async XLA Ops:
  0.6 11.1 %copy-start.10 = (bf16[192,768]{1,0:T(8,128)(2,1)S(1)}, bf16[192,768]{1,0:T(8,128)(2,1)}, u32[]{:S(2)}) copy-start(bf16[192,768]{1,0:T(8,128)(2,1)} %param.21) | copy-start | bytes 884740
  14.2 2.6 copy-start.7
  14.5 3.4 %copy-start.6 = (bf16[192,2,768]{2,1,0:T(2,128)(2,1)S(1)}, bf16[192,2,768]{2,1,0:T(2,128)(2,1)}, u32[]{:S(2)}) copy-start(bf16[192,2,768]{2,1,0:T(2,128)(2,1)} %param.27) | copy-start | bytes 1769476
  15.8 3.1 copy-start.3
  303.9 2.6 copy-start.13
  303.9 4.4 %copy-start.11 = (bf16[256,512]{1,0:T(8,128)(2,1)S(1)}, bf16[256,512]{1,0:T(8,128)(2,1)}, u32[]{:S(2)}) copy-start(bf16[256,512]{1,0:T(8,128)(2,1)} %get-tuple-element.76) | copy-start | bytes 786436
  303.9 5.4 %copy-start.12 = (bf16[256,768]{1,0:T(8,128)(2,1)S(1)}, bf16[256,768]{1,0:T(8,128)(2,1)}, u32[]{:S(2)}) copy-start(bf16[256,768]{1,0:T(8,128)(2,1)} %get-tuple-element.73) | copy-start | bytes 1179652
  303.9 6.3 %copy-start.5 = (bf16[384,768]{1,0:T(8,128)(2,1)S(1)}, bf16[384,768]{1,0:T(8,128)(2,1)}, u32[]{:S(2)}) copy-start(bf16[384,768]{1,0:T(8,128)(2,1)} %get-tuple-element.79) | copy-start | bytes 1769476
  313.1 1.7 copy-start.2
  314.8 1.7 copy-start.1
  316.5 2.4 copy-start
  322.2 5.7 %copy-start.9 = (bf16[2,128,768]{2,1,0:T(8,128)(2,1)S(1)}, bf16[2,128,768]{2,1,0:T(8,128)(2,1)}, u32[]{:S(2)}) copy-start(bf16[2,128,768]{2,1,0:T(8,128)(2,1)} %get-tuple-element.213) | copy-start | bytes 1179652
  322.2 6.4 %copy-start.8 = (bf16[2,128,768]{2,1,0:T(8,128)(2,1)S(1)}, bf16[2,128,768]{2,1,0:T(8,128)(2,1)}, u32[]{:S(2)}) copy-start(bf16[2,128,768]{2,1,0:T(8,128)(2,1)} %get-tuple-element.214) | copy-start | bytes 1179652
  327.9 1.5 copy-start.4

commit v6 on v5

--- a/solution.py
+++ b/solution.py
@@ -68,13 +68,6 @@
 VMEM = pl.BlockSpec(memory_space=pltpu.VMEM)
 
 
-def gru_weights(w_gru, gate_bias):
-    width, _, _, units = w_gru.shape
-    matrix = jnp.pad(jnp.swapaxes(w_gru, 1, 2), ((0, 0), (0, 0), (0, 0), (0, LANE - units)))
-    bias = jnp.pad(gate_bias, ((0, 0), (0, LANE - units)))
-    return matrix.reshape(width, 4 * LANE), bias.reshape(1, 2 * LANE)
-
-
 def nn(left, right):
     return jnp.dot(left, right, preferred_element_type=F32)
 
@@ -330,12 +323,14 @@
 
 
 def forward_kernel(
-    units, channels, tokens, chars, wq, wout, win, wdown, wg, gate_bias, wc, wm, gain, bias, cot_t, cot_c,
+    units, channels, tokens, chars, wq_in, wout_in, win, wdown, wg_in, gate_in, wc_in, wm, gain, bias,
+    cot_t, cot_c,
     segc, segr, pickc, keep, edges,
     token_out, char_out, o_x, o_c, o_qkv, o_p, o_ctx, o_h, o_act, o_dact, o_mid, o_st, o_mg,
-    o_dmg, o_states, o_decay, o_unit0, o_unit1, o_scale, o_res3, o_res4, o_branch, norm_grads,
+    o_dmg, o_states, o_decay, o_unit0, o_unit1, o_scale, o_res3, o_res4, o_branch,
+    o_wq, o_wout, o_wg, o_wc, norm_grads,
     x, c, qkv, p, ctx, h, act, dact, mid, st, mg, dmg, low_states, decays, unit0, unit1, scale, res3, res4, branch,
-    hidden, middle, outs_t, outs_c, states, drive, taps, perm,
+    wq, wout, wg, wc, hidden, middle, outs_t, outs_c, states, drive, taps, perm, gate_bias,
     stage, got, held, temp, send, recv, local,
 ):
     seqs, length = tokens.shape[0], segr.shape[2]
@@ -390,6 +385,36 @@
         lax.fori_loop(0, seqs, run, 0)
 
     each(lambda s: (own_x(s).start(), own_c(s).start()))
+    base = (2 + len(plan)) * seqs
+    rows_in = wq_in.shape[0]
+    fills = [
+        (wq_in, wq.at[pl.ds(0, rows_in), :]),
+        (wout_in, wout.at[pl.ds(0, wout_in.shape[0]), :]),
+        (wc_in.at[:, pl.ds(0, width)], wc.at[pl.ds(0, rows_in), pl.ds(0, width)]),
+    ]
+    for d in range(2):
+        for k in range(2):
+            fills.append((wg_in.at[d, k], wg.at[pl.ds((2 * k + d) * LANE, units), :]))
+    pieces = -(-rows_in // shard)
+    for j in range(pieces):
+        size = min(shard, rows_in - j * shard)
+        fills.append(
+            (
+                wc_in.at[pl.ds(j * shard, size), pl.ds(width, width)],
+                mid.at[j // 4, j % 4, pl.ds(0, size), :],
+            )
+        )
+
+    def fill(number):
+        return pltpu.make_async_copy(*fills[number], local.at[base + number])
+
+    keeps = [(wq, o_wq), (wout, o_wout), (wg, o_wg), (wc, o_wc)]
+
+    def keep_weights(number):
+        return pltpu.make_async_copy(*keeps[number], local.at[base + len(fills) + number])
+
+    for number in range(len(fills)):
+        fill(number).start()
     g.greet()
     each(gx.start)
     each(gc.start)
@@ -403,6 +428,26 @@
             perm[pl.ds((2 * t + d) * LANE, LANE), :] = hit.astype(F32).astype(BF16)
     taps[...] = jnp.zeros_like(taps)
     norm_grads[...] = jnp.zeros_like(norm_grads)
+    gate_bias[...] = jnp.zeros_like(gate_bias)
+    gate_bias[:, pl.ds(0, units)] = gate_in[...]
+    rest = wq.shape[0] - rows_in
+    wq[pl.ds(rows_in, rest), :] = jnp.zeros((rest, width), BF16)
+    wc[pl.ds(rows_in, rest), :] = jnp.zeros((rest, wc.shape[1]), BF16)
+    more = wout.shape[0] - wout_in.shape[0]
+    wout[pl.ds(wout_in.shape[0], more), :] = jnp.zeros((more, width), BF16)
+    for j in range(4):
+        wg[pl.ds(j * LANE + units, LANE - units), :] = jnp.zeros(
+            (LANE - units, wg.shape[1]), BF16
+        )
+    for number in range(len(fills)):
+        fill(number).wait()
+    for j in range(pieces):
+        size = min(shard, rows_in - j * shard)
+        wc[pl.ds(j * shard, size), pl.ds(width, 8 * LANE)] = nt(
+            mid[j // 4, j % 4, pl.ds(0, size), :], perm[...]
+        ).astype(BF16)
+    for number in range(len(keeps)):
+        keep_weights(number).start()
 
     lane = lax.broadcasted_iota(jnp.int32, (shard, LANE), 1)
     left = lane < HD
@@ -415,7 +460,7 @@
 
         def project(t, carry):
             rows = pl.ds(pl.multiple_of(t * shard, shard), shard)
-            first, second, third = unpack3(nn(x[s, t], wq[...]), HD * heads)
+            first, second, third = unpack3(nt(x[s, t], wq[...]), HD * heads)
             qkv[s, 0, rows, :] = (first * 0.125).astype(BF16)
             qkv[s, 1, rows, :] = second.astype(BF16)
             qkv[s, 2, rows, :] = third.astype(BF16)
@@ -471,17 +516,14 @@
             rows = pl.ds(pl.multiple_of(t * LANE, LANE), LANE)
             per = block_chars // LANE
             inner = pl.ds(pl.multiple_of((t % per) * LANE, LANE), LANE)
-            proj = nn(c[s, t // per, inner, :], wg[...])
+            proj = nt(c[s, t // per, inner, :], wg[...])
             for tile in range(2):
                 cols = slice(tile * LANE, (tile + 1) * LANE)
-                gate = jax.nn.sigmoid(proj[:, cols] + gate_bias_pad(tile))
+                gate = jax.nn.sigmoid(proj[:, cols] + gate_bias[tile : tile + 1])
                 cand = proj[:, (2 + tile) * LANE : (3 + tile) * LANE]
                 decays[s, tile, rows, :] = (1.0 - gate) * keep[s, rows, tile : tile + 1]
                 drive[tile, rows, :] = gate * cand
             return carry
-
-        def gate_bias_pad(tile):
-            return gate_bias[:, tile * LANE : (tile + 1) * LANE]
 
         total = 4 * block_chars
         lax.fori_loop(0, total // LANE, gates, 0)
@@ -545,10 +587,10 @@
         save(s, mid, st)
         def mix(t, carry):
             rows = pl.ds(pl.multiple_of(t * shard, shard), shard)
-            total = nn(mid[s, t], wc[pl.ds(0, width), :])
+            total = nt(mid[s, t], wc[:, pl.ds(0, width)])
             for u in range(4):
-                weights = wc[pl.ds(width + u * 2 * LANE, 2 * LANE), :]
-                total = total + nn(st[s, u, rows, :], weights)
+                weights = wc[:, pl.ds(width + u * 2 * LANE, 2 * LANE)]
+                total = total + nt(st[s, u, rows, :], weights)
             taps[pl.ds(pl.multiple_of(8 + t * shard, 8), shard), :] = total
             return carry
 
@@ -619,6 +661,8 @@
             local_copy(2 + number, s, source.at[s], target.at[s]).wait()
 
     each(drain)
+    for number in range(len(keeps)):
+        keep_weights(number).wait()
 
 
 def forward_call(tokens, chars, weights, small, group_slots=27):
@@ -626,8 +670,13 @@
     length, block_chars = shard * 4, chars.shape[1]
     total = block_chars * 4
     wq, wout, win, wdown, wg, gate_bias, wc, wm = weights
-    cols = wout.shape[0]
+    cols = -(-wout.shape[0] // LANE) * LANE
+    packed = -(-wq.shape[0] // LANE) * LANE
     heads = small["heads"]
+    kept = [
+        ((packed, width), BF16), ((cols, width), BF16), ((4 * LANE, chars.shape[2]), BF16),
+        ((packed, width + 8 * LANE), BF16),
+    ]
     sds = jax.ShapeDtypeStruct
     big = {
         "x": ((seqs, 4, shard, width), BF16),
@@ -653,18 +702,19 @@
     }
     rows = ((seqs, shard, width), F32)
     low_rows = ((seqs, shard, width), BF16)
-    scratch = list(big.values()) + [
+    scratch = list(big.values()) + kept + [
         rows, rows, low_rows, low_rows,
         ((2, total, LANE), F32),
         ((2, total, LANE), F32),
-        ((length + 16, wc.shape[1]), F32),
+        ((length + 16, packed), F32),
         ((8 * LANE, width), BF16),
+        ((2, LANE), F32),
         ((seqs, 3, shard, 2 * width), BF16), ((seqs, 3, shard, 2 * width), BF16),
         ((seqs, shard, 2 * width), F32), ((shard, 2 * width), F32),
     ]
     anyspace = pl.BlockSpec(memory_space=pl.ANY)
     vmem = pl.BlockSpec(memory_space=pltpu.VMEM)
-    out_shapes = [sds(low_rows[0], BF16)] * 2 + [sds(*v) for v in big.values()]
+    out_shapes = [sds(low_rows[0], BF16)] * 2 + [sds(*v) for v in list(big.values()) + kept]
     ins = (
         tokens, chars, wq, wout, win, wdown, wg, gate_bias, wc, wm, small["gain"], small["bias"],
         small["cot_t"], small["cot_c"], small["segc"], small["segr"], small["pickc"],
@@ -673,19 +723,21 @@
     outs = pl.pallas_call(
         functools.partial(forward_kernel, small["units"], small["channels"]),
         out_shape=out_shapes + [sds((4, width), F32)],
-        in_specs=[anyspace] * 2 + [vmem] * (len(ins) - 2),
+        in_specs=[
+            anyspace if k in (0, 1, 2, 3, 6, 8) else vmem for k in range(len(ins))
+        ],
         out_specs=[anyspace] * len(out_shapes) + [vmem],
         scratch_shapes=[pltpu.VMEM(*v) for v in scratch]
         + [
             pltpu.SemaphoreType.DMA((group_slots * seqs,)),
             pltpu.SemaphoreType.DMA((group_slots * seqs,)),
-            pltpu.SemaphoreType.DMA((26 * seqs,)),
+            pltpu.SemaphoreType.DMA((26 * seqs + 24,)),
         ],
         compiler_params=pltpu.CompilerParams(
             collective_id=0, has_side_effects=True, vmem_limit_bytes=62 * MIB
         ),
     )(*ins)
-    names = ["token_out", "char_out"] + list(big) + ["norm_grads"]
+    names = ["token_out", "char_out"] + list(big) + ["wq", "wout", "wg", "wc", "norm_grads"]
     return dict(zip(names, outs))
 
 
@@ -903,50 +955,49 @@
 )
 GRADS = ("merge", "conv", "down", "win", "gru", "out", "qkv")
 PIECES = (
-    (0, 384, True),
-    (1, 640, False),
-    (1, 768, True),
-    (1, 128, True),
-    (2, 384, True),
-    (2, 384, True),
+    (0, 384, False),
+    (1, 256, False),
+    (1, 512, True),
+    (1, 384, True),
+    (2, 512, True),
+    (2, 256, True),
     (3, 768, True),
-    (4, 128, True),
-    (4, 128, True),
-    (5, 256, False),
-    (6, 512, True),
-    (6, 256, False),
+    (4, 384, True),
+    (5, 384, True),
+    (6, 384, False),
+    (6, 768, False),
 )
 SCHEDULE = (
     (),
     (0, 10, 20, 30,),
     (),
-    (11,),
-    (1,),
+    (1, 11,),
+    (21,),
+    (2,),
+    (40, 50, 12,),
+    (60, 22, 31,),
+    (3,),
+    (13,),
+    (23,),
+    (32, 41, 24,),
+    (51, 33,),
+    (42,),
+    (25, 52,),
+    (34, 43,),
+    (61, 26, 53, 4, 14, 35, 44,),
+    (27, 5, 62, 15, 54, 36,),
     (),
-    (40, 50, 12,),
-    (60, 2,),
-    (21,),
-    (31,),
-    (13,),
-    (3, 22, 41, 32,),
-    (4,),
-    (51, 23, 42, 33,),
-    (5,),
-    (52, 24,),
-    (43, 34, 6, 61, 53, 14,),
-    (25, 44, 35, 7,),
-    (15, 62,),
-    (90, 100, 110, 54, 26, 45, 36,),
-    (8, 16,),
-    (),
-    (63, 91, 27, 111, 101, 37, 46, 55, 17,),
-    (64,),
-    (47, 92, 112,),
-    (70, 80, 56, 102, 18, 28, 38, 65, 93,),
-    (113, 103, 57, 48,),
-    (71, 81, 66, 94, 104, 114, 72,),
-    (82, 67, 73, 83, 105, 58, 95,),
-    (74, 115, 84, 106, 96, 75, 116, 85, 107, 97, 76, 68, 117, 86, 98, 77, 118, 87, 108, 78, 88,),
+    (80, 90, 100, 45, 6,),
+    (63, 28, 16, 37, 55,),
+    (81, 91, 46,),
+    (101, 7, 64, 38, 82, 17, 56,),
+    (92, 47,),
+    (102, 8,),
+    (70, 65, 83, 18, 57, 93, 48,),
+    (103, 71,),
+    (66, 84, 72, 58, 94,),
+    (104, 73, 67, 85, 95,),
+    (74, 105, 86, 96, 75, 106, 87, 97, 76, 107, 68, 98, 77, 88, 108, 78,),
 )
 
 
@@ -954,7 +1005,7 @@
     refs = list(refs)
     take = lambda count: [refs.pop(0) for _ in range(count)]
     hbm = SimpleNamespace(**dict(zip(SAVED, take(len(SAVED)))))
-    wq, wout, win, wdown, wg, gate_bias, wc, wm, gain, pickr, edges, norm_in = take(12)
+    wq, wout, win, wdown, wg, gate_in, wc, wm, gain, pickr, edges, norm_in = take(12)
     grad_tokens, grad_chars = take(2)
     grads_out = dict(zip(GRADS, take(len(GRADS))))
     (small_out,) = take(1)
@@ -964,7 +1015,7 @@
      stage, got, held, temp, cstage, cgot, cheld, ctemp) = take(22)
     land = dict(zip(GRADS, take(len(GRADS))))
     big = SimpleNamespace(**dict(zip(GRADS, take(len(GRADS)))))
-    small, small_land, send, recv, dsend, drecv, local, marks, credit = take(9)
+    small, small_land, gate_bias, send, recv, dsend, drecv, local, marks, credit = take(10)
 
     seqs, shard, width = grad_tokens.shape
     length = 4 * shard
@@ -1044,6 +1095,16 @@
     pl.semaphore_wait(barrier, len(places))
     each(gb.start)
     dpre[...] = jnp.zeros_like(dpre)
+    gate_bias[...] = jnp.zeros_like(gate_bias)
+    gate_bias[:, pl.ds(0, units)] = gate_in[...]
+    side = 2 * LANE
+    for t in range(4):
+        for j in range(width // side):
+            row = lax.broadcasted_iota(jnp.int32, (side, side), 0)
+            col = lax.broadcasted_iota(jnp.int32, (side, side), 1) + j * side
+            unit = row % LANE
+            hit = (col == row // LANE * 4 * units + t * units + unit) & (unit < units)
+            cstage[t // 2, j, pl.ds(t % 2 * side, side), :] = hit.astype(F32).astype(BF16)
     small[...] = jnp.zeros_like(small)
     small[0, pl.ds(0, 4), :] = norm_in[...]
     lane = lax.broadcasted_iota(jnp.int32, (shard, LANE), 1)
@@ -1086,7 +1147,7 @@
         lax.fori_loop(0, 4, taps, 0)
 
         def mid_part(b, out):
-            out[...] = nt(dyk[s, block_rows(b, shard), :], wc[pl.ds(0, width), :])
+            out[...] = nn(dyk[s, block_rows(b, shard), :], wc[:, pl.ds(0, width)])
 
         s_mid.start(s, mid_part)
 
@@ -1134,22 +1195,30 @@
                     :, at : at + size
                 ]
                 at += size
-        def conv_mid(j, carry):
-            colsj = pl.ds(pl.multiple_of(j * step_w, step_w), step_w)
-            out = tn(v.mid[:, :, :, colsj].reshape(tokens, step_w), dyk[...].reshape(tokens, -1))
-            big.conv[block_rows(j, step_w), :] = out.astype(BF16)
+        taps = 3 * channels
+
+        def conv_rows(j, carry):
+            lanes = pl.ds(pl.multiple_of(j * LANE, LANE), LANE)
+            left_rows = dyk[:, :, lanes].reshape(tokens, LANE)
+            size = min(LANE, taps - LANE * j) if isinstance(j, int) else LANE
+            first = j * LANE if isinstance(j, int) else pl.multiple_of(j * LANE, LANE)
+            out = tn(left_rows, v.mid[...].reshape(tokens, width))
+            big.conv[pl.ds(first, size), :] = out[:size].astype(BF16)
+            padded = [
+                tn(left_rows, v.st[:, t].reshape(tokens, side)).astype(BF16) for t in range(4)
+            ]
+            first = taps + j * LANE if isinstance(j, int) else pl.multiple_of(taps + j * LANE, 64)
+            for k in range(width // side):
+                out = None
+                for t in range(4):
+                    piece = nn(padded[t], cstage[t // 2, k, pl.ds(t % 2 * side, side), :])
+                    out = piece if out is None else out + piece
+                big.conv[pl.ds(first, size), pl.ds(k * side, side)] = out[:size].astype(BF16)
             return carry
 
-        lax.fori_loop(0, width // step_w, conv_mid, 0)
-
-        def conv_char(t, carry):
-            out = tn(v.st[:, t].reshape(tokens, 2 * LANE), dyk[...].reshape(tokens, -1))
-            for d in range(2):
-                first = pl.multiple_of(width + d * 4 * units + t * units, 16)
-                big.conv[pl.ds(first, units), :] = out[d * LANE : d * LANE + units].astype(BF16)
-            return carry
-
-        lax.fori_loop(0, 4, conv_char, 0)
+        lax.fori_loop(0, taps // LANE, conv_rows, 0)
+        if taps % LANE:
+            conv_rows(taps // LANE, 0)
         p_copy().start()
         fire(1)
 
@@ -1226,7 +1295,7 @@
     def chars_back(s):
         def char_part(b, out):
             first = pl.multiple_of(width + b * 2 * LANE, 2 * LANE)
-            out[...] = nt(dyk[s], wc[pl.ds(first, 2 * LANE), :])
+            out[...] = nn(dyk[s], wc[:, pl.ds(first, 2 * LANE)])
             out[block_rows(me, shard), :] += v.res4[s, b].astype(F32)
 
         s_chr.start(s, char_part)
@@ -1317,7 +1386,7 @@
         lax.fori_loop(0, 4, pack, 0)
 
         def part(b, out):
-            out[...] = nt(dyk[s, block_rows(b, shard), :], wq[...])
+            out[...] = nn(dyk[s, block_rows(b, shard), :], wq[...])
 
         s_tok.start(s, part)
 
@@ -1328,16 +1397,27 @@
 
     x_copy().wait()
 
+    tall = 3 * HD * heads
+    half_w = width // 2
+
     def qkv_weights(j, carry):
-        colsj = pl.ds(pl.multiple_of(j * step_w, step_w), step_w)
-        out = tn(v.h[:, :, :, colsj].reshape(tokens, step_w), dyk[...].reshape(tokens, -1))
-        big.qkv[block_rows(j, step_w), :] = out.astype(BF16)
+        lanes = pl.ds(pl.multiple_of(j * LANE, LANE), LANE)
+        size = min(LANE, tall - LANE * j) if isinstance(j, int) else LANE
+        out = tn(dyk[:, :, lanes].reshape(tokens, LANE), v.h[...].reshape(tokens, width))
+        for k in range(2):
+            first = k * tall + j * LANE
+            first = first if isinstance(j, int) else pl.multiple_of(first, 64)
+            big.qkv[pl.ds(first, size), :] = out[:size, k * half_w : (k + 1) * half_w].astype(BF16)
         return carry
 
-    lax.fori_loop(0, width // step_w, qkv_weights, 0)
-    big.out[...] = tn(
-        v.ctx[...].reshape(tokens, -1), v.mid[...].reshape(tokens, width)
-    ).astype(BF16)
+    lax.fori_loop(0, tall // LANE, qkv_weights, 0)
+    if tall % LANE:
+        qkv_weights(tall // LANE, 0)
+    out = tn(v.ctx[...].reshape(tokens, -1), v.mid[...].reshape(tokens, width))
+    for k in range(2):
+        big.out[pl.ds(k * HD * heads, HD * heads), :] = out[
+            : HD * heads, k * half_w : (k + 1) * half_w
+        ].astype(BF16)
     fire(19)
 
     load("c").wait()
@@ -1373,11 +1453,11 @@
             def finish(t, sums):
                 inner = block_rows(t, LANE)
                 rows = pl.ds(pl.multiple_of(b * block_chars + t * LANE, LANE), LANE)
-                proj = nn(v.c[s, b, inner, :], wg[...])
+                proj = nt(v.c[s, b, inner, :], wg[...])
                 new = []
                 for tile in range(2):
                     colst = slice(tile * LANE, (tile + 1) * LANE)
-                    gate = jax.nn.sigmoid(proj[:, colst] + gate_bias[:, colst])
+                    gate = jax.nn.sigmoid(proj[:, colst] + gate_bias[tile : tile + 1])
                     cand = proj[:, (2 + tile) * LANE : (3 + tile) * LANE]
                     flow = drive[tile, rows, :] * gate
                     logit = flow * (cand - states[tile, rows, :].astype(F32))
@@ -1390,8 +1470,8 @@
             sums = lax.fori_loop(0, block_chars // LANE, finish, (zero, zero))
             for tile in range(2):
                 small[6, 0:1, pl.ds(tile * LANE, LANE)] += sums[tile]
-            out[...] = nt(dproj[...], wg[...])
-            gru_acc[...] += tn(v.c[s, b], dproj[...])
+            out[...] = nn(dproj[...], wg[...])
+            gru_acc[...] += tn(dproj[...], v.c[s, b])
 
         pl.semaphore_wait(credit.at[s], 2)
         s_cout.start(s, part)
@@ -1406,7 +1486,11 @@
             pl.when(s == 0)(functools.partial(fire, 22))
 
     each(gru_back)
-    big.gru[...] = gru_acc[...].astype(BF16)
+    for d in range(2):
+        for k in range(2):
+            big.gru[pl.ds((2 * d + k) * units, units), :] = gru_acc[
+                pl.ds((2 * k + d) * LANE, units), :
+            ].astype(BF16)
     small_step(2) if hops else None
     fire(25)
 
@@ -1450,15 +1534,17 @@
     length = shard * 4
     block_chars, char_width = saved["c"].shape[2:]
     total = 4 * block_chars
-    cols, packed = wout.shape[0], wc.shape[1]
+    cols, packed = wout.shape[0], wc.shape[0]
+    tall = 3 * HD * small["heads"]
     channels = small["channels"]
     saved_in = [saved[n] for n in SAVED]
     names = [n for n in SAVED if n not in ("branch", "states", "decay", "p", "x")]
     shapes = [(saved[n].shape, saved[n].dtype) for n in names]
     grads = {
-        "merge": (2 * channels, width), "conv": (2 * width, packed),
+        "merge": (2 * channels, width), "conv": (2 * 3 * channels, width),
         "down": (win.shape[1], width), "win": (width, win.shape[1]),
-        "gru": (char_width, 4 * LANE), "out": (cols, width), "qkv": (width, wq.shape[1]),
+        "gru": (4 * small["units"], char_width), "out": (2 * tall // 3, width // 2),
+        "qkv": (2 * tall, width // 2),
     }
     pad = (seqs, 3, shard, width)
     cpad = (seqs, 3, length, 2 * LANE)
@@ -1472,7 +1558,7 @@
         ((seqs, 4, shard, width), BF16),
         ((length, 2 * LANE), BF16),
         ((block_chars, 4 * LANE), BF16),
-        ((char_width, 4 * LANE), F32),
+        ((4 * LANE, char_width), F32),
         ((seqs, shard, width), F32),
         ((seqs, shard, width), F32),
         ((4, shard, length), BF16),
@@ -1484,7 +1570,7 @@
         landing = sum(Reduce.landing_rows(n, way) for k, n, way in PIECES if k == which)
         scratch.append(((landing if dp_size == 8 else 16, grads[name][1]), BF16))
     scratch += [(shape, BF16) for shape in grads.values()]
-    scratch += [((7, 16, width), F32), ((5, 16, width), F32)]
+    scratch += [((7, 16, width), F32), ((5, 16, width), F32), ((2, LANE), F32)]
     anyspace = pl.BlockSpec(memory_space=pl.ANY)
     vmem = pl.BlockSpec(memory_space=pltpu.VMEM)
     ins = saved_in + list(weights) + [small["gain"], small["pickr"], small["edges"], saved["norm_grads"]]
@@ -1511,6 +1597,58 @@
     )(*ins)
     names = ["grad_tokens", "grad_chars"] + list(grads) + ["small"]
     return dict(zip(names, outs))
+
+
+def finish_kernel(
+    conv, qkv, out, down, win, gru, chars, tokens, first, second,
+    o_conv, o_qkv, o_out, o_down, o_win, o_gru, o_chars, o_tokens, o_first, o_second,
+):
+    for source, target in ((conv, o_conv), (qkv, o_qkv), (out, o_out)):
+        half = source.shape[2]
+        for k in range(2):
+            target[:, k * half : (k + 1) * half] = source[k].astype(F32)
+    for source, target in ((down, o_down), (win, o_win), (gru, o_gru)):
+        target[...] = source[...].astype(F32)
+    for j in range(8):
+        o_chars[0, j] = chars[0, :, j, :]
+    for source, target in ((tokens, o_tokens), (first, o_first), (second, o_second)):
+        target[...] = source[...]
+
+
+def finish_call(grads, grad_chars, grad_tokens, token_out, char_out):
+    seqs, block_chars, char_width = grad_chars.shape
+    steps = block_chars // 8
+    turns = 2 * seqs
+    chars = grad_chars.reshape(seqs, steps, 8, char_width)
+    pairs = [a.reshape(2, -1, a.shape[1]) for a in (grads["conv"], grads["qkv"], grads["out"])]
+    plain = [grads["down"], grads["win"], grads["gru"]]
+    copied = [grad_tokens, token_out, char_out]
+    flat = [(a.shape[1], 2 * a.shape[2]) for a in pairs] + [a.shape for a in plain]
+
+    def rows_spec(shape):
+        return pl.BlockSpec((shape[0] // turns, shape[1]), lambda i: (i, 0))
+
+    def pair_spec(shape):
+        return pl.BlockSpec((2, shape[1] // turns, shape[2]), lambda i: (0, i, 0))
+
+    def halves(shape):
+        return pl.BlockSpec((1, shape[1] // 2, shape[2]), lambda i: (i // 2, i % 2, 0))
+
+    return pl.pallas_call(
+        finish_kernel,
+        grid=(turns,),
+        out_shape=[jax.ShapeDtypeStruct(shape, F32) for shape in flat]
+        + [jax.ShapeDtypeStruct((seqs, 8, steps, char_width), F32)]
+        + [jax.ShapeDtypeStruct(a.shape, a.dtype) for a in copied],
+        in_specs=[pair_spec(a.shape) for a in pairs]
+        + [rows_spec(a.shape) for a in plain]
+        + [pl.BlockSpec((1, steps // 2, 8, char_width), lambda i: (i // 2, i % 2, 0, 0))]
+        + [halves(a.shape) for a in copied],
+        out_specs=[rows_spec(shape) for shape in flat]
+        + [pl.BlockSpec((1, 8, steps // 2, char_width), lambda i: (i // 2, 0, i % 2, 0))]
+        + [halves(a.shape) for a in copied],
+        compiler_params=pltpu.CompilerParams(vmem_limit_bytes=62 * MIB),
+    )(*pairs, *plain, chars, *copied)
 
 
 def local(
@@ -1543,23 +1681,11 @@
     heads_here = head_cols // HD
     units_here = w_gru.shape[3]
     merge_here = w_conv.shape[2]
-    gru_matrix, gru_bias = gru_weights(w_gru, gate_bias)
-    spare = -head_cols % LANE
+    wq = jnp.transpose(w_qkv, (1, 2, 0)).reshape(3 * head_cols, model_width)
+    wc = jnp.transpose(w_conv, (0, 2, 1)).reshape(3 * merge_here, 2 * model_width)
+    wg = jnp.transpose(w_gru, (1, 2, 3, 0))
     more = -merge_here % LANE
-    wq = jnp.pad(
-        w_qkv.reshape(model_width, 3 * head_cols), ((0, 0), (0, -3 * head_cols % LANE))
-    )
-    wout = jnp.pad(w_out, ((0, spare), (0, 0)))
     wm = jnp.pad(w_merge.reshape(merge_here, 2 * model_width), ((0, more), (0, 0)))
-    conv = jnp.swapaxes(w_conv, 0, 1).reshape(2 * model_width, 3 * merge_here)
-    conv = jnp.pad(conv, ((0, 0), (0, -3 * merge_here % LANE)))
-    conv_char = conv[model_width:].reshape(2, group_size, units_here, -1)
-    conv_char = jnp.pad(
-        jnp.swapaxes(conv_char, 0, 1), ((0, 0), (0, 0), (0, LANE - units_here), (0, 0))
-    )
-    wc = jnp.concatenate(
-        [conv[:model_width], conv_char.reshape(group_size * 2 * LANE, -1)], axis=0
-    )
     layouts = [layout(doc_lengths[i], token_chars[i], char_total) for i in range(micro_count)]
     stacked_layout = [jnp.stack(parts) for parts in zip(*layouts)]
     segment, first_char, last_char, keep_forward, keep_backward, prev_ok, next_ok = stacked_layout
@@ -1590,8 +1716,9 @@
         ),
         heads=heads_here, units=units_here, channels=merge_here,
     )
-    weights = (wq, wout, w_in, w_down, gru_matrix, gru_bias, wc, wm)
+    weights = (wq, w_out, w_in, w_down, wg, gate_bias, wc, wm)
     fw = forward_call(tokens, reorder(characters), weights, small)
+    weights = (fw["wq"], fw["wout"], w_in, w_down, fw["wg"], gate_bias, fw["wc"], wm)
     dp_size = lax.axis_size("dp")
     bw = backward_call(fw, weights, small, dp_size)
     rows = bw["small"]
@@ -1600,27 +1727,25 @@
     if dp_size != 8:
         grads, gate_row = lax.psum((grads, gate_row), "dp")
         rows = lax.psum(rows, ("dp", "tensor"))
-    grads = {name: value.astype(F32) for name, value in grads.items()}
-    grad_conv = jnp.stack(
-        [grads["conv"][:, k * merge_here : (k + 1) * merge_here] for k in range(3)], axis=0
+    grad_merge = grads["merge"].astype(F32).reshape(2, merge_here, model_width)
+    conv, qkv, out, down, win, gru, chars, tokens_grad, first, second = finish_call(
+        grads, bw["grad_chars"], bw["grad_tokens"], fw["token_out"], fw["char_out"]
     )
-    grad_merge = grads["merge"].reshape(2, merge_here, model_width)
-    grad_gru = grads["gru"].reshape(char_width, 2, 2, LANE)[..., :units_here]
-    grad_chars = jnp.swapaxes(
-        bw["grad_chars"].reshape(micro_count, steps, 8, char_width), 1, 2
-    )
+    conv = conv.reshape(3, merge_here, 2 * model_width)
+    qkv = qkv.reshape(3, head_cols, model_width)
+    gru = gru.reshape(2, 2, units_here, char_width)
     return (
-        fw["token_out"],
-        fw["char_out"],
-        bw["grad_tokens"],
-        grad_chars.reshape(bw["grad_chars"].shape),
-        grads["qkv"][:, : 3 * head_cols].reshape(model_width, 3, head_cols),
-        grads["out"][:head_cols],
-        grads["win"],
-        grads["down"],
-        jnp.swapaxes(grad_gru, 1, 2),
+        first,
+        second,
+        tokens_grad,
+        chars.reshape(bw["grad_chars"].shape),
+        jnp.transpose(qkv, (2, 0, 1)),
+        out,
+        win,
+        down,
+        jnp.transpose(gru, (3, 0, 1, 2)),
         gate_row.reshape(2, LANE)[:, :units_here],
-        grad_conv,
+        jnp.transpose(conv, (0, 2, 1)),
         jnp.swapaxes(grad_merge, 0, 1),
         jnp.concatenate([rows[4:6], rows[0:2]], axis=0),
         jnp.concatenate([rows[6:8], rows[2:4]], axis=0),

time: 331 us -> 303 us (0.915)
  local copies, waits for them, and re-layouts: 34.9 us -> 14.4 us
  other arithmetic: 17.9 us -> 7.5 us
    unnamed x35 -> x5, local copies, waits for them, and re-layouts: 10.3 us -> 0.07 us
    pallas_call x0 -> x1, Pallas kernels: none -> 8.56 us  [finish_call(): pl.pallas_call(finish_kernel, grid=(turns,), out_shape=[jax.ShapeDtypeStr...]
    pallas_call x1, Pallas kernels: 175 us -> 168 us  [backward_call(): pl.pallas_call(functools.partial(backward_kernel, small['units'], channel...]
    reshape x6 -> x0, local copies, waits for them, and re-layouts: 6.02 us -> none  [the longest x1 2.73 us: local(): conv = jnp.swapaxes(w_conv, 0, 1).reshape(2 * model_width, 3 * merge_here)]
    pad x5 -> x0, local copies, waits for them, and re-layouts: 3.49 us -> none  [the longest x1 1.29 us: gru_weights(): bias = jnp.pad(gate_bias, ((0, 0), (0, LANE - units)))]
    convert_element_type x3 -> x0, other arithmetic: 3.41 us -> none  [local(): grads = {name: value.astype(F32) for name, value in grads.items()}]
where the time goes in v6:
time: 303 us; the launch traced here: 302 us
  Pallas kernels  279 us (92%)
  local copies, waits for them, and re-layouts  14.4 us (5%)
  other arithmetic  7.5 us (2%)
    pallas_call x1, Pallas kernels, backward_call(): pl.pallas_call(functools.partial(backward_kernel, small['units'], channel...  168 us
    pallas_call x1, Pallas kernels, forward_call(): pl.pallas_call(functools.partial(forward_kernel, small['units'], small['c...  103 us
    pallas_call x1, Pallas kernels, finish_call(): pl.pallas_call(finish_kernel, grid=(turns,), out_shape=[jax.ShapeDtypeStr...  8.56 us

profile of v6, /device:TPU:0, one launch (start us, length us, event | category | flops | bytes accessed | tf_op | source)
XLA Modules:
  0.0 302.4 jit_solution(18008763833389319788)
XLA Ops:
  0.6 0.8 slice_bitcast_fusion.1
  1.4 0.1 select_reduce_fusion.6
  1.5 0.8 fusion.18
  2.3 0.1 fusion.7
  2.4 0.1 fusion.6
  2.5 0.1 convert_reduce_fusion
  2.6 0.1 convert_reduce_fusion.1
  2.7 0.8 fusion.20
  3.4 0.1 fusion.9
  3.5 0.1 fusion.8
  3.7 0.1 pad_bitcast_fusion
  3.7 0.1 fusion.16
  3.8 0.6 broadcast_in_dim.122.segr
  4.4 0.8 fusion.24
  5.2 0.2 select_reduce_fusion.2
  5.4 0.2 select_reduce_fusion
  5.6 0.2 select_reduce_fusion.4
  5.8 0.2 select_reduce_fusion.1
  6.0 0.1 fusion
  6.1 0.1 fusion.1
  6.2 0.1 fusion.2
  6.3 0.1 fusion.3
  6.4 0.8 slice_subtract_fusion.1
  7.2 0.1 sub.188
  7.3 0.1 sub.192
  7.4 0.1 sub.195
  7.5 0.1 sub.198
  7.5 0.7 fusion.27.refs_29_
  8.2 0.1 fusion.12
  8.3 1.0 copy.75.pickc
  9.3 0.2 copy.72
  9.5 0.2 copy.70
  9.8 0.2 copy.73
  10.0 0.0 copy-start.1
  10.0 0.2 copy.71
  10.2 0.0 copy-start
  10.2 1.3 pad_maximum_fusion.edges.refs_30_
  11.5 1.0 copy.74.segc
  12.5 0.0 copy-done.1
  12.5 1.1 copy.81
  13.6 0.0 copy-done
  13.6 0.1 copy.77
  13.7 0.9 pad.6.wm.refs_27_
  14.6 2.0 copy.69
  16.7 102.6 %shard_map.263 = (bf16[2,128,768]{2,1,0:T(8,128)(2,1)}, bf16[2,128,768]{2,1,0:T(8,128)(2,1)}, bf16[2,4,128,768]{3,2,1,0:T(8,128)(2,1)}, bf16[2,4,512,256]{3,2,1,...) custom-call(bf16[2,128,768]{2,1,0:T(8,128)(2,1)} %tokens.1, ...), custom_call_target="tpu_custom_call" | custom-call | tf_op jit(solution)/shard_map/pallas_call | solution.py:723
  119.3 168.3 %shard_map.264 = (f32[2,128,768]{2,1,0:T(8,128)}, f32[2,512,256]{2,1,0:T(8,128)}, bf16[384,768]{1,0:T(8,128)(2,1)}, bf16[1152,768]{1,0:T(8,128)(2,1)}, bf16[768,...) custom-call(bf16[2,3,128,512]{3,2,1,0:T(8,128)(2,1)} %get-tuple-elem, ...), custom_call_target="tpu_custom_call" | custom-call | tf_op jit(solution)/shard_map/pallas_call | solution.py:1577
  287.6 1.3 slice.42
  288.9 0.9 fusion.23
  289.8 0.6 pad_maximum_fusion.2
  290.4 0.6 pad_maximum_fusion.1
  291.0 2.7 copy.80
  293.7 8.6 %shard_map.265 = (f32[576,1536]{1,0:T(8,128)}, f32[576,768]{1,0:T(8,128)}, f32[192,768]{1,0:T(8,128)}, f32[768,768]{1,0:T(8,128)}, f32[768,768]{1,0:T(8,128)}, /...) custom-call(bf16[2,576,768]{2,1,0:T(8,128)(2,1)} %bitcast.86, ...), custom_call_target="tpu_custom_call" | custom-call | tf_op jit(solution)/shard_map/pallas_call | solution.py:1637
  (20 shorter events, 0.1 us)
Async XLA Ops:
  10.0 2.6 copy-start.1
  10.2 3.4 %copy-start = (bf16[192,2,768]{2,1,0:T(2,128)(2,1)S(1)}, bf16[192,2,768]{2,1,0:T(2,128)(2,1)}, u32[]{:S(2)}) copy-start(bf16[192,2,768]{2,1,0:T(2,128)(2,1)} %param.27) | copy-start | bytes 1769476

commit v7 on v6

--- a/solution.py
+++ b/solution.py
@@ -16,56 +16,10 @@
 HIGH_PRECISION = lax.Precision.HIGHEST
 
 
-def layout(doc_sizes, char_counts, char_total):
-    length = char_counts.shape[0]
-    docs = doc_sizes.shape[0]
-    doc_ids = jnp.arange(docs, dtype=jnp.int32)
-    doc_ends = jnp.sum(
-        jnp.where(doc_ids[None, :] <= doc_ids[:, None], doc_sizes[None, :], 0), axis=1
-    )
-    positions = jnp.arange(length, dtype=jnp.int32)
-    segment = jnp.sum(
-        (positions[:, None] >= doc_ends[None, :]).astype(jnp.int32), axis=1, dtype=jnp.int32
-    )
-    token_ends = jnp.sum(
-        jnp.where(positions[None, :] <= positions[:, None], char_counts[None, :], 0), axis=1
-    )
-    last_char = token_ends - 1
-    first_char = token_ends - char_counts
-    char_ends = jnp.sum(
-        jnp.where(positions[None, :] < doc_ends[:, None], char_counts[None, :], 0), axis=1
-    )
-    char_positions = jnp.arange(char_total, dtype=jnp.int32)
-    starts = char_ends - jnp.sum(
-        jnp.where(
-            (positions[None, :] < doc_ends[:, None])
-            & (positions[None, :] >= (doc_ends - doc_sizes)[:, None]),
-            char_counts[None, :],
-            0,
-        ),
-        axis=1,
-    )
-    keep_forward = 1.0 - jnp.any(char_positions[:, None] == starts[None, :], axis=1).astype(
-        jnp.float32
-    )
-    keep_backward = 1.0 - jnp.any(
-        char_positions[:, None] == (char_ends - 1)[None, :], axis=1
-    ).astype(jnp.float32)
-    token_starts = doc_ends - doc_sizes
-    prev_ok = 1.0 - jnp.any(positions[:, None] == token_starts[None, :], axis=1).astype(
-        jnp.float32
-    )
-    next_ok = 1.0 - jnp.any(positions[:, None] == (doc_ends - 1)[None, :], axis=1).astype(
-        jnp.float32
-    )
-    return (segment, first_char, last_char, keep_forward, keep_backward, prev_ok, next_ok)
-
-
 F32 = jnp.float32
 BF16 = jnp.bfloat16
 LANE = 128
 MIB = 1024 * 1024
-VMEM = pl.BlockSpec(memory_space=pltpu.VMEM)
 
 
 def nn(left, right):
@@ -323,17 +277,17 @@
 
 
 def forward_kernel(
-    units, channels, tokens, chars, wq_in, wout_in, win, wdown, wg_in, gate_in, wc_in, wm, gain, bias,
-    cot_t, cot_c,
-    segc, segr, pickc, keep, edges,
+    units, channels, docs, counts, tokens, chars, wq_in, wout_in, win_in, wdown_in, wg_in, gate_in,
+    wc_in, wm_in, gain, bias, cot_t_in, cot_c_in,
     token_out, char_out, o_x, o_c, o_qkv, o_p, o_ctx, o_h, o_act, o_dact, o_mid, o_st, o_mg,
     o_dmg, o_states, o_decay, o_unit0, o_unit1, o_scale, o_res3, o_res4, o_branch,
-    o_wq, o_wout, o_wg, o_wc, norm_grads,
+    o_wq, o_wout, o_wg, o_wc, norm_grads, pickr, edges,
     x, c, qkv, p, ctx, h, act, dact, mid, st, mg, dmg, low_states, decays, unit0, unit1, scale, res3, res4, branch,
     wq, wout, wg, wc, hidden, middle, outs_t, outs_c, states, drive, taps, perm, gate_bias,
+    win, wdown, wm, cot_t, cot_c, segc, segr, pickc, keep,
     stage, got, held, temp, send, recv, local,
 ):
-    seqs, length = tokens.shape[0], segr.shape[2]
+    seqs, length = counts.shape[0], counts.shape[2]
     shard, width = tokens.shape[1], tokens.shape[2]
     block_chars = chars.shape[1]
     heads = p.shape[1] // 4
@@ -386,6 +340,7 @@
 
     each(lambda s: (own_x(s).start(), own_c(s).start()))
     base = (2 + len(plan)) * seqs
+    late = [(win_in, win), (wdown_in, wdown), (wm_in, wm), (cot_t_in, cot_t), (cot_c_in, cot_c)]
     rows_in = wq_in.shape[0]
     fills = [
         (wq_in, wq.at[pl.ds(0, rows_in), :]),
@@ -404,6 +359,8 @@
                 mid.at[j // 4, j % 4, pl.ds(0, size), :],
             )
         )
+
+    fills += late
 
     def fill(number):
         return pltpu.make_async_copy(*fills[number], local.at[base + number])
@@ -439,7 +396,7 @@
         wg[pl.ds(j * LANE + units, LANE - units), :] = jnp.zeros(
             (LANE - units, wg.shape[1]), BF16
         )
-    for number in range(len(fills)):
+    for number in range(len(fills) - len(late)):
         fill(number).wait()
     for j in range(pieces):
         size = min(shard, rows_in - j * shard)
@@ -451,6 +408,57 @@
 
     lane = lax.broadcasted_iota(jnp.int32, (shard, LANE), 1)
     left = lane < HD
+    steps = block_chars // 8
+    assert steps & (steps - 1) == 0
+
+    def place(char):
+        inner = char & (block_chars - 1)
+        return char - inner + ((inner & (steps - 1)) << 3) + (inner >> (steps.bit_length() - 1))
+
+    def hits(positions, marks):
+        total = jnp.zeros(positions.shape, F32)
+        for mark in marks:
+            total = total + (positions == mark).astype(F32)
+        return total
+
+    def structure(s):
+        ends, running = [], 0
+        for d in range(docs.shape[1]):
+            running = running + docs[s, d]
+            ends.append(running)
+        along = lax.broadcasted_iota(jnp.int32, (1, length), 1)
+        down = lax.broadcasted_iota(jnp.int32, (length, 1), 0)
+        seg_row, seg_col = jnp.zeros_like(along), jnp.zeros_like(down)
+        for end in ends:
+            seg_row = seg_row + (along >= end).astype(jnp.int32)
+            seg_col = seg_col + (down >= end).astype(jnp.int32)
+        segr[s] = seg_row
+        segc[s] = seg_col
+        edges[s, :, 0:1] = 1.0 - hits(down, [0] + ends[:-1])
+        edges[s, :, 1:2] = 1.0 - hits(down + 1, ends)
+        count = counts[s].astype(F32)
+        many = jnp.broadcast_to(count, (LANE, length)).astype(BF16)
+        rows = lax.broadcasted_iota(jnp.int32, (length, length), 0)
+        cols = lax.broadcasted_iota(jnp.int32, (length, length), 1)
+        ends_row = nn(many[:16], (rows <= cols).astype(F32).astype(BF16))[0:1]
+        ends_col = nt((cols <= rows).astype(F32).astype(BF16), many)[:, 0:1]
+        starts_col = nt((cols < rows).astype(F32).astype(BF16), many)[:, 0:1]
+        pickr[s, 0:1, :] = place(ends_row.astype(jnp.int32) - 1)
+        pickr[s, 1:2, :] = place((ends_row - count).astype(jnp.int32))
+        pickc[s, :, 0:1] = place(ends_col.astype(jnp.int32) - 1)
+        pickc[s, :, 1:2] = place(starts_col.astype(jnp.int32))
+        cuts = [
+            jnp.sum(jnp.where(along < end, count, 0.0), axis=1, keepdims=True) for end in ends
+        ]
+        row = lax.broadcasted_iota(jnp.int32, (4 * block_chars, 1), 0)
+        inner = row & (block_chars - 1)
+        char = (row - inner + (inner & 7) * steps + (inner >> 3)).astype(F32)
+        keep[s, :, 0:1] = 1.0 - hits(char, [0.0] + cuts[:-1])
+        keep[s, :, 1:2] = 1.0 - hits(char + 1.0, cuts)
+
+    each(structure)
+    for number in range(len(fills) - len(late), len(fills)):
+        fill(number).wait()
 
     def attention(s):
         gx.forward(s)
@@ -702,6 +710,7 @@
     }
     rows = ((seqs, shard, width), F32)
     low_rows = ((seqs, shard, width), BF16)
+    total = block_chars * 4
     scratch = list(big.values()) + kept + [
         rows, rows, low_rows, low_rows,
         ((2, total, LANE), F32),
@@ -709,6 +718,9 @@
         ((length + 16, packed), F32),
         ((8 * LANE, width), BF16),
         ((2, LANE), F32),
+        (win.shape, BF16), (wdown.shape, BF16), (wm.shape, BF16), rows, rows,
+        ((seqs, length, 1), jnp.int32), ((seqs, 1, length), jnp.int32),
+        ((seqs, length, 2), jnp.int32), ((seqs, total, 2), F32),
         ((seqs, 3, shard, 2 * width), BF16), ((seqs, 3, shard, 2 * width), BF16),
         ((seqs, shard, 2 * width), F32), ((shard, 2 * width), F32),
     ]
@@ -716,17 +728,21 @@
     vmem = pl.BlockSpec(memory_space=pltpu.VMEM)
     out_shapes = [sds(low_rows[0], BF16)] * 2 + [sds(*v) for v in list(big.values()) + kept]
     ins = (
-        tokens, chars, wq, wout, win, wdown, wg, gate_bias, wc, wm, small["gain"], small["bias"],
-        small["cot_t"], small["cot_c"], small["segc"], small["segr"], small["pickc"],
-        small["keep"], small["edges"],
+        small["docs"], small["counts"], tokens, chars, wq, wout, win, wdown, wg, gate_bias, wc, wm,
+        small["gain"], small["bias"], small["cot_t"], small["cot_c"],
     )
+    smem = pl.BlockSpec(memory_space=pltpu.SMEM)
+    places = [smem, vmem] + [anyspace] * 7 + [vmem] + [anyspace] * 2 + [vmem] * 2 + [anyspace] * 2
     outs = pl.pallas_call(
         functools.partial(forward_kernel, small["units"], small["channels"]),
-        out_shape=out_shapes + [sds((4, width), F32)],
-        in_specs=[
-            anyspace if k in (0, 1, 2, 3, 6, 8) else vmem for k in range(len(ins))
+        out_shape=out_shapes
+        + [
+            sds((4, width), F32),
+            sds((seqs, 2, length), jnp.int32),
+            sds((seqs, length, 2), F32),
         ],
-        out_specs=[anyspace] * len(out_shapes) + [vmem],
+        in_specs=places,
+        out_specs=[anyspace] * len(out_shapes) + [vmem] * 3,
         scratch_shapes=[pltpu.VMEM(*v) for v in scratch]
         + [
             pltpu.SemaphoreType.DMA((group_slots * seqs,)),
@@ -738,6 +754,7 @@
         ),
     )(*ins)
     names = ["token_out", "char_out"] + list(big) + ["wq", "wout", "wg", "wc", "norm_grads"]
+    names += ["pickr", "edges"]
     return dict(zip(names, outs))
 
 
@@ -1005,12 +1022,15 @@
     refs = list(refs)
     take = lambda count: [refs.pop(0) for _ in range(count)]
     hbm = SimpleNamespace(**dict(zip(SAVED, take(len(SAVED)))))
-    wq, wout, win, wdown, wg, gate_in, wc, wm, gain, pickr, edges, norm_in = take(12)
+    weights_in = take(7)
+    gate_in, gain, pickr, edges, norm_in = take(5)
     grad_tokens, grad_chars = take(2)
     grads_out = dict(zip(GRADS, take(len(GRADS))))
     (small_out,) = take(1)
     names = [n for n in SAVED if n not in ("branch", "states", "decay", "p", "x")]
     v = SimpleNamespace(**dict(zip(names, take(len(names)))))
+    weights = take(7)
+    wq, wout, win, wdown, wg, wc, wm = weights
     (pb, states, decay, drive, dpre, dyk, fg, gtok, dproj, gru_acc, res2, res1, ds, parts,
      stage, got, held, temp, cstage, cgot, cheld, ctemp) = take(22)
     land = dict(zip(GRADS, take(len(GRADS))))
@@ -1075,9 +1095,15 @@
             hbm.branch.at[s], gb.at(s, me), local.at[spare + 4 + 2 * seqs + s]
         )
 
+    def weight(number):
+        return pltpu.make_async_copy(weights_in[number], weights[number], local.at[40 + number])
+
     each(lambda s: own_branch(s).start())
+    weight(6).start()
     for name in ("dmg", "res4", "mg", "mid", "st"):
         load(name).start()
+    for number in (5, 3, 2, 1, 0, 4):
+        weight(number).start()
     states_copy(0).start()
     for tile in range(2):
         decay_copy(0, tile).start()
@@ -1111,6 +1137,8 @@
     left = lane < HD
     for name in ("dmg", "res4"):
         load(name).wait()
+    weight(6).wait()
+    weight(5).wait()
 
     def block_rows(t, size):
         return pl.ds(pl.multiple_of(t * size, size), size)
@@ -1137,8 +1165,8 @@
             rows = block_rows(t, shard)
             window = dpre[pl.ds(pl.multiple_of(t * shard, 8), shard + 16), :]
             marks = edges[s, rows, :]
-            before = window[9 : 9 + shard] * marks[:, 2:3]
-            after = window[7 : 7 + shard] * marks[:, 3:4]
+            before = window[9 : 9 + shard] * marks[:, 1:2]
+            after = window[7 : 7 + shard] * marks[:, 0:1]
             dyk[s, rows, :] = pack3(
                 [before, window[8 : 8 + shard], after], channels
             ).astype(BF16)
@@ -1239,6 +1267,8 @@
     each(second_back)
     for name in ("dact", "act", "h"):
         load(name).wait()
+    weight(3).wait()
+    weight(2).wait()
 
     def ffn_back(s):
         gf.forward(s)
@@ -1327,6 +1357,8 @@
     small_step(0) if hops else None
     for name in ("qkv", "ctx"):
         load(name).wait()
+    weight(1).wait()
+    weight(0).wait()
     p_copy().wait()
 
     def attention_back(s):
@@ -1421,6 +1453,7 @@
     fire(19)
 
     load("c").wait()
+    weight(4).wait()
 
     def gru_back(s):
         gtok[...] = s_chr.finish(s).astype(BF16)
@@ -1528,7 +1561,7 @@
 
 
 def backward_call(saved, weights, small, dp_size):
-    wq, wout, win, wdown, wg, gate_bias, wc, wm = weights
+    wq, wout, win, wdown, wg, wc, wm, gate_bias = weights
     sds = jax.ShapeDtypeStruct
     seqs, shard, width = saved["res3"].shape
     length = shard * 4
@@ -1548,7 +1581,7 @@
     }
     pad = (seqs, 3, shard, width)
     cpad = (seqs, 3, length, 2 * LANE)
-    scratch = shapes + [
+    scratch = shapes + [(w.shape, BF16) for w in weights[:7]] + [
         (saved["p"].shape, BF16),
         ((2, total, LANE), BF16),
         ((2, total, LANE), F32),
@@ -1573,13 +1606,14 @@
     scratch += [((7, 16, width), F32), ((5, 16, width), F32), ((2, LANE), F32)]
     anyspace = pl.BlockSpec(memory_space=pl.ANY)
     vmem = pl.BlockSpec(memory_space=pltpu.VMEM)
-    ins = saved_in + list(weights) + [small["gain"], small["pickr"], small["edges"], saved["norm_grads"]]
+    ins = saved_in + list(weights) + [small["gain"]]
+    ins += [saved["pickr"], saved["edges"], saved["norm_grads"]]
     outs = pl.pallas_call(
         functools.partial(backward_kernel, small["units"], channels, dp_size),
         out_shape=[sds((seqs, shard, width), F32), sds((seqs, block_chars, char_width), F32)]
         + [sds(shape, BF16) for shape in grads.values()]
         + [sds((16, width), F32)],
-        in_specs=[anyspace] * len(saved_in) + [vmem] * (len(ins) - len(saved_in)),
+        in_specs=[anyspace] * (len(saved_in) + 7) + [vmem] * 5,
         out_specs=[anyspace] * (2 + len(grads)) + [vmem],
         scratch_shapes=[pltpu.VMEM(*one) for one in scratch]
         + [
@@ -1587,7 +1621,7 @@
             pltpu.SemaphoreType.DMA((32 * seqs,)),
             pltpu.SemaphoreType.DMA((14 * len(PIECES) + 4,)),
             pltpu.SemaphoreType.DMA((14 * len(PIECES) + 4,)),
-            pltpu.SemaphoreType.DMA((40,)),
+            pltpu.SemaphoreType.DMA((48,)),
             pltpu.SemaphoreType.DMA((len(PIECES),)),
             pltpu.SemaphoreType.REGULAR((seqs,)),
         ],
@@ -1600,13 +1634,20 @@
 
 
 def finish_kernel(
-    conv, qkv, out, down, win, gru, chars, tokens, first, second,
-    o_conv, o_qkv, o_out, o_down, o_win, o_gru, o_chars, o_tokens, o_first, o_second,
+    units, conv, qkv, out, merge, down, win, gru, chars, tokens, first, second, rows,
+    o_conv, o_qkv, o_out, o_merge, o_down, o_win, o_gru, o_chars, o_tokens, o_first, o_second,
+    o_gain, o_bias, o_gate,
 ):
     for source, target in ((conv, o_conv), (qkv, o_qkv), (out, o_out)):
         half = source.shape[2]
         for k in range(2):
             target[:, k * half : (k + 1) * half] = source[k].astype(F32)
+    for k in range(2):
+        o_merge[:, k, :] = merge[k].astype(F32)
+        o_gate[k : k + 1, :] = rows[8:9, k * LANE : k * LANE + units]
+    for target, at in ((o_gain, 0), (o_bias, 2)):
+        target[0:2] = rows[4 + at : 6 + at]
+        target[2:4] = rows[at : at + 2]
     for source, target in ((down, o_down), (win, o_win), (gru, o_gru)):
         target[...] = source[...].astype(F32)
     for j in range(8):
@@ -1615,15 +1656,21 @@
         target[...] = source[...]
 
 
-def finish_call(grads, grad_chars, grad_tokens, token_out, char_out):
+def finish_call(grads, grad_chars, grad_tokens, token_out, char_out, rows, units):
     seqs, block_chars, char_width = grad_chars.shape
     steps = block_chars // 8
     turns = 2 * seqs
     chars = grad_chars.reshape(seqs, steps, 8, char_width)
-    pairs = [a.reshape(2, -1, a.shape[1]) for a in (grads["conv"], grads["qkv"], grads["out"])]
+    pairs = [
+        grads[n].reshape(2, -1, grads[n].shape[1]) for n in ("conv", "qkv", "out", "merge")
+    ]
     plain = [grads["down"], grads["win"], grads["gru"]]
     copied = [grad_tokens, token_out, char_out]
-    flat = [(a.shape[1], 2 * a.shape[2]) for a in pairs] + [a.shape for a in plain]
+    flat = [(a.shape[1], 2 * a.shape[2]) for a in pairs[:3]]
+    channels, width = pairs[3].shape[1:]
+    merged = (channels, 2, width)
+    plain_shapes = [a.shape for a in plain]
+    ends = [(4, width), (4, width), (2, units)]
 
     def rows_spec(shape):
         return pl.BlockSpec((shape[0] // turns, shape[1]), lambda i: (i, 0))
@@ -1635,20 +1682,25 @@
         return pl.BlockSpec((1, shape[1] // 2, shape[2]), lambda i: (i // 2, i % 2, 0))
 
     return pl.pallas_call(
-        finish_kernel,
+        functools.partial(finish_kernel, units),
         grid=(turns,),
-        out_shape=[jax.ShapeDtypeStruct(shape, F32) for shape in flat]
+        out_shape=[jax.ShapeDtypeStruct(shape, F32) for shape in flat + [merged] + plain_shapes]
         + [jax.ShapeDtypeStruct((seqs, 8, steps, char_width), F32)]
-        + [jax.ShapeDtypeStruct(a.shape, a.dtype) for a in copied],
+        + [jax.ShapeDtypeStruct(a.shape, a.dtype) for a in copied]
+        + [jax.ShapeDtypeStruct(shape, F32) for shape in ends],
         in_specs=[pair_spec(a.shape) for a in pairs]
         + [rows_spec(a.shape) for a in plain]
         + [pl.BlockSpec((1, steps // 2, 8, char_width), lambda i: (i // 2, i % 2, 0, 0))]
-        + [halves(a.shape) for a in copied],
+        + [halves(a.shape) for a in copied]
+        + [pl.BlockSpec(rows.shape, lambda i: (0, 0))],
         out_specs=[rows_spec(shape) for shape in flat]
+        + [pl.BlockSpec((channels // turns, 2, width), lambda i: (i, 0, 0))]
+        + [rows_spec(shape) for shape in plain_shapes]
         + [pl.BlockSpec((1, 8, steps // 2, char_width), lambda i: (i // 2, 0, i % 2, 0))]
-        + [halves(a.shape) for a in copied],
+        + [halves(a.shape) for a in copied]
+        + [pl.BlockSpec(shape, lambda i: (0, 0)) for shape in ends],
         compiler_params=pltpu.CompilerParams(vmem_limit_bytes=62 * MIB),
-    )(*pairs, *plain, chars, *copied)
+    )(*pairs, *plain, chars, *copied, rows)
 
 
 def local(
@@ -1686,50 +1738,29 @@
     wg = jnp.transpose(w_gru, (1, 2, 3, 0))
     more = -merge_here % LANE
     wm = jnp.pad(w_merge.reshape(merge_here, 2 * model_width), ((0, more), (0, 0)))
-    layouts = [layout(doc_lengths[i], token_chars[i], char_total) for i in range(micro_count)]
-    stacked_layout = [jnp.stack(parts) for parts in zip(*layouts)]
-    segment, first_char, last_char, keep_forward, keep_backward, prev_ok, next_ok = stacked_layout
     block_chars = characters.shape[1]
     steps = block_chars // 8
-
-    def reorder(rows):
-        split = rows.reshape(micro_count, -1, 8, steps, rows.shape[-1])
-        return jnp.swapaxes(split, 2, 3).reshape(rows.shape)
-
-    keep = reorder(jnp.stack([keep_forward, keep_backward], axis=2))
-    picks = jnp.stack([last_char, first_char], axis=2)
-    inner = picks % block_chars
-    picks = picks - inner + inner % steps * 8 + inner // steps
-    zero = jnp.zeros_like(prev_ok[:, :1])
+    chars = jnp.swapaxes(
+        characters.reshape(micro_count, 8, steps, char_width), 1, 2
+    ).reshape(characters.shape)
     small = dict(
-        gain=norm_gain, bias=norm_bias, cot_t=token_cot, cot_c=char_cot,
-        segc=segment[:, :, None], segr=segment[:, None, :], pickc=picks, keep=keep,
-        pickr=jnp.swapaxes(picks, 1, 2),
-        edges=jnp.stack(
-            [
-                prev_ok,
-                next_ok,
-                jnp.concatenate([prev_ok[:, 1:], zero], axis=1),
-                jnp.concatenate([zero, next_ok[:, :-1]], axis=1),
-            ],
-            axis=2,
-        ),
-        heads=heads_here, units=units_here, channels=merge_here,
+        gain=norm_gain, bias=norm_bias, cot_t=token_cot, cot_c=char_cot, docs=doc_lengths,
+        counts=token_chars[:, None, :], heads=heads_here, units=units_here, channels=merge_here,
     )
     weights = (wq, w_out, w_in, w_down, wg, gate_bias, wc, wm)
-    fw = forward_call(tokens, reorder(characters), weights, small)
-    weights = (fw["wq"], fw["wout"], w_in, w_down, fw["wg"], gate_bias, fw["wc"], wm)
+    fw = forward_call(tokens, chars, weights, small)
+    weights = (fw["wq"], fw["wout"], w_in, w_down, fw["wg"], fw["wc"], wm, gate_bias)
     dp_size = lax.axis_size("dp")
     bw = backward_call(fw, weights, small, dp_size)
     rows = bw["small"]
-    gate_row = rows[8, : 2 * LANE]
     grads = {name: bw[name] for name in GRADS}
     if dp_size != 8:
-        grads, gate_row = lax.psum((grads, gate_row), "dp")
-        rows = lax.psum(rows, ("dp", "tensor"))
-    grad_merge = grads["merge"].astype(F32).reshape(2, merge_here, model_width)
-    conv, qkv, out, down, win, gru, chars, tokens_grad, first, second = finish_call(
-        grads, bw["grad_chars"], bw["grad_tokens"], fw["token_out"], fw["char_out"]
+        grads, gate_rows = lax.psum((grads, rows[8:]), "dp")
+        rows = jnp.concatenate([lax.psum(rows[:8], ("dp", "tensor")), gate_rows], axis=0)
+    (conv, qkv, out, merge, down, win, gru, chars, tokens_grad, first, second, gain_grad, bias_grad,
+     gate_grad) = finish_call(
+        grads, bw["grad_chars"], bw["grad_tokens"], fw["token_out"], fw["char_out"], rows,
+        units_here,
     )
     conv = conv.reshape(3, merge_here, 2 * model_width)
     qkv = qkv.reshape(3, head_cols, model_width)
@@ -1744,11 +1775,11 @@
         win,
         down,
         jnp.transpose(gru, (3, 0, 1, 2)),
-        gate_row.reshape(2, LANE)[:, :units_here],
+        gate_grad,
         jnp.transpose(conv, (0, 2, 1)),
-        jnp.swapaxes(grad_merge, 0, 1),
-        jnp.concatenate([rows[4:6], rows[0:2]], axis=0),
-        jnp.concatenate([rows[6:8], rows[2:4]], axis=0),
+        merge,
+        gain_grad,
+        bias_grad,
     )
 
 

time: 303 us -> 288 us (0.950)
  local copies, waits for them, and re-layouts: 14.4 us -> 5.46 us
  other arithmetic: 7.5 us -> 0 us
    transpose x2 -> x0, local copies, waits for them, and re-layouts: 4.72 us -> none  [the longest x1 2.68 us: local(): jnp.swapaxes(grad_merge, 0, 1)]
    pallas_call x1, Pallas kernels: 103 us -> 106 us  [forward_call(): pl.pallas_call(functools.partial(forward_kernel, small['units'], small['c...]
where the time goes in v7:
time: 288 us; the launch traced here: 287 us
  Pallas kernels  281 us (98%)
  local copies, waits for them, and re-layouts  5.46 us (2%)
    pallas_call x1, Pallas kernels, backward_call(): pl.pallas_call(functools.partial(backward_kernel, small['units'], channel...  166 us
    pallas_call x1, Pallas kernels, forward_call(): pl.pallas_call(functools.partial(forward_kernel, small['units'], small['c...  106 us
    pallas_call x1, Pallas kernels, finish_call(): pl.pallas_call(functools.partial(finish_kernel, units), grid=(turns,), ou...  9.13 us

profile of v7, /device:TPU:0, one launch (start us, length us, event | category | flops | bytes accessed | tf_op | source)
XLA Modules:
  0.0 287.3 jit_solution(17592769468362958171)
XLA Ops:
  0.6 1.3 broadcast_in_dim.3.counts
  1.9 2.1 copy.33
  4.1 1.1 copy.31
  5.2 0.9 pad.4.wm_in.refs_26_
  6.1 105.7 %shard_map.263 = (bf16[2,128,768]{2,1,0:T(8,128)(2,1)}, bf16[2,128,768]{2,1,0:T(8,128)(2,1)}, bf16[2,4,128,768]{3,2,1,0:T(8,128)(2,1)}, bf16[2,4,512,256]{3,2,1,...) custom-call(s32[2,8]{1,0:T(2,128)} %docs.1, ...), custom_call_target="tpu_custom_call" | custom-call | tf_op jit(solution)/shard_map/pallas_call | solution.py:736
  111.8 166.2 %shard_map.264 = (f32[2,128,768]{2,1,0:T(8,128)}, f32[2,512,256]{2,1,0:T(8,128)}, bf16[384,768]{1,0:T(8,128)(2,1)}, bf16[1152,768]{1,0:T(8,128)(2,1)}, bf16[768,...) custom-call(bf16[2,3,128,512]{3,2,1,0:T(8,128)(2,1)} %get-tuple-elem, ...), custom_call_target="tpu_custom_call" | custom-call | tf_op jit(solution)/shard_map/pallas_call | solution.py:1611
  278.0 9.1 %shard_map.265 = (f32[576,1536]{1,0:T(8,128)}, f32[576,768]{1,0:T(8,128)}, f32[192,768]{1,0:T(8,128)}, f32[192,2,768]{2,1,0:T(2,128)}, f32[768,768]{1,0:T(8,128)...) custom-call(bf16[2,576,768]{2,1,0:T(8,128)(2,1)} %bitcast.32, ...), custom_call_target="tpu_custom_call" | custom-call | tf_op jit(solution)/shard_map/pallas_call | solution.py:1684

commit v8 on v7

--- a/solution.py
+++ b/solution.py
@@ -287,7 +287,7 @@
     win, wdown, wm, cot_t, cot_c, segc, segr, pickc, keep,
     stage, got, held, temp, send, recv, local,
 ):
-    seqs, length = counts.shape[0], counts.shape[2]
+    seqs, length = counts.shape
     shard, width = tokens.shape[1], tokens.shape[2]
     block_chars = chars.shape[1]
     heads = p.shape[1] // 4
@@ -301,7 +301,7 @@
     def local_copy(number, seq, source, target):
         return pltpu.make_async_copy(source, target, local.at[number * seqs + seq])
 
-    gx, gc = Gather(g, x, tokens), Gather(g, c, chars)
+    gx, gc = Gather(g, x, tokens), Gather(g, c)
     gh, gm, gs = Gather(g, h), Gather(g, mid), Gather(g, st)
     narrow = lambda ref: (lambda s, i: ref.at[s, i, :, pl.ds(0, width)])
     wide = lambda ref: (lambda s, i: ref.at[s, i])
@@ -374,15 +374,19 @@
         fill(number).start()
     g.greet()
     each(gx.start)
-    each(gc.start)
-
-    for t in range(4):
-        for d in range(2):
-            row = lax.broadcasted_iota(jnp.int32, (LANE, width), 0)
-            col = lax.broadcasted_iota(jnp.int32, (LANE, width), 1)
-            first = d * 4 * units + t * units
-            hit = (col - first == row) & (row < units)
-            perm[pl.ds((2 * t + d) * LANE, LANE), :] = hit.astype(F32).astype(BF16)
+    steps = block_chars // 8
+    assert steps & (steps - 1) == 0
+
+    def reorder(s):
+        own_c(s).wait()
+        row = lax.broadcasted_iota(jnp.int32, (block_chars, block_chars), 0)
+        col = lax.broadcasted_iota(jnp.int32, (block_chars, block_chars), 1)
+        hit = (col == (row & 7) * steps + (row >> 3)).astype(F32).astype(BF16)
+        c[s, me] = nn(hit, c[s, me]).astype(BF16)
+        gc.start(s)
+
+    each(reorder)
+
     taps[...] = jnp.zeros_like(taps)
     norm_grads[...] = jnp.zeros_like(norm_grads)
     gate_bias[...] = jnp.zeros_like(gate_bias)
@@ -396,20 +400,10 @@
         wg[pl.ds(j * LANE + units, LANE - units), :] = jnp.zeros(
             (LANE - units, wg.shape[1]), BF16
         )
-    for number in range(len(fills) - len(late)):
-        fill(number).wait()
-    for j in range(pieces):
-        size = min(shard, rows_in - j * shard)
-        wc[pl.ds(j * shard, size), pl.ds(width, 8 * LANE)] = nt(
-            mid[j // 4, j % 4, pl.ds(0, size), :], perm[...]
-        ).astype(BF16)
-    for number in range(len(keeps)):
-        keep_weights(number).start()
-
+    fill(0).wait()
+    fill(1).wait()
     lane = lax.broadcasted_iota(jnp.int32, (shard, LANE), 1)
     left = lane < HD
-    steps = block_chars // 8
-    assert steps & (steps - 1) == 0
 
     def place(char):
         inner = char & (block_chars - 1)
@@ -436,7 +430,7 @@
         segc[s] = seg_col
         edges[s, :, 0:1] = 1.0 - hits(down, [0] + ends[:-1])
         edges[s, :, 1:2] = 1.0 - hits(down + 1, ends)
-        count = counts[s].astype(F32)
+        count = counts[pl.ds(s, 1), :].astype(F32)
         many = jnp.broadcast_to(count, (LANE, length)).astype(BF16)
         rows = lax.broadcasted_iota(jnp.int32, (length, length), 0)
         cols = lax.broadcasted_iota(jnp.int32, (length, length), 1)
@@ -457,7 +451,7 @@
         keep[s, :, 1:2] = 1.0 - hits(char + 1.0, cuts)
 
     each(structure)
-    for number in range(len(fills) - len(late), len(fills)):
+    for number in (3, 4, 5, 6):
         fill(number).wait()
 
     def attention(s):
@@ -517,7 +511,6 @@
     def gru(s):
         gc.forward(s)
         gc.finish(s)
-        own_c(s).wait()
         save(s, c)
 
         def gates(t, carry):
@@ -573,6 +566,24 @@
 
         s_ffn.start(s, part)
         save(s, act, dact)
+
+    for t in range(4):
+        for d in range(2):
+            row = lax.broadcasted_iota(jnp.int32, (LANE, width), 0)
+            col = lax.broadcasted_iota(jnp.int32, (LANE, width), 1)
+            first = d * 4 * units + t * units
+            hit = (col - first == row) & (row < units)
+            perm[pl.ds((2 * t + d) * LANE, LANE), :] = hit.astype(F32).astype(BF16)
+    for number in range(2, len(fills)):
+        if number not in (3, 4, 5, 6):
+            fill(number).wait()
+    for j in range(pieces):
+        size = min(shard, rows_in - j * shard)
+        wc[pl.ds(j * shard, size), pl.ds(width, 8 * LANE)] = nt(
+            mid[j // 4, j % 4, pl.ds(0, size), :], perm[...]
+        ).astype(BF16)
+    for number in range(len(keeps)):
+        keep_weights(number).start()
 
     each(ffn)
 
@@ -972,49 +983,50 @@
 )
 GRADS = ("merge", "conv", "down", "win", "gru", "out", "qkv")
 PIECES = (
-    (0, 384, False),
-    (1, 256, False),
-    (1, 512, True),
-    (1, 384, True),
+    (0, 384, True),
+    (1, 640, True),
+    (1, 384, False),
+    (1, 128, True),
+    (2, 256, True),
     (2, 512, True),
-    (2, 256, True),
-    (3, 768, True),
+    (3, 384, True),
+    (3, 384, True),
     (4, 384, True),
     (5, 384, True),
-    (6, 384, False),
-    (6, 768, False),
+    (6, 256, True),
+    (6, 896, False),
 )
 SCHEDULE = (
     (),
     (0, 10, 20, 30,),
     (),
-    (1, 11,),
     (21,),
-    (2,),
-    (40, 50, 12,),
-    (60, 22, 31,),
+    (1,),
+    (),
+    (40, 50, 22,),
+    (60, 70, 2,),
+    (11,),
+    (23, 31,),
     (3,),
-    (13,),
-    (23,),
-    (32, 41, 24,),
-    (51, 33,),
-    (42,),
-    (25, 52,),
-    (34, 43,),
-    (61, 26, 53, 4, 14, 35, 44,),
-    (27, 5, 62, 15, 54, 36,),
+    (12, 41, 32, 4,),
     (),
-    (80, 90, 100, 45, 6,),
-    (63, 28, 16, 37, 55,),
-    (81, 91, 46,),
-    (101, 7, 64, 38, 82, 17, 56,),
-    (92, 47,),
-    (102, 8,),
-    (70, 65, 83, 18, 57, 93, 48,),
-    (103, 71,),
-    (66, 84, 72, 58, 94,),
-    (104, 73, 67, 85, 95,),
-    (74, 105, 86, 96, 75, 106, 87, 97, 76, 107, 68, 98, 77, 88, 108, 78,),
+    (13, 42, 51, 33,),
+    (5,),
+    (14, 43, 61,),
+    (6, 52, 34,),
+    (15, 44, 71, 7, 62, 24,),
+    (53, 35,),
+    (90, 100, 110, 16, 72, 45, 63,),
+    (54, 8, 36, 25,),
+    (17, 111, 46, 91, 73,),
+    (64, 101, 37, 55, 26, 47,),
+    (112,),
+    (92, 18, 74, 56,),
+    (80, 38, 65, 102, 27, 48, 113, 93,),
+    (75, 57, 81,),
+    (66, 103, 114, 82, 28, 94,),
+    (76, 83, 67, 104, 95, 77,),
+    (58, 84, 105, 96, 115, 85, 106, 97, 68, 116, 86, 107, 78, 117, 87, 98, 108, 118, 88,),
 )
 
 
@@ -1738,17 +1750,12 @@
     wg = jnp.transpose(w_gru, (1, 2, 3, 0))
     more = -merge_here % LANE
     wm = jnp.pad(w_merge.reshape(merge_here, 2 * model_width), ((0, more), (0, 0)))
-    block_chars = characters.shape[1]
-    steps = block_chars // 8
-    chars = jnp.swapaxes(
-        characters.reshape(micro_count, 8, steps, char_width), 1, 2
-    ).reshape(characters.shape)
     small = dict(
         gain=norm_gain, bias=norm_bias, cot_t=token_cot, cot_c=char_cot, docs=doc_lengths,
-        counts=token_chars[:, None, :], heads=heads_here, units=units_here, channels=merge_here,
+        counts=token_chars, heads=heads_here, units=units_here, channels=merge_here,
     )
     weights = (wq, w_out, w_in, w_down, wg, gate_bias, wc, wm)
-    fw = forward_call(tokens, chars, weights, small)
+    fw = forward_call(tokens, characters, weights, small)
     weights = (fw["wq"], fw["wout"], w_in, w_down, fw["wg"], fw["wc"], wm, gate_bias)
     dp_size = lax.axis_size("dp")
     bw = backward_call(fw, weights, small, dp_size)

time: 288 us -> 279 us (0.969)
  Pallas kernels: 281 us -> 276 us
  local copies, waits for them, and re-layouts: 5.46 us -> 2.06 us
    pallas_call x1, Pallas kernels: 166 us -> 163 us  [backward_call(): pl.pallas_call(functools.partial(backward_kernel, small['units'], channel...]
where the time goes in v8:
time: 279 us
  Pallas kernels  276 us (99%)
    pallas_call x1, Pallas kernels, backward_call(): pl.pallas_call(functools.partial(backward_kernel, small['units'], channel...  163 us
    pallas_call x1, Pallas kernels, forward_call(): pl.pallas_call(functools.partial(forward_kernel, small['units'], small['c...  104 us
    pallas_call x1, Pallas kernels, finish_call(): pl.pallas_call(functools.partial(finish_kernel, units), grid=(turns,), ou...  9.13 us

profile of v8, /device:TPU:0, one launch (start us, length us, event | category | flops | bytes accessed | tf_op | source)
XLA Modules:
  0.0 279.1 jit_solution(133336595975113780)
XLA Ops:
  0.6 1.1 copy.30
  1.8 0.9 pad.4.wm_in.refs_26_
  2.7 104.3 %shard_map.263 = (bf16[2,128,768]{2,1,0:T(8,128)(2,1)}, bf16[2,128,768]{2,1,0:T(8,128)(2,1)}, bf16[2,4,128,768]{3,2,1,0:T(8,128)(2,1)}, bf16[2,4,512,256]{3,2,1,...) custom-call(s32[2,8]{1,0:T(2,128)} %docs.1, ...), custom_call_target="tpu_custom_call" | custom-call | tf_op jit(solution)/shard_map/pallas_call | solution.py:747
  107.0 162.7 %shard_map.264 = (f32[2,128,768]{2,1,0:T(8,128)}, f32[2,512,256]{2,1,0:T(8,128)}, bf16[384,768]{1,0:T(8,128)(2,1)}, bf16[1152,768]{1,0:T(8,128)(2,1)}, bf16[768,...) custom-call(bf16[2,3,128,512]{3,2,1,0:T(8,128)(2,1)} %get-tuple-elem, ...), custom_call_target="tpu_custom_call" | custom-call | tf_op jit(solution)/shard_map/pallas_call | solution.py:1623
  269.8 9.1 %shard_map.265 = (f32[576,1536]{1,0:T(8,128)}, f32[576,768]{1,0:T(8,128)}, f32[192,768]{1,0:T(8,128)}, f32[192,2,768]{2,1,0:T(2,128)}, f32[768,768]{1,0:T(8,128)...) custom-call(bf16[2,576,768]{2,1,0:T(8,128)(2,1)} %bitcast.25, ...), custom_call_target="tpu_custom_call" | custom-call | tf_op jit(solution)/shard_map/pallas_call | solution.py:1696

commit v9 on v8

--- a/solution.py
+++ b/solution.py
@@ -248,7 +248,7 @@
         return tuple(new)
 
     zero, one = jnp.zeros((8, LANE), F32), jnp.ones((8, LANE), F32)
-    ends = lax.fori_loop(0, steps, summary, (zero, one) * 8, unroll=4)
+    ends = lax.fori_loop(0, steps, summary, (zero, one) * 8, unroll=8)
     starts = []
     for tile in range(2):
         state = jnp.concatenate([ends[2 * (4 * tile + t)] for t in range(4)], axis=0)
@@ -273,7 +273,7 @@
             outs[tile, here, :] = value
         return tuple(new)
 
-    lax.fori_loop(0, steps, write, tuple(starts), unroll=4)
+    lax.fori_loop(0, steps, write, tuple(starts), unroll=8)
 
 
 def forward_kernel(
@@ -281,7 +281,7 @@
     wc_in, wm_in, gain, bias, cot_t_in, cot_c_in,
     token_out, char_out, o_x, o_c, o_qkv, o_p, o_ctx, o_h, o_act, o_dact, o_mid, o_st, o_mg,
     o_dmg, o_states, o_decay, o_unit0, o_unit1, o_scale, o_res3, o_res4, o_branch,
-    o_wq, o_wout, o_wg, o_wc, norm_grads, pickr, edges,
+    o_wq, o_wout, o_wg, o_wc, o_wm, norm_grads, pickr, edges,
     x, c, qkv, p, ctx, h, act, dact, mid, st, mg, dmg, low_states, decays, unit0, unit1, scale, res3, res4, branch,
     wq, wout, wg, wc, hidden, middle, outs_t, outs_c, states, drive, taps, perm, gate_bias,
     win, wdown, wm, cot_t, cot_c, segc, segr, pickc, keep,
@@ -340,7 +340,7 @@
 
     each(lambda s: (own_x(s).start(), own_c(s).start()))
     base = (2 + len(plan)) * seqs
-    late = [(win_in, win), (wdown_in, wdown), (wm_in, wm), (cot_t_in, cot_t), (cot_c_in, cot_c)]
+    late = [(win_in, win), (wdown_in, wdown), (cot_t_in, cot_t), (cot_c_in, cot_c)]
     rows_in = wq_in.shape[0]
     fills = [
         (wq_in, wq.at[pl.ds(0, rows_in), :]),
@@ -365,7 +365,7 @@
     def fill(number):
         return pltpu.make_async_copy(*fills[number], local.at[base + number])
 
-    keeps = [(wq, o_wq), (wout, o_wout), (wg, o_wg), (wc, o_wc)]
+    keeps = [(wq, o_wq), (wout, o_wout), (wg, o_wg), (wc, o_wc), (wm, o_wm)]
 
     def keep_weights(number):
         return pltpu.make_async_copy(*keeps[number], local.at[base + len(fills) + number])
@@ -582,6 +582,11 @@
         wc[pl.ds(j * shard, size), pl.ds(width, 8 * LANE)] = nt(
             mid[j // 4, j % 4, pl.ds(0, size), :], perm[...]
         ).astype(BF16)
+    for k in range(2):
+        wm[pl.ds(0, channels), pl.ds(k * width, width)] = wm_in[:, k, :]
+    wm[pl.ds(channels, wm.shape[0] - channels), :] = jnp.zeros(
+        (wm.shape[0] - channels, 2 * width), BF16
+    )
     for number in range(len(keeps)):
         keep_weights(number).start()
 
@@ -692,6 +697,7 @@
     cols = -(-wout.shape[0] // LANE) * LANE
     packed = -(-wq.shape[0] // LANE) * LANE
     heads = small["heads"]
+    merge_shape = (-(-wm.shape[0] // LANE) * LANE, 2 * width)
     kept = [
         ((packed, width), BF16), ((cols, width), BF16), ((4 * LANE, chars.shape[2]), BF16),
         ((packed, width + 8 * LANE), BF16),
@@ -708,8 +714,8 @@
         "dact": ((seqs, 4, shard, win.shape[1]), BF16),
         "mid": ((seqs, 4, shard, width), BF16),
         "st": ((seqs, 4, length, 2 * LANE), BF16),
-        "mg": ((seqs, length, wm.shape[0]), BF16),
-        "dmg": ((seqs, length, wm.shape[0]), BF16),
+        "mg": ((seqs, length, merge_shape[0]), BF16),
+        "dmg": ((seqs, length, merge_shape[0]), BF16),
         "states": ((seqs, 2, total, LANE), BF16),
         "decay": ((seqs, 2, total, LANE), F32),
         "unit0": ((seqs, shard, width), F32),
@@ -729,7 +735,7 @@
         ((length + 16, packed), F32),
         ((8 * LANE, width), BF16),
         ((2, LANE), F32),
-        (win.shape, BF16), (wdown.shape, BF16), (wm.shape, BF16), rows, rows,
+        (win.shape, BF16), (wdown.shape, BF16), (merge_shape, BF16), rows, rows,
         ((seqs, length, 1), jnp.int32), ((seqs, 1, length), jnp.int32),
         ((seqs, length, 2), jnp.int32), ((seqs, total, 2), F32),
         ((seqs, 3, shard, 2 * width), BF16), ((seqs, 3, shard, 2 * width), BF16),
@@ -737,13 +743,14 @@
     ]
     anyspace = pl.BlockSpec(memory_space=pl.ANY)
     vmem = pl.BlockSpec(memory_space=pltpu.VMEM)
-    out_shapes = [sds(low_rows[0], BF16)] * 2 + [sds(*v) for v in list(big.values()) + kept]
+    out_shapes = [sds(low_rows[0], BF16)] * 2
+    out_shapes += [sds(*v) for v in list(big.values()) + kept + [(merge_shape, BF16)]]
     ins = (
         small["docs"], small["counts"], tokens, chars, wq, wout, win, wdown, wg, gate_bias, wc, wm,
         small["gain"], small["bias"], small["cot_t"], small["cot_c"],
     )
     smem = pl.BlockSpec(memory_space=pltpu.SMEM)
-    places = [smem, vmem] + [anyspace] * 7 + [vmem] + [anyspace] * 2 + [vmem] * 2 + [anyspace] * 2
+    places = [smem, vmem] + [anyspace] * 7 + [vmem, anyspace] + [vmem] * 3 + [anyspace] * 2
     outs = pl.pallas_call(
         functools.partial(forward_kernel, small["units"], small["channels"]),
         out_shape=out_shapes
@@ -764,7 +771,7 @@
             collective_id=0, has_side_effects=True, vmem_limit_bytes=62 * MIB
         ),
     )(*ins)
-    names = ["token_out", "char_out"] + list(big) + ["wq", "wout", "wg", "wc", "norm_grads"]
+    names = ["token_out", "char_out"] + list(big) + ["wq", "wout", "wg", "wc", "wm", "norm_grads"]
     names += ["pickr", "edges"]
     return dict(zip(names, outs))
 
@@ -998,7 +1005,7 @@
 )
 SCHEDULE = (
     (),
-    (0, 10, 20, 30,),
+    (10, 20, 30,),
     (),
     (21,),
     (1,),
@@ -1027,6 +1034,7 @@
     (66, 103, 114, 82, 28, 94,),
     (76, 83, 67, 104, 95, 77,),
     (58, 84, 105, 96, 115, 85, 106, 97, 68, 116, 86, 107, 78, 117, 87, 98, 108, 118, 88,),
+    (0,),
 )
 
 
@@ -1235,6 +1243,7 @@
                     :, at : at + size
                 ]
                 at += size
+        fire(30)
         taps = 3 * channels
 
         def conv_rows(j, carry):
@@ -1748,15 +1757,13 @@
     wq = jnp.transpose(w_qkv, (1, 2, 0)).reshape(3 * head_cols, model_width)
     wc = jnp.transpose(w_conv, (0, 2, 1)).reshape(3 * merge_here, 2 * model_width)
     wg = jnp.transpose(w_gru, (1, 2, 3, 0))
-    more = -merge_here % LANE
-    wm = jnp.pad(w_merge.reshape(merge_here, 2 * model_width), ((0, more), (0, 0)))
     small = dict(
         gain=norm_gain, bias=norm_bias, cot_t=token_cot, cot_c=char_cot, docs=doc_lengths,
         counts=token_chars, heads=heads_here, units=units_here, channels=merge_here,
     )
-    weights = (wq, w_out, w_in, w_down, wg, gate_bias, wc, wm)
+    weights = (wq, w_out, w_in, w_down, wg, gate_bias, wc, w_merge)
     fw = forward_call(tokens, characters, weights, small)
-    weights = (fw["wq"], fw["wout"], w_in, w_down, fw["wg"], fw["wc"], wm, gate_bias)
+    weights = (fw["wq"], fw["wout"], w_in, w_down, fw["wg"], fw["wc"], fw["wm"], gate_bias)
     dp_size = lax.axis_size("dp")
     bw = backward_call(fw, weights, small, dp_size)
     rows = bw["small"]

time: 279 us -> 279 us (level)
  no operation moved by 1% of the time
where the time goes in v9:
time: 279 us; the launch traced here: 278 us
  Pallas kernels  278 us (100%)
    pallas_call x1, Pallas kernels, backward_call(): pl.pallas_call(functools.partial(backward_kernel, small['units'], channel...  163 us
    pallas_call x1, Pallas kernels, forward_call(): pl.pallas_call(functools.partial(forward_kernel, small['units'], small['c...  106 us
    pallas_call x1, Pallas kernels, finish_call(): pl.pallas_call(functools.partial(finish_kernel, units), grid=(turns,), ou...  9.13 us

profile of v9, /device:TPU:0, one launch (start us, length us, event | category | flops | bytes accessed | tf_op | source)
XLA Modules:
  0.0 278.5 jit_solution(6128780747392651468)
XLA Ops:
  0.6 105.5 %shard_map.263 = (bf16[2,128,768]{2,1,0:T(8,128)(2,1)}, bf16[2,128,768]{2,1,0:T(8,128)(2,1)}, bf16[2,4,128,768]{3,2,1,0:T(8,128)(2,1)}, bf16[2,4,512,256]{3,2,1,...) custom-call(s32[2,8]{1,0:T(2,128)} %docs.1, ...), custom_call_target="tpu_custom_call" | custom-call | tf_op jit(solution)/shard_map/pallas_call | solution.py:754
  106.2 163.0 %shard_map.264 = (f32[2,128,768]{2,1,0:T(8,128)}, f32[2,512,256]{2,1,0:T(8,128)}, bf16[384,768]{1,0:T(8,128)(2,1)}, bf16[1152,768]{1,0:T(8,128)(2,1)}, bf16[768,...) custom-call(bf16[2,3,128,512]{3,2,1,0:T(8,128)(2,1)} %get-tuple-elem, ...), custom_call_target="tpu_custom_call" | custom-call | tf_op jit(solution)/shard_map/pallas_call | solution.py:1632
  269.2 9.1 %shard_map.265 = (f32[576,1536]{1,0:T(8,128)}, f32[576,768]{1,0:T(8,128)}, f32[192,768]{1,0:T(8,128)}, f32[192,2,768]{2,1,0:T(2,128)}, f32[768,768]{1,0:T(8,128)...) custom-call(bf16[2,576,768]{2,1,0:T(8,128)(2,1)} %bitcast.23, ...), custom_call_target="tpu_custom_call" | custom-call | tf_op jit(solution)/shard_map/pallas_call | solution.py:1705
